TPU v7x, 128 devices: a whole 4x4x4 slice. The times are simulated.
128 devices in a mesh: chain: 32 (over z, x, core), group: 4 (over y).
Axes of the slice: x: 4, y: 4, z: 4, core: 2. Of those that a mesh axis runs over, the one named last changes fastest.
Arguments:
- points: bfloat16 [262144, 384], P(('chain', 'group')), may hold values from -6 to 6
- norm_gains: float32 [4, 384], replicated, may hold values from 0.1 to 1.9
- qkv_weight: bfloat16 [2, 384, 1152], replicated, may hold values from -8 to 8
- proj_weight: bfloat16 [2, 384, 384], replicated, may hold values from -0.75 to 0.75
- up_weight: bfloat16 [2, 384, 1536], replicated, may hold values from -0.3125 to 0.3125
- down_weight: bfloat16 [2, 1536, 384], replicated, may hold values from -0.15625 to 0.15625
- dest_slot: int32 [2048], P(('chain', 'group')), may hold values from 0 to 31, as said below
- owner_from: int32 [3072], P(('chain', 'group')), may hold values from -1 to 31, as said below
Outputs:
- features: bfloat16 [262144, 384], P(('chain', 'group'))
Inputs may be any that keep to these rules, and one draw needn't show every extreme that they name: `dest_slot`: the 16 entries of one device are distinct. An entry o + e sends the tile to the owner at index o of chain in the same group as its e-th tile from this device; at most 1 tiles go from one device to one owner, and that many do in every draw. Together with owner_from it describes one assignment. `owner_from`: an owner's live slots come first; -1 marks an empty slot; a live entry c + e names the e-th tile that device c of chain in the same group sends here. Owners hold from 0 to 24 live tiles, and some owner holds 24 in every draw. Every tile of every device has exactly one slot.
All inputs are finite; a program needn't handle non-finite values.
Results may differ from a plain program's by a relative error of at most 0.015.
Values may be sent and summed in bfloat16 or wider, within the bound.
No kernel may reach another device: no remote copies, remote signals or barrier semaphores. Data moves between devices by JAX's collectives and lax.ppermute only.
A program may use at most 128 MiB of HBM per device.

v0:
```python
import jax
import jax.numpy as jnp
from jax import lax
from jax.sharding import PartitionSpec as P

D = 384
HEADS = 6
HEAD_DIM = 64
PATCH = 1024
TILE = 128
TILES_DEV = 16
SLOTS = 24


norm_epsilon = 1e-05
masked_score = -1000000000.0


def with_halo(cells, sides, width):
    for axis, dim in sides:
        count = lax.axis_size(axis)
        head = lax.slice_in_dim(cells, 0, width, axis=dim)
        tail = lax.slice_in_dim(cells, cells.shape[dim] - width, cells.shape[dim], axis=dim)
        cells = jnp.concatenate(
            [
                lax.ppermute(tail, axis, [(i, (i + 1) % count) for i in range(count)]),
                cells,
                lax.ppermute(head, axis, [((i + 1) % count, i) for i in range(count)]),
            ],
            axis=dim,
        )
    return cells


def layer_norm(values, gain_row):
    floats = values.astype(jnp.float32)
    center = floats - jnp.mean(floats, axis=-1, keepdims=True)
    spread = jnp.mean(center * center, axis=-1, keepdims=True)
    return (center * lax.rsqrt(spread + norm_epsilon) * gain_row).astype(jnp.bfloat16)


def project_heads(values, gain_row, weights):
    normed = layer_norm(values, gain_row)
    return jnp.dot(normed, weights, preferred_element_type=jnp.float32).astype(jnp.bfloat16)


def attend(queries, keys_in, values_in, key_live):
    query_count = queries.shape[0]
    key_count = keys_in.shape[0]
    query_heads = queries.reshape(query_count, HEADS, HEAD_DIM)
    key_heads = keys_in.reshape(key_count, HEADS, HEAD_DIM)
    value_heads = values_in.reshape(key_count, HEADS, HEAD_DIM)
    scores = jnp.einsum(
        "qhd,khd->hqk", query_heads, key_heads, preferred_element_type=jnp.float32
    ) * HEAD_DIM ** (-0.5)
    if key_live is not None:
        scores = jnp.where(key_live[None, None, :], scores, masked_score)
    peak = jnp.max(scores, axis=-1, keepdims=True)
    exponent = jnp.exp(scores - peak)
    weights = (exponent / jnp.sum(exponent, axis=-1, keepdims=True)).astype(jnp.bfloat16)
    mixed = jnp.einsum("hqk,khd->qhd", weights, value_heads, preferred_element_type=jnp.float32)
    return mixed.reshape(query_count, D).astype(jnp.bfloat16)


def residual_add(base, mixed, weights):
    return (
        base.astype(jnp.float32) + jnp.dot(mixed, weights, preferred_element_type=jnp.float32)
    ).astype(jnp.bfloat16)


def feed_forward(values, gain_row, weight_up, weight_down):
    normed = layer_norm(values, gain_row)
    hidden = jax.nn.gelu(
        jnp.dot(normed, weight_up, preferred_element_type=jnp.float32), approximate=False
    ).astype(jnp.bfloat16)
    return residual_add(values, hidden, weight_down)


def body(
    points, norm_gains, qkv_weight, proj_weight, up_weight, down_weight, dest_slot, owner_from
):
    row_count = points.shape[0]
    half_rows = PATCH // 2
    inner_count = row_count // PATCH
    qkv_rows = project_heads(points, norm_gains[0], qkv_weight[0])
    pieces = []
    widened = with_halo(qkv_rows[:, D:], ((("chain", "group"), 0),), half_rows)
    for index in range(inner_count + 1):
        lower = max(index * PATCH - half_rows, 0)
        upper = min(index * PATCH + half_rows, row_count)
        window = widened[index * PATCH : (index + 1) * PATCH]
        pieces.append(attend(qkv_rows[lower:upper, :D], window[:, :D], window[:, D:], None))
    mixed = jnp.concatenate(pieces, axis=0)
    inner_a = residual_add(points, mixed, proj_weight[0])
    outer_a = feed_forward(inner_a, norm_gains[1], up_weight[0], down_weight[0])
    chain_size = lax.axis_size("chain")
    peer_tiles = max(1, -(-SLOTS // chain_size))
    slot_total = chain_size * peer_tiles
    peer_index = jnp.arange(slot_total, dtype=jnp.int32)
    send_table = (dest_slot[None, :] == peer_index[:, None]).astype(jnp.bfloat16)
    columns = outer_a.shape[1]
    packed = jnp.dot(
        send_table, outer_a.reshape(TILES_DEV, TILE * columns), preferred_element_type=jnp.float32
    ).astype(jnp.bfloat16)
    arrived = lax.all_to_all(
        packed.reshape(slot_total, TILE, columns), "chain", split_axis=0, concat_axis=0, tiled=True
    )
    slot_live = owner_from >= 0
    gathered = jnp.take(arrived, jnp.maximum(owner_from, 0), axis=0)
    placed = jnp.where(slot_live[:, None, None], gathered, jnp.zeros((), jnp.bfloat16)).reshape(
        SLOTS * TILE, columns
    )
    row_live = jnp.repeat(slot_live, TILE)
    patch_outputs = []
    for patch_start in range(0, SLOTS * TILE, PATCH):
        patch = placed[patch_start : patch_start + PATCH]
        key_live = row_live[patch_start : patch_start + PATCH]
        qkv_patch = project_heads(patch, norm_gains[2], qkv_weight[1])
        attended = attend(
            qkv_patch[:, :D], qkv_patch[:, D : 2 * D], qkv_patch[:, 2 * D :], key_live
        )
        result = residual_add(patch, attended, proj_weight[1])
        result = feed_forward(result, norm_gains[3], up_weight[1], down_weight[1])
        patch_outputs.append(result)
    owner_done = jnp.concatenate(patch_outputs, axis=0).reshape(SLOTS, TILE * D)
    back_table = (owner_from[None, :] == peer_index[:, None]).astype(jnp.bfloat16)
    back_packed = jnp.dot(back_table, owner_done, preferred_element_type=jnp.float32).astype(
        jnp.bfloat16
    )
    returned = lax.all_to_all(
        back_packed.reshape(slot_total, TILE, D), "chain", split_axis=0, concat_axis=0, tiled=True
    )
    home_rows = jnp.take(returned, dest_slot, axis=0).reshape(row_count, D)
    return home_rows


def solution(mesh):
    placed = (
        P(("chain", "group"), None),
        P(),
        P(),
        P(),
        P(),
        P(),
        P(("chain", "group")),
        P(("chain", "group")),
    )
    return jax.shard_map(
        body, mesh=mesh, in_specs=placed, out_specs=P(("chain", "group"), None), check_vma=False
    )
```

profile of v0, /device:TPU:0, one launch (start us, length us, event | category | flops | bytes accessed | tf_op | source)
XLA Modules:
  0.0 398.1 jit_solution(17032869531303731723)
XLA Ops:
  3.1 3.1 convolution_convert_fusion.2
  9.3 6.5 %collective-permute-start.1 = (bf16[512,768]{0,1:T(8,128)(2,1)}, bf16[512,768]{0,1:T(8,128)(2,1)}, u32[]{:S(2)}, u32[]{:S(2)}) collective-permute-start(bf16[512,768]{0,1:T(8,128)(2,1)} %get-tuple-element.18), channel_id=1, source_target_pairs={{1,0},{2,1},{3,2},{4,3},{5,4},{6,5},{7,6},{8,7},{9,8},{10,9},{11,1... | collective-permute-start | bytes 2359304 | tf_op jit(solution)/shard_map/ppermute | solution.py:28
  17.0 13.5 %fusion.354 = (f32[6,1024]{1,0:T(8,128)S(1)}, f32[6,1024,1024]{1,2,0:T(8,128)}) fusion(bf16[1024,6,64]{0,2,1:T(8,128)(2,1)} %bitcast.153, bf16[1024,6,64]{0,2,1:T(8,128)(2,1)S(1)} %bitcast.152), kind=kOutput, calls=%fused_computation.441 | convolution fusion | flops 824181760 | bytes 26763264 | tf_op jit(solution)/shard_map/sub | solution.py:59
  30.5 10.9 %fusion.147 = bf16[6,64,1024]{2,1,0:T(8,128)(2,1)} fusion(bf16[1024,6,64]{0,2,1:T(8,128)(2,1)S(1)} %bitcast.151, f32[6,1024,1024]{1,2,0:T(8,128)} %get-tuple-element.51, f32[6,1024]{1,0:T(8,128)S(1)} %get-tuple-element.50), kind=kOutput, calls=%fused_computation.214 | convolution fusion | flops 818282496 | bytes 26763264 | tf_op jit(solution)/shard_map/hqk,khd->qhd/dot_general | solution.py:61
  41.4 2.3 copy-done.1
  44.7 2.9 pad_maximum_fusion.3
  47.6 9.9 %fusion.355 = (f32[6,512]{1,0:T(8,128)}, f32[6,512,1024]{2,1,0:T(8,128)}) fusion(bf16[512,6,64]{0,2,1:T(8,128)(2,1)} %bitcast.174, bf16[1024,6,64]{0,2,1:T(8,128)(2,1)} %bitcast.172), kind=kOutput, calls=%fused_computation.442 | convolution fusion | flops 412091392 | bytes 13774848 | tf_op jit(solution)/shard_map/sub | solution.py:59
  57.6 9.7 %fusion.353 = (f32[6,512]{1,0:T(8,128)}, f32[6,512,1024]{2,1,0:T(8,128)}) fusion(bf16[512,6,64]{0,2,1:T(8,128)(2,1)S(1)} %bitcast.173, bf16[1024,6,64]{0,2,1:T(8,128)(2,1)} %bitcast.171), kind=kOutput, calls=%fused_computation.440 | convolution fusion | flops 412091392 | bytes 13774848 | tf_op jit(solution)/shard_map/sub | solution.py:59
  67.3 6.8 %fusion.149 = bf16[6,64,512]{2,1,0:T(8,128)(2,1)S(1)} fusion(bf16[1024,6,64]{0,2,1:T(8,128)(2,1)S(1)} %bitcast.170, f32[6,512,1024]{2,1,0:T(8,128)} %get-tuple-element.53, f32[6,512]{1,0:T(8,128)} %get-tuple-element.52), kind=kOutput, calls=%fused_computation.216 | convolution fusion | flops 409141248 | bytes 13774848 | tf_op jit(solution)/shard_map/hqk,khd->qhd/dot_general | solution.py:61
  75.4 2.3 fusion.148
  79.3 34.8 %fusion.91 = bf16[2048,384]{0,1:T(8,128)(2,1)} fusion(bf16[2048,384]{0,1:T(8,128)(2,1)S(1)} %get-tuple-element.55, f32[384]{0:T(512)S(1)} %get-tuple-element.12, f32[2048]{0:T(1024)S(1)} %add_rsqrt_fusion, f32[2048]{0:T(1024)S(1)} %broadcast_multiply_fusion, bf16[2,1536,384]{2,1,0:T(8,128)(2,1)} %param.13, bf16[2,384,1536]{2,1,0:T(8,128)(2,1)} %param.12), kind=kOutput, calls=%fused_computation.151 | convolution fusion | flops 5042601984 | bytes 7096320 | tf_op jit(solution)/shard_map/dot_general | solution.py:67
  120.0 4.1 %all-to-all-start = ((bf16[32,128,384]{2,1,0:T(8,128)(2,1)}), bf16[32,128,384]{2,1,0:T(8,128)(2,1)S(1)}, u32[]{:S(2)}, u32[]{:S(2)}) async-start(bf16[32,128,384]{2,1,0:T(8,128)(2,1)} %bitcast.56), calls=%async_computation | async-start | bytes 6291456 | tf_op jit(solution)/shard_map/all_to_all | solution.py:105
  124.9 41.2 %all-to-all-done = bf16[32,128,384]{2,1,0:T(8,128)(2,1)S(1)} async-done(((bf16[32,128,384]{2,1,0:T(8,128)(2,1)}), bf16[32,128,384]{2,1,0:T(8,128)(2,1)S(1)}, u32[]{:S(2)}, u32[]{:S(2)}) %all-to-all-start) | async-done | bytes 3145760 | tf_op jit(solution)/shard_map/all_to_all | solution.py:105
  166.1 2.4 gather_fusion
  181.3 2.3 copy.37
  183.6 2.3 copy.35
  187.7 14.5 %fusion.358 = (f32[6,1024]{1,0:T(8,128)S(1)}, f32[6,1024,1024]{1,2,0:T(8,128)}) fusion(pred[1024]{0:T(1024)(128)(4,1)S(1)} %broadcast_bitcast_fusion.3, bf16[1024,6,64]{0,2,1:T(8,128)(2,1)} %bitcast.157, bf16[1024,6,64]{0,2,1:T(8,128)(2,1)} %bitcast.159), kind=kOutput, calls=%fused_computation.445 | convolution fusion | flops 830473216 | bytes 26764288 | tf_op jit(solution)/shard_map/sub | solution.py:59
  202.2 9.9 %fusion.146 = bf16[6,64,1024]{2,1,0:T(8,128)(2,1)S(1)} fusion(bf16[1024,6,64]{0,2,1:T(8,128)(2,1)S(1)} %bitcast.160, f32[6,1024,1024]{1,2,0:T(8,128)} %get-tuple-element.65, f32[6,1024]{1,0:T(8,128)S(1)} %get-tuple-element.64), kind=kOutput, calls=%fused_computation.213 | convolution fusion | flops 818282496 | bytes 26763264 | tf_op jit(solution)/shard_map/hqk,khd->qhd/dot_general | solution.py:61
  221.4 14.5 %fusion.357 = (f32[6,1024]{1,0:T(8,128)S(1)}, f32[6,1024,1024]{1,2,0:T(8,128)}) fusion(pred[1024]{0:T(1024)(128)(4,1)S(1)} %get-tuple-element.71, bf16[1024,6,64]{0,2,1:T(8,128)(2,1)} %bitcast.158, bf16[1024,6,64]{0,2,1:T(8,128)(2,1)} %bitcast.161), kind=kOutput, calls=%fused_computation.444 | convolution fusion | flops 830473216 | bytes 26764288 | tf_op jit(solution)/shard_map/sub | solution.py:59
  235.9 9.9 %fusion.145 = bf16[6,64,1024]{2,1,0:T(8,128)(2,1)S(1)} fusion(bf16[1024,6,64]{0,2,1:T(8,128)(2,1)S(1)} %bitcast.162, f32[6,1024,1024]{1,2,0:T(8,128)} %get-tuple-element.61, f32[6,1024]{1,0:T(8,128)S(1)} %get-tuple-element.60), kind=kOutput, calls=%fused_computation.212 | convolution fusion | flops 818282496 | bytes 26763264 | tf_op jit(solution)/shard_map/hqk,khd->qhd/dot_general | solution.py:61
  246.7 18.7 %fusion.117 = bf16[1024,384]{0,1:T(8,128)(2,1)} fusion(bf16[1024,384]{0,1:T(8,128)(2,1)S(1)} %copy-done.5, bf16[2,1536,384]{2,1,0:T(8,128)(2,1)} %param.13, bf16[2,384,1536]{2,1,0:T(8,128)(2,1)} %param.12, f32[384]{0:T(512)S(1)} %copy-done.18, f32[1024]{0:T(1024)S(1)} %add_rsqrt_fusion.6, f32[1024]{0:T(1024)S(1)} %broadcast_multiply_fusion.4), kind=kOutput, calls=%fused_computation.182 | convolution fusion | flops 2521300992 | bytes 4728832 | tf_op jit(solution)/shard_map/dot_general | solution.py:67
  265.5 18.6 %fusion.118 = bf16[1024,384]{0,1:T(8,128)(2,1)} fusion(bf16[1024,384]{0,1:T(8,128)(2,1)S(1)} %get-tuple-element.63, bf16[2,1536,384]{2,1,0:T(8,128)(2,1)} %param.13, bf16[2,384,1536]{2,1,0:T(8,128)(2,1)} %param.12, f32[1024]{0:T(1024)S(1)} %add_rsqrt_fusion.4, f32[1024]{0:T(1024)S(1)} %broadcast_multiply_fusion.3, f32[384]{0:T(512)S(1)} %copy-done.18), kind=kOutput, calls=%fused_computation.183 | convolution fusion | flops 2521300992 | bytes 4728832 | tf_op jit(solution)/shard_map/dot_general | solution.py:67
  284.1 2.7 convolution_convert_fusion.3
  288.0 2.3 copy.48
  293.5 14.5 %fusion.356 = (f32[6,1024]{1,0:T(8,128)S(1)}, f32[6,1024,1024]{1,2,0:T(8,128)}) fusion(pred[1024]{0:T(1024)(128)(4,1)S(1)} %copy-done.19, bf16[1024,6,64]{0,2,1:T(8,128)(2,1)} %bitcast.154, bf16[1024,6,64]{0,2,1:T(8,128)(2,1)} %bitcast.155), kind=kOutput, calls=%fused_computation.443 | convolution fusion | flops 830473216 | bytes 26764288 | tf_op jit(solution)/shard_map/sub | solution.py:59
  308.1 9.6 %fusion.144 = bf16[6,64,1024]{2,1,0:T(8,128)(2,1)S(1)} fusion(bf16[1024,6,64]{0,2,1:T(8,128)(2,1)S(1)} %bitcast.156, f32[6,1024,1024]{1,2,0:T(8,128)} %get-tuple-element.57, f32[6,1024]{1,0:T(8,128)S(1)} %get-tuple-element.56), kind=kOutput, calls=%fused_computation.211 | convolution fusion | flops 818282496 | bytes 26763264 | tf_op jit(solution)/shard_map/hqk,khd->qhd/dot_general | solution.py:61
  318.6 18.6 %fusion.119 = bf16[1024,384]{0,1:T(8,128)(2,1)} fusion(bf16[1024,384]{0,1:T(8,128)(2,1)S(1)} %get-tuple-element.59, bf16[2,1536,384]{2,1,0:T(8,128)(2,1)} %param.13, bf16[2,384,1536]{2,1,0:T(8,128)(2,1)} %param.12, f32[1024]{0:T(1024)S(1)} %add_rsqrt_fusion.2, f32[1024]{0:T(1024)S(1)} %broadcast_multiply_fusion.2, f32[384]{0:T(512)S(1)} %copy-done.18), kind=kOutput, calls=%fused_computation.184 | convolution fusion | flops 2521300992 | bytes 4728832 | tf_op jit(solution)/shard_map/dot_general | solution.py:67
  338.7 2.4 copy.52
  341.1 3.0 reshape.323
  347.4 4.1 %all-to-all-start.1 = ((bf16[32,128,384]{2,1,0:T(8,128)(2,1)}), bf16[32,128,384]{2,1,0:T(8,128)(2,1)S(1)}, u32[]{:S(2)}, u32[]{:S(2)}) async-start(bf16[32,128,384]{2,1,0:T(8,128)(2,1)} %bitcast.58), calls=%async_computation.1 | async-start | bytes 6291456 | tf_op jit(solution)/shard_map/all_to_all | solution.py:130
  351.6 41.9 %all-to-all-done.1 = bf16[32,128,384]{2,1,0:T(8,128)(2,1)S(1)} async-done(((bf16[32,128,384]{2,1,0:T(8,128)(2,1)}), bf16[32,128,384]{2,1,0:T(8,128)(2,1)S(1)}, u32[]{:S(2)}, u32[]{:S(2)}) %all-to-all-start.1) | async-done | bytes 3145760 | tf_op jit(solution)/shard_map/all_to_all | solution.py:130
  395.4 2.5 bitcast_select_fusion
  (131 shorter events, 54.5 us)
Async XLA Ops:
  0.0 2.6 copy-start.17
  0.0 3.1 copy-start.24
  6.2 9.6 %copy-start = (bf16[2048,1152]{0,1:T(8,128)(2,1)}, bf16[2048,1152]{0,1:T(8,128)(2,1)S(1)}, u32[]{:S(2)}) copy-start(bf16[2048,1152]{0,1:T(8,128)(2,1)S(1)} %convolution_convert_fusion.2) | copy-start | bytes 14155780
  7.6 37.0 %collective-permute-start = (bf16[512,768]{0,1:T(8,128)(2,1)}, bf16[512,768]{0,1:T(8,128)(2,1)}, u32[]{:S(2)}, u32[]{:S(2)}) collective-permute-start(bf16[512,768]{0,1:T(8,128)(2,1)} %get-tuple-element.17), channel_id=1, source_target_pairs={{0,1},{1,2},{2,3},{3,4},{4,5},{5,6},{6,7},{7,8},{8,9},{9,10},{10,1... | collective-permute-start | bytes 2359304 | tf_op jit(solution)/shard_map/ppermute | solution.py:26
  9.3 35.3 %collective-permute-start.1 = (bf16[512,768]{0,1:T(8,128)(2,1)}, bf16[512,768]{0,1:T(8,128)(2,1)}, u32[]{:S(2)}, u32[]{:S(2)}) collective-permute-start(bf16[512,768]{0,1:T(8,128)(2,1)} %get-tuple-element.18), channel_id=1, source_target_pairs={{1,0},{2,1},{3,2},{4,3},{5,4},{6,5},{7,6},{8,7},{9,8},{10,9},{11,1... | collective-permute-start | bytes 2359304 | tf_op jit(solution)/shard_map/ppermute | solution.py:28
  41.4 2.3 copy-start.1
  41.4 3.3 slice-start
  67.3 8.2 %copy-start.28 = (f32[6,512,1024]{2,1,0:T(8,128)S(1)}, f32[6,512,1024]{2,1,0:T(8,128)}, u32[]{:S(2)}) copy-start(f32[6,512,1024]{2,1,0:T(8,128)} %get-tuple-element.49) | copy-start | bytes 37748740
  67.3 8.2 %copy-start.29 = (f32[6,512]{1,0:T(8,128)S(1)}, f32[6,512]{1,0:T(8,128)}, u32[]{:S(2)}) copy-start(f32[6,512]{1,0:T(8,128)} %get-tuple-element.48) | copy-start | bytes 36868
  114.1 2.7 copy-start.22
  117.7 6.4 %copy-start.20 = (s32[24]{0:T(128)S(1)}, s32[24]{0:T(128)}, u32[]{:S(2)}) copy-start(s32[24]{0:T(128)} %param.15) | copy-start | bytes 292
  120.0 46.1 %all-to-all-start = ((bf16[32,128,384]{2,1,0:T(8,128)(2,1)}), bf16[32,128,384]{2,1,0:T(8,128)(2,1)S(1)}, u32[]{:S(2)}, u32[]{:S(2)}) async-start(bf16[32,128,384]{2,1,0:T(8,128)(2,1)} %bitcast.56), calls=%async_computation | async-start | bytes 6291456 | tf_op jit(solution)/shard_map/all_to_all | solution.py:105
  170.6 3.5 copy-start.16
  171.1 4.9 %copy-start.25 = (bf16[2,384,1152]{2,1,0:T(8,128)(2,1)S(1)}, bf16[2,384,1152]{2,1,0:T(8,128)(2,1)}, u32[]{:S(2)}) copy-start(bf16[2,384,1152]{2,1,0:T(8,128)(2,1)} %param.10) | copy-start | bytes 5308420
  187.7 14.5 %copy-start.12 = (bf16[1024,384]{0,1:T(8,128)(2,1)S(1)}, bf16[1024,384]{0,1:T(8,128)(2,1)}, u32[]{:S(2)}) copy-start(bf16[1024,384]{0,1:T(8,128)(2,1)} %copy.35) | copy-start | bytes 2359300
  202.2 9.9 %copy-start.3 = (f32[1024,384]{0,1:T(8,128)S(1)}, f32[1024,384]{0,1:T(8,128)}, u32[]{:S(2)}) copy-start(f32[1024,384]{0,1:T(8,128)} %copy.61) | copy-start | bytes 4718596
  202.2 9.9 %copy-start.7 = (bf16[2,384,384]{2,1,0:T(8,128)(2,1)S(1)}, bf16[2,384,384]{2,1,0:T(8,128)(2,1)}, u32[]{:S(2)}) copy-start(bf16[2,384,384]{2,1,0:T(8,128)(2,1)} %param.11) | copy-start | bytes 1769476
  202.2 11.5 %copy-start.15 = (bf16[8,128,384]{2,1,0:T(8,128)(2,1)S(1)}, bf16[8,128,384]{2,1,0:T(8,128)(2,1)}, u32[]{:S(2)}) copy-start(bf16[8,128,384]{2,1,0:T(8,128)(2,1)} %get-tuple-element.29) | copy-start | bytes 2359300
  202.2 11.5 %copy-start.26 = (bf16[2,384,1152]{2,1,0:T(8,128)(2,1)S(1)}, bf16[2,384,1152]{2,1,0:T(8,128)(2,1)}, u32[]{:S(2)}) copy-start(bf16[2,384,1152]{2,1,0:T(8,128)(2,1)} %param.10) | copy-start | bytes 5308420
  221.4 14.6 %copy-start.13 = (bf16[1024,384]{0,1:T(8,128)(2,1)S(1)}, bf16[1024,384]{0,1:T(8,128)(2,1)}, u32[]{:S(2)}) copy-start(bf16[1024,384]{0,1:T(8,128)(2,1)} %copy.41) | copy-start | bytes 2359300
  235.9 9.9 %copy-start.8 = (bf16[2,384,384]{2,1,0:T(8,128)(2,1)S(1)}, bf16[2,384,384]{2,1,0:T(8,128)(2,1)}, u32[]{:S(2)}) copy-start(bf16[2,384,384]{2,1,0:T(8,128)(2,1)} %param.11) | copy-start | bytes 1769476
  235.9 10.8 %copy-start.5 = (bf16[1024,384]{0,1:T(8,128)(2,1)S(1)}, bf16[1024,384]{0,1:T(8,128)(2,1)}, u32[]{:S(2)}) copy-start(bf16[1024,384]{0,1:T(8,128)(2,1)} %copy-done.4) | copy-start | bytes 2359300
  235.9 10.8 %copy-start.18 = (f32[384]{0:T(512)S(1)}, f32[384]{0:T(512)}, u32[]{:S(2)}) copy-start(f32[384]{0:T(512)} %get-tuple-element.11) | copy-start | bytes 4612
  265.5 18.6 %copy-start.14 = (bf16[8,128,384]{2,1,0:T(8,128)(2,1)S(1)}, bf16[8,128,384]{2,1,0:T(8,128)(2,1)}, u32[]{:S(2)}) copy-start(bf16[8,128,384]{2,1,0:T(8,128)(2,1)} %get-tuple-element.30) | copy-start | bytes 2359300
  284.1 8.5 %copy-start.2 = (f32[8,128,384]{2,1,0:T(8,128)S(1)}, f32[8,128,384]{2,1,0:T(8,128)}, u32[]{:S(2)}) copy-start(f32[8,128,384]{2,1,0:T(8,128)} %get-tuple-element.35) | copy-start | bytes 4718596
  286.8 6.7 %copy-start.19 = (pred[1024]{0:T(1024)(128)(4,1)S(1)}, pred[1024]{0:T(1024)(128)(4,1)}, u32[]{:S(2)}) copy-start(pred[1024]{0:T(1024)(128)(4,1)} %get-tuple-element.70) | copy-start | bytes 3076
  293.5 14.6 %copy-start.11 = (bf16[1024,384]{0,1:T(8,128)(2,1)S(1)}, bf16[1024,384]{0,1:T(8,128)(2,1)}, u32[]{:S(2)}) copy-start(bf16[1024,384]{0,1:T(8,128)(2,1)} %copy.47) | copy-start | bytes 2359300
  308.1 9.6 %copy-start.9 = (bf16[2,384,384]{2,1,0:T(8,128)(2,1)S(1)}, bf16[2,384,384]{2,1,0:T(8,128)(2,1)}, u32[]{:S(2)}) copy-start(bf16[2,384,384]{2,1,0:T(8,128)(2,1)} %param.11) | copy-start | bytes 1769476
  318.6 18.6 %copy-start.10 = (bf16[1024,384]{0,1:T(8,128)(2,1)S(1)}, bf16[1024,384]{0,1:T(8,128)(2,1)}, u32[]{:S(2)}) copy-start(bf16[1024,384]{0,1:T(8,128)(2,1)} %fusion.117) | copy-start | bytes 2359300
  337.1 7.0 %copy-start.21 = (s32[24]{0:T(128)S(1)}, s32[24]{0:T(128)}, u32[]{:S(2)}) copy-start(s32[24]{0:T(128)} %param.15) | copy-start | bytes 292
  345.1 6.4 %copy-start.23 = (s32[16]{0:T(128)S(1)}, s32[16]{0:T(128)}, u32[]{:S(2)}) copy-start(s32[16]{0:T(128)} %param.14) | copy-start | bytes 196
  347.4 46.1 %all-to-all-start.1 = ((bf16[32,128,384]{2,1,0:T(8,128)(2,1)}), bf16[32,128,384]{2,1,0:T(8,128)(2,1)S(1)}, u32[]{:S(2)}, u32[]{:S(2)}) async-start(bf16[32,128,384]{2,1,0:T(8,128)(2,1)} %bitcast.58), calls=%async_computation.1 | async-start | bytes 6291456 | tf_op jit(solution)/shard_map/all_to_all | solution.py:130
  (3 other events, 5.6 us)
where the time goes:
time: 405 us; the launch traced here: 398 us
  matrix products  230 us (57%)
  waiting for transfers between devices  83.1 us (21%)
  local copies, waits for them, and re-layouts  51.3 us (13%)
  starting transfers between devices  16.4 us (4%)
  other arithmetic  16.3 us (4%)
    dot_general x8, matrix products, residual_add(): jnp.dot(mixed, weights, preferred_element_type=jnp.float32)  93.7 us
    sub x6, matrix products, attend(): exponent = jnp.exp(scores - peak)  76.7 us
    dot_general x6, matrix products, attend(): jnp.einsum('hqk,khd->qhd', weights, value_heads, preferred_element_type=j...  49.3 us
    all_to_all x1, waiting for transfers between devices, body(): lax.all_to_all(back_packed.reshape(slot_total, TILE, D), 'chain', split_a...  41.9 us
    all_to_all x1, waiting for transfers between devices, body(): lax.all_to_all(packed.reshape(slot_total, TILE, columns), 'chain', split_...  41.2 us
    unnamed x63, local copies, waits for them, and re-layouts  10.9 us
    dot_general x4, matrix products, project_heads(): jnp.dot(normed, weights, preferred_element_type=jnp.float32)  8.7 us
    slice x6, local copies, waits for them, and re-layouts, body(): qkv_patch[:, D:2 * D]  8.39 us
  transfers between devices with their start and end apart: 4, of which 2 were waited for; matrix products, arithmetic and copies ran while one was open for 7% of the time, Pallas kernels for 0%

commit v1 on v0

v1 whole, which is shorter than its diff:
```python
import functools

import jax
import jax.numpy as jnp
from jax import lax
from jax.experimental import pallas as pl
from jax.experimental.pallas import tpu as pltpu
from jax.sharding import PartitionSpec as P

D = 384
HEADS = 6
HEAD_DIM = 64
FF = 1536
PATCH = 1024
TILE = 128
TILES_DEV = 16
SLOTS = 24
PEERS = 32
PAIRS = HEADS // 2
CHUNKS = 2
PART = TILE // CHUNKS
PATCH_TILES = PATCH // TILE
UNIT_TILES = 4
HALF = PATCH // 2
HID = 256

norm_epsilon = 1e-05
masked_score = -1000000000.0
query_scale = HEAD_DIM ** (-0.5) * 1.4426950408889634
f32 = jnp.float32
bf16 = jnp.bfloat16


def norm_rows(values, gain_row):
    center = values - jnp.mean(values, axis=-1, keepdims=True)
    spread = jnp.mean(center * center, axis=-1, keepdims=True)
    return (center * lax.rsqrt(spread + norm_epsilon) * gain_row).astype(bf16)


def gelu(x):
    return (0.5 * x) * (1.0 + lax.erf(x * 0.5 ** 0.5))


def dot(a, b):
    return jnp.dot(a, b, preferred_element_type=f32)


def dot_t(a, b):
    return lax.dot_general(a, b, (((1,), (1,)), ((), ())), preferred_element_type=f32)


def whole(shape):
    zeros = (0,) * len(shape)
    return pl.BlockSpec(shape, lambda *_: zeros)


def layer_of(shape, layer):
    zeros = (0,) * len(shape)
    return pl.BlockSpec((None, *shape), lambda *_: (layer, *zeros))


def qkv_own_kernel(x_ref, gains_ref, w_ref, q_ref, k_ref, v_ref):
    normed = norm_rows(x_ref[...].astype(f32), gains_ref[0:1, :])
    out = dot(normed, w_ref[...])
    q_ref[...] = (out[:, :D] * query_scale).astype(bf16)
    k_ref[...] = out[:, D : 2 * D].astype(bf16)
    v_ref[...] = out[:, 2 * D :].astype(bf16)


def qkv_own(points, gains, qkv_weight):
    rows = points.shape[0]
    ext = jax.ShapeDtypeStruct((rows + PATCH, D), bf16)
    return pl.pallas_call(
        qkv_own_kernel,
        grid=(rows // HALF,),
        in_specs=[
            pl.BlockSpec((HALF, D), lambda i: (i, 0)),
            whole((4, D)),
            layer_of((D, 3 * D), 0),
        ],
        out_specs=[
            pl.BlockSpec((HALF, D), lambda i: (i, 0)),
            pl.BlockSpec((HALF, D), lambda i: (i + 1, 0)),
            pl.BlockSpec((HALF, D), lambda i: (i + 1, 0)),
        ],
        out_shape=[jax.ShapeDtypeStruct((rows, D), bf16), ext, ext],
        name="qkv_own",
    )(points, gains, qkv_weight)


def qkv_halo_kernel(a_ref, b_ref, gains_ref, w_ref, k_in, v_in, k_ref, v_ref):
    first = pl.program_id(0) == 0
    rows = jnp.where(first, a_ref[...].astype(f32), b_ref[...].astype(f32))
    normed = norm_rows(rows, gains_ref[0:1, :])
    out = dot(normed, w_ref[:, D:])
    k_ref[...] = out[:, :D].astype(bf16)
    v_ref[...] = out[:, D:].astype(bf16)


def qkv_halo(before, after, gains, qkv_weight, keys, values):
    last = keys.shape[0] // HALF - 1
    ext = jax.ShapeDtypeStruct(keys.shape, bf16)
    return pl.pallas_call(
        qkv_halo_kernel,
        grid=(2,),
        in_specs=[
            whole((HALF, D)),
            whole((HALF, D)),
            whole((4, D)),
            layer_of((D, 3 * D), 0),
            pl.BlockSpec(memory_space=pl.ANY),
            pl.BlockSpec(memory_space=pl.ANY),
        ],
        out_specs=[pl.BlockSpec((HALF, D), lambda i: (i * last, 0))] * 2,
        out_shape=[ext, ext],
        input_output_aliases={4: 0, 5: 1},
        name="qkv_halo",
    )(before, after, gains, qkv_weight, keys, values)


def qkv_owner_kernel(from_ref, part_ref, gains_ref, w_ref, x_ref, q_ref, k_ref, v_ref):
    step = pl.program_id(0)
    tiles = []
    for t in range(PATCH_TILES):
        source = from_ref[step * PATCH_TILES + t]
        tile = part_ref[jnp.maximum(source, 0)]
        tiles.append(jnp.where(source >= 0, tile.astype(f32), 0.0))
    rows = jnp.concatenate(tiles, axis=0)
    shape = (PATCH_TILES, PART, D)
    x_ref[...] = rows.astype(bf16).reshape(shape)
    normed = norm_rows(rows, gains_ref[2:3, :])
    out = dot(normed, w_ref[...])
    q_ref[...] = (out[:, :D] * query_scale).astype(bf16).reshape(shape)
    k_ref[...] = out[:, D : 2 * D].astype(bf16).reshape(shape)
    v_ref[...] = out[:, 2 * D :].astype(bf16).reshape(shape)


def qkv_owner(owner_from, part, gains, qkv_weight):
    block = pl.BlockSpec((PATCH_TILES, PART, D), lambda i, *_: (i, 0, 0))
    shape = jax.ShapeDtypeStruct((SLOTS, PART, D), bf16)
    return pl.pallas_call(
        qkv_owner_kernel,
        grid_spec=pltpu.PrefetchScalarGridSpec(
            num_scalar_prefetch=1,
            grid=(SLOTS // PATCH_TILES,),
            in_specs=[whole((PEERS, PART, D)), whole((4, D)), layer_of((D, 3 * D), 1)],
            out_specs=[block] * 4,
        ),
        out_shape=[shape] * 4,
        name="qkv_owner",
    )(owner_from, part, gains, qkv_weight)


def block_kernel(units, masked, gain, pieces, table_ref, x_ref, q_ref, *refs):
    k_refs, refs = refs[:pieces], refs[pieces:]
    v_refs, refs = refs[:pieces], refs[pieces:]
    gains_ref, proj_ref, up_ref, down_ref, out_ref, inner_ref, normed_ref = refs
    step = pl.program_id(0)
    count = UNIT_TILES * PART
    lanes = lax.broadcasted_iota(jnp.int32, (1, 128), 1)
    low = lanes < HEAD_DIM
    picks = [low.astype(f32).astype(bf16), (~low).astype(f32).astype(bf16)]

    def attention_parts():
        queries = q_ref[...].reshape(count, D)
        rows = PATCH // pieces
        ones = jnp.ones((rows, 128), bf16)
        extra_q = extra_k = None
        if masked:
            unit = jnp.minimum(step, units - 1)
            base = (unit * UNIT_TILES) // PATCH_TILES * PATCH_TILES
            extra_q = jnp.broadcast_to((lanes == 0).astype(f32).astype(bf16), (count, 128))
            marks = []
            for t in range(PATCH_TILES):
                mark = jnp.where(table_ref[base + t] >= 0, 0.0, masked_score)
                marks.append(jnp.full((rows // PATCH_TILES, 128), mark, f32).astype(bf16))
            extra_k = jnp.concatenate(marks, axis=0)

        def scores(h):
            cols = slice(128 * (h // 2), 128 * (h // 2) + 128)
            q = queries[:, cols] * picks[h % 2]
            if masked:
                q = jnp.concatenate([q, extra_q], axis=1)
            out = []
            for k_ref in k_refs:
                k = k_ref[...].reshape(rows, D)[:, cols]
                if masked:
                    k = jnp.concatenate([k, extra_k], axis=1)
                out.append(dot_t(q, k))
            return out

        def soften(parts):
            peak = functools.reduce(
                jnp.maximum, [jnp.max(s, axis=-1, keepdims=True) for s in parts]
            )
            return [jnp.exp2(s - peak).astype(bf16) for s in parts]

        def mix(h, parts):
            cols = slice(128 * (h // 2), 128 * (h // 2) + 128)
            total = None
            for p, v_ref in zip(parts, v_refs):
                v = v_ref[...].reshape(rows, D)[:, cols]
                one = dot(p, jnp.concatenate([v, ones], axis=1))
                total = one if total is None else total + one
            return total[:, :128] / total[:, 128:]

        return scores, soften, mix

    def join(mixed):
        pairs = [jnp.where(low, mixed[2 * i], mixed[2 * i + 1]) for i in range(PAIRS)]
        joined = jnp.concatenate(pairs, axis=1).astype(bf16)
        base = x_ref[...].reshape(count, D).astype(f32)
        inner = (base + dot(joined, proj_ref[...])).astype(bf16)
        inner_ref[...] = inner
        normed_ref[...] = norm_rows(inner.astype(f32), gains_ref[gain : gain + 1, :])

    def hidden(normed, j):
        return gelu(dot(normed, up_ref[:, HID * j : HID * (j + 1)])).astype(bf16)

    def down(part, j):
        return dot(part, down_ref[HID * j : HID * (j + 1), :])

    def emit(inner, total):
        outer = (inner.astype(f32) + total).astype(bf16)
        for t in range(UNIT_TILES):
            slot = table_ref[(step - 1) * UNIT_TILES + t]

            @pl.when(slot >= 0)
            def _():
                out_ref[jnp.maximum(slot, 0)] = outer[t * PART : (t + 1) * PART]

    @pl.when(step == 0)
    def _():
        scores, soften, mix = attention_parts()
        mixed = []
        s = scores(0)
        for h in range(HEADS):
            later = scores(h + 1) if h + 1 < HEADS else None
            mixed.append(mix(h, soften(s)))
            s = later
        join(mixed)

    @pl.when((step > 0) & (step < units))
    def _():
        scores, soften, mix = attention_parts()
        inner, normed = inner_ref[...], normed_ref[...]
        mixed = []
        total = None
        s = scores(0)
        for h in range(HEADS):
            later = scores(h + 1) if h + 1 < HEADS else None
            part = hidden(normed, h)
            mixed.append(mix(h, soften(s)))
            one = down(part, h)
            total = one if total is None else total + one
            s = later
        emit(inner, total)
        join(mixed)

    @pl.when(step == units)
    def _():
        inner, normed = inner_ref[...], normed_ref[...]
        total = None
        for h in range(HEADS):
            one = down(hidden(normed, h), h)
            total = one if total is None else total + one
        emit(inner, total)


def block(name, table, x, q, keys, values, x_spec, key_spec, units, masked, layer, weights):
    gains, proj_weight, up_weight, down_weight = weights
    pieces = len(keys)
    count = UNIT_TILES * PART
    return pl.pallas_call(
        functools.partial(block_kernel, units, masked, 2 * layer + 1, pieces),
        grid_spec=pltpu.PrefetchScalarGridSpec(
            num_scalar_prefetch=1,
            grid=(units + 1,),
            in_specs=[x_spec, x_spec]
            + [key_spec] * (2 * pieces)
            + [
                whole((4, D)),
                layer_of((D, D), layer),
                layer_of((D, FF), layer),
                layer_of((FF, D), layer),
            ],
            out_specs=whole((PEERS, PART, D)),
            scratch_shapes=[pltpu.VMEM((count, D), bf16), pltpu.VMEM((count, D), bf16)],
        ),
        out_shape=jax.ShapeDtypeStruct((PEERS, PART, D), bf16),
        name=name,
    )(table, x, q, *keys, *values, gains, proj_weight, up_weight, down_weight)


def last_unit(i, units):
    return jnp.minimum(i, units - 1)


def block_a(chunk, table, x, q, keys, values, weights):
    units = TILES_DEV // UNIT_TILES
    x_spec = pl.BlockSpec(
        (UNIT_TILES, PART, D), lambda i, *_: (last_unit(i, units), chunk, 0)
    )
    key_spec = pl.BlockSpec((PATCH, D), lambda i, *_: ((last_unit(i, units) + 1) // 2, 0))
    return block(
        "block_a", table, x, q, [keys], [values], x_spec, key_spec, units, False, 0, weights
    )


def block_b(table, x, q, keys, values, weights):
    units = SLOTS // UNIT_TILES
    x_spec = pl.BlockSpec((UNIT_TILES, PART, D), lambda i, *_: (last_unit(i, units), 0, 0))
    key_spec = pl.BlockSpec(
        (PATCH_TILES, PART, D), lambda i, *_: (last_unit(i, units) // 2, 0, 0)
    )
    return block(
        "block_b", table, x, q, keys, values, x_spec, key_spec, units, True, 1, weights
    )


def home_kernel(table_ref, *refs):
    parts, out_ref, sems = refs[:CHUNKS], refs[CHUNKS], refs[CHUNKS + 1]
    copies = []
    for c, part_ref in enumerate(parts):
        for t in range(TILES_DEV):
            copies.append(
                pltpu.make_async_copy(
                    part_ref.at[table_ref[t]],
                    out_ref.at[t, pl.ds(c * PART, PART)],
                    sems.at[c * TILES_DEV + t],
                )
            )
    for copy in copies:
        copy.start()
    for copy in copies:
        copy.wait()


def home(table, parts):
    return pl.pallas_call(
        home_kernel,
        grid_spec=pltpu.PrefetchScalarGridSpec(
            num_scalar_prefetch=1,
            grid=(1,),
            in_specs=[pl.BlockSpec(memory_space=pl.ANY)] * CHUNKS,
            out_specs=pl.BlockSpec(memory_space=pl.ANY),
            scratch_shapes=[pltpu.SemaphoreType.DMA((CHUNKS * TILES_DEV,))],
        ),
        out_shape=jax.ShapeDtypeStruct((TILES_DEV, TILE, D), bf16),
        name="home",
    )(table, *parts)


def exchange(part):
    return lax.all_to_all(part, "chain", split_axis=0, concat_axis=0, tiled=True)


def body(
    points, norm_gains, qkv_weight, proj_weight, up_weight, down_weight, dest_slot, owner_from
):
    rows = points.shape[0]
    axes = ("chain", "group")
    ring = lax.axis_size(axes)
    before = lax.ppermute(points[rows - HALF :], axes, [(i, (i + 1) % ring) for i in range(ring)])
    after = lax.ppermute(points[:HALF], axes, [((i + 1) % ring, i) for i in range(ring)])
    weights = (norm_gains, proj_weight, up_weight, down_weight)
    q, keys, values = qkv_own(points, norm_gains, qkv_weight)
    keys, values = qkv_halo(before, after, norm_gains, qkv_weight, keys, values)
    tiled = (TILES_DEV, TILE, D)
    x, q = points.reshape(tiled), q.reshape(tiled)
    sent = []
    for chunk in range(CHUNKS):
        packed = block_a(chunk, dest_slot, x, q, keys, values, weights)
        sent.append(exchange(packed))
    owned = [qkv_owner(owner_from, part, norm_gains, qkv_weight) for part in sent]
    owner_keys = [one[2] for one in owned]
    owner_values = [one[3] for one in owned]
    returned = []
    for chunk in range(CHUNKS):
        done = block_b(
            owner_from, owned[chunk][0], owned[chunk][1], owner_keys, owner_values, weights
        )
        returned.append(exchange(done))
    return home(dest_slot, returned).reshape(rows, D)


def solution(mesh):
    placed = (
        P(("chain", "group"), None),
        P(),
        P(),
        P(),
        P(),
        P(),
        P(("chain", "group")),
        P(("chain", "group")),
    )
    return jax.shard_map(
        body, mesh=mesh, in_specs=placed, out_specs=P(("chain", "group"), None), check_vma=False
    )
```

time: 405 us -> 251 us (0.62); the launches traced: 398 us -> 249 us
  matrix products: 230 us -> 0 us
  Pallas kernels: 0 us -> 165 us
  waiting for transfers between devices: 83.1 us -> 28.1 us
  local copies, waits for them, and re-layouts: 51.3 us -> 4.22 us
  blocking collectives: 0 us -> 30 us
  other arithmetic: 16.3 us -> 0 us
  starting transfers between devices: 16.4 us -> 20.9 us
    pallas_call x0 -> x9, Pallas kernels: none -> 165 us  [the longest x4 93 us: block(): pl.pallas_call(functools.partial(block_kernel, units, masked, 2 * layer +...]
    dot_general x20 -> x0, matrix products: 154 us -> none  [the longest x8 93.7 us: residual_add(): jnp.dot(mixed, weights, preferred_element_type=jnp.float32)]
    sub x6 -> x0, matrix products: 76.7 us -> none  [attend(): exponent = jnp.exp(scores - peak)]
    all_to_all x2 -> x3, waiting for transfers between devices: 83.1 us -> 21.7 us  [exchange(): lax.all_to_all(part, 'chain', split_axis=0, concat_axis=0, tiled=True)]
    all_to_all x0 -> x1, blocking collectives: none -> 30 us  [exchange(): lax.all_to_all(part, 'chain', split_axis=0, concat_axis=0, tiled=True)]
    slice x19 -> x1, local copies, waits for them, and re-layouts: 24.2 us -> 1.19 us  [body(): points[:HALF]]
    unnamed x63 -> x10, local copies, waits for them, and re-layouts: 10.9 us -> 3.03 us
    ppermute x2, waiting for transfers between devices: 0.01 us -> 6.33 us  [the longest x1 6.33 us: body(): lax.ppermute(points[rows - HALF:], axes, [(i, (i + 1) % ring) for i in ra...]
  transfers between devices with their start and end apart: 4 -> 5, of which waited for: 2 -> 3; matrix products, arithmetic and copies ran while one was open for 7% -> 0% of each run, Pallas kernels for 0% -> 24%
where the time goes in v1:
time: 251 us; the launch traced here: 249 us
  Pallas kernels  165 us (66%)
  blocking collectives  30 us (12%)
  waiting for transfers between devices  28.1 us (11%)
  starting transfers between devices  20.9 us (8%)
  local copies, waits for them, and re-layouts  4.22 us (2%)
    pallas_call x4, Pallas kernels, block(): pl.pallas_call(functools.partial(block_kernel, units, masked, 2 * layer +...  93 us
    pallas_call x1, Pallas kernels, home(): pl.pallas_call(home_kernel, grid_spec=pltpu.PrefetchScalarGridSpec(num_sc...  49.7 us
    all_to_all x1, blocking collectives, exchange(): lax.all_to_all(part, 'chain', split_axis=0, concat_axis=0, tiled=True)  30 us
    all_to_all x3, waiting for transfers between devices, exchange(): lax.all_to_all(part, 'chain', split_axis=0, concat_axis=0, tiled=True)  21.7 us
    all_to_all x3, starting transfers between devices, exchange(): lax.all_to_all(part, 'chain', split_axis=0, concat_axis=0, tiled=True)  12.6 us
    pallas_call x2, Pallas kernels, qkv_owner(): pl.pallas_call(qkv_owner_kernel, grid_spec=pltpu.PrefetchScalarGridSpec(n...  12.4 us
    ppermute x1, starting transfers between devices, body(): lax.ppermute(points[:HALF], axes, [((i + 1) % ring, i) for i in range(rin...  8.31 us
    ppermute x1, waiting for transfers between devices, body(): lax.ppermute(points[rows - HALF:], axes, [(i, (i + 1) % ring) for i in ra...  6.33 us
  transfers between devices with their start and end apart: 5, of which 3 were waited for; matrix products, arithmetic and copies ran while one was open for 0% of the time, Pallas kernels for 24%

profile of v1, /device:TPU:0, one launch (start us, length us, event | category | flops | bytes accessed | tf_op | source)
XLA Modules:
  0.0 248.8 jit_solution(3224252284013461664)
XLA Ops:
  0.0 1.2 fusion
  1.2 8.3 %collective-permute-start.1 = (bf16[512,384]{1,0:T(8,128)(2,1)S(1)}, bf16[512,384]{1,0:T(8,128)(2,1)S(1)}, u32[]{:S(2)}, u32[]{:S(2)}) collective-permute-start(bf16[512,384]{1,0:T(8,128)(2,1)S(1)} %get-tuple-element.31), channel_id=1, source_target_pairs={{1,0},{2,1},{3,2},{4,3},{5,4},{6,5},{7,6},{8,7},{9,8},{10,9},{11,1... | collective-permute-start | bytes 1179656 | tf_op jit(solution)/shard_map/ppermute | solution.py:365
  9.5 0.0 collective-permute-start
  9.5 6.3 %qkv_own.1 = (bf16[2048,384]{1,0:T(8,128)(2,1)}, bf16[3072,384]{1,0:T(8,128)(2,1)}, bf16[3072,384]{1,0:T(8,128)(2,1)}) custom-call(bf16[2048,384]{1,0:T(8,128)(2,1)} %x_ref.1, f32[4,384]{1,0:T(4,128)} %refs_4_.7, bf16[2,384,1152]{2,1,0:T(8,128)(2,1)} %w_ref.7), custom_call_target="tpu_custom_call" | custom-call | tf_op jit(solution)/shard_map/qkv_own/pallas_call | solution.py:73
  15.8 0.0 collective-permute-done.1.b_ref
  15.8 0.0 copy-start.3
  15.8 6.3 %collective-permute-done.a_ref = bf16[512,384]{1,0:T(8,128)(2,1)S(1)} collective-permute-done((bf16[512,384]{1,0:T(8,128)(2,1)S(1)}, bf16[512,384]{1,0:T(8,128)(2,1)S(1)}, u32[]{:S(2)}, u32[]{:S(2)}) %collective-permute-start) | collective-permute-done | bytes 393248 | tf_op jit(solution)/shard_map/ppermute | solution.py:364
  22.1 0.0 copy-start.4
  22.1 0.0 copy-done.3
  22.1 0.7 copy-done.4
  22.9 4.0 %qkv_halo.1 = (bf16[3072,384]{1,0:T(8,128)(2,1)}, bf16[3072,384]{1,0:T(8,128)(2,1)}) custom-call(bf16[512,384]{1,0:T(8,128)(2,1)} %copy-done.4, bf16[512,384]{1,0:T(8,128)(2,1)} %copy-done.3, f32[4,384]{1,0:T(4,128)} %refs_4_.7, bf16[2,384,1152]{2,1,0:T(8,128)(2,1)} %w_ref.7, ...), custom_call_target="tpu_custom_call", output_to_operand_aliasing={{0}: (4, {}), {1}: (5, {})} | custom-call | tf_op jit(solution)/shard_map/qkv_halo/pallas_call | solution.py:103
  26.8 19.4 %block_a.3 = bf16[32,64,384]{2,1,0:T(8,128)(2,1)} custom-call(s32[16]{0:T(128)} %table_ref.9, bf16[16,128,384]{2,1,0:T(8,128)(2,1)} %bitcast.3, bf16[16,128,384]{2,1,0:T(8,128)(2,1)} %bitcast.5, bf16[3072,384]{1,0:T(8,128)(2,1)} %get-tuple-element.21.refs_0_, bf16[3072,384]{1,0:T(8,128)(2,1)} %get-tuple-element.22.refs_1_, f32[4,384]{1,0:T(4,128)} %refs_4_.7, ...), custom_call_target="tpu_custom_call" | custom-call | tf_op jit(solution)/shard_map/block_a/pallas_call | solution.py:274
  46.3 4.2 %all-to-all-start.1 = ((bf16[32,64,384]{2,1,0:T(8,128)(2,1)}), bf16[32,64,384]{2,1,0:T(8,128)(2,1)S(1)}, u32[]{:S(2)}, u32[]{:S(2)}) async-start(bf16[32,64,384]{2,1,0:T(8,128)(2,1)} %block_a.3), calls=%async_computation.1 | async-start | bytes 3145728 | tf_op jit(solution)/shard_map/all_to_all | solution.py:355
  50.4 19.5 %block_a.2 = bf16[32,64,384]{2,1,0:T(8,128)(2,1)} custom-call(s32[16]{0:T(128)} %table_ref.9, bf16[16,128,384]{2,1,0:T(8,128)(2,1)} %bitcast.4, bf16[16,128,384]{2,1,0:T(8,128)(2,1)} %bitcast.6, bf16[3072,384]{1,0:T(8,128)(2,1)} %get-tuple-element.21.refs_0_, bf16[3072,384]{1,0:T(8,128)(2,1)} %get-tuple-element.22.refs_1_, f32[4,384]{1,0:T(4,128)} %refs_4_.7, ...), custom_call_target="tpu_custom_call" | custom-call | tf_op jit(solution)/shard_map/block_a/pallas_call | solution.py:274
  69.9 4.3 %all-to-all-done.1.part_ref = bf16[32,64,384]{2,1,0:T(8,128)(2,1)S(1)} async-done(((bf16[32,64,384]{2,1,0:T(8,128)(2,1)}), bf16[32,64,384]{2,1,0:T(8,128)(2,1)S(1)}, u32[]{:S(2)}, u32[]{:S(2)}) %all-to-all-start.1) | async-done | bytes 1572896 | tf_op jit(solution)/shard_map/all_to_all | solution.py:355
  74.1 0.0 copy-start
  74.1 1.1 copy-done
  75.3 4.2 %all-to-all-start = ((bf16[32,64,384]{2,1,0:T(8,128)(2,1)}), bf16[32,64,384]{2,1,0:T(8,128)(2,1)S(1)}, u32[]{:S(2)}, u32[]{:S(2)}) async-start(bf16[32,64,384]{2,1,0:T(8,128)(2,1)} %block_a.2), calls=%async_computation | async-start | bytes 3145728 | tf_op jit(solution)/shard_map/all_to_all | solution.py:355
  79.5 6.2 %qkv_owner.3 = (bf16[24,64,384]{2,1,0:T(8,128)(2,1)}, bf16[24,64,384]{2,1,0:T(8,128)(2,1)}, bf16[24,64,384]{2,1,0:T(8,128)(2,1)}, bf16[24,64,384]{2,1,0:T(8,128)(2,1)}) custom-call(s32[24]{0:T(128)} %table_ref.8, bf16[32,64,384]{2,1,0:T(8,128)(2,1)} %copy-done, f32[4,384]{1,0:T(4,128)} %refs_4_.7, bf16[2,384,1152]{2,1,0:T(8,128)(2,1)} %w_ref.7), custom_call_target="tpu_custom_call" | custom-call | tf_op jit(solution)/shard_map/qkv_owner/pallas_call | solution.py:141
  85.7 17.5 %all-to-all-done.part_ref = bf16[32,64,384]{2,1,0:T(8,128)(2,1)S(1)} async-done(((bf16[32,64,384]{2,1,0:T(8,128)(2,1)}), bf16[32,64,384]{2,1,0:T(8,128)(2,1)S(1)}, u32[]{:S(2)}, u32[]{:S(2)}) %all-to-all-start) | async-done | bytes 1572896 | tf_op jit(solution)/shard_map/all_to_all | solution.py:355
  103.2 0.0 copy-start.1
  103.2 1.1 copy-done.1
  104.3 6.2 %qkv_owner.2 = (bf16[24,64,384]{2,1,0:T(8,128)(2,1)}, bf16[24,64,384]{2,1,0:T(8,128)(2,1)}, bf16[24,64,384]{2,1,0:T(8,128)(2,1)}, bf16[24,64,384]{2,1,0:T(8,128)(2,1)}) custom-call(s32[24]{0:T(128)} %table_ref.8, bf16[32,64,384]{2,1,0:T(8,128)(2,1)} %copy-done.1, f32[4,384]{1,0:T(4,128)} %refs_4_.7, bf16[2,384,1152]{2,1,0:T(8,128)(2,1)} %w_ref.7), custom_call_target="tpu_custom_call" | custom-call | tf_op jit(solution)/shard_map/qkv_owner/pallas_call | solution.py:141
  110.5 27.0 %block_b.2 = bf16[32,64,384]{2,1,0:T(8,128)(2,1)} custom-call(s32[24]{0:T(128)} %table_ref.8, bf16[24,64,384]{2,1,0:T(8,128)(2,1)} %get-tuple-element.23.x_ref, bf16[24,64,384]{2,1,0:T(8,128)(2,1)} %get-tuple-element.24.q_ref, bf16[24,64,384]{2,1,0:T(8,128)(2,1)} %get-tuple-element.25.refs_0_, bf16[24,64,384]{2,1,0:T(8,128)(2,1)} %get-tuple-element.26.refs_1_, ...), custom_call_target="tpu_custom_call" | custom-call | tf_op jit(solution)/shard_map/block_b/pallas_call | solution.py:274
  137.5 4.2 %all-to-all-start.2 = ((bf16[32,64,384]{2,1,0:T(8,128)(2,1)}), bf16[32,64,384]{2,1,0:T(8,128)(2,1)S(1)}, u32[]{:S(2)}, u32[]{:S(2)}) async-start(bf16[32,64,384]{2,1,0:T(8,128)(2,1)} %block_b.2), calls=%async_computation.2 | async-start | bytes 3145728 | tf_op jit(solution)/shard_map/all_to_all | solution.py:355
  141.8 27.1 %block_b.3 = bf16[32,64,384]{2,1,0:T(8,128)(2,1)} custom-call(s32[24]{0:T(128)} %table_ref.8, bf16[24,64,384]{2,1,0:T(8,128)(2,1)} %get-tuple-element.29.x_ref, bf16[24,64,384]{2,1,0:T(8,128)(2,1)} %get-tuple-element.30.q_ref, bf16[24,64,384]{2,1,0:T(8,128)(2,1)} %get-tuple-element.25.refs_0_, bf16[24,64,384]{2,1,0:T(8,128)(2,1)} %get-tuple-element.26.refs_1_, ...), custom_call_target="tpu_custom_call" | custom-call | tf_op jit(solution)/shard_map/block_b/pallas_call | solution.py:274
  168.9 0.0 all-to-all-done.2.refs_0_
  168.9 0.0 copy-start.2
  168.9 30.0 %all_to_all.20.refs_1_ = bf16[32,64,384]{2,1,0:T(8,128)(2,1)} all-to-all(bf16[32,64,384]{2,1,0:T(8,128)(2,1)} %block_b.3), channel_id=1, replica_groups=mesh['chain'=32,'group'=4] {'chain'}, dimensions={0} | all-to-all | bytes 3145728 | tf_op jit(solution)/shard_map/all_to_all | solution.py:355
  198.9 0.0 copy-done.2
  198.9 49.7 %home.1 = bf16[16,128,384]{2,1,0:T(8,128)(2,1)} custom-call(s32[16]{0:T(128)} %table_ref.9, bf16[32,64,384]{2,1,0:T(8,128)(2,1)} %copy-done.2, bf16[32,64,384]{2,1,0:T(8,128)(2,1)} %all_to_all.20.refs_1_), custom_call_target="tpu_custom_call" | custom-call | tf_op jit(solution)/shard_map/home/pallas_call | solution.py:340
Async XLA Ops:
  1.2 14.6 %collective-permute-start.1 = (bf16[512,384]{1,0:T(8,128)(2,1)S(1)}, bf16[512,384]{1,0:T(8,128)(2,1)S(1)}, u32[]{:S(2)}, u32[]{:S(2)}) collective-permute-start(bf16[512,384]{1,0:T(8,128)(2,1)S(1)} %get-tuple-element.31), channel_id=1, source_target_pairs={{1,0},{2,1},{3,2},{4,3},{5,4},{6,5},{7,6},{8,7},{9,8},{10,9},{11,1... | collective-permute-start | bytes 1179656 | tf_op jit(solution)/shard_map/ppermute | solution.py:365
  9.5 12.6 %collective-permute-start = (bf16[512,384]{1,0:T(8,128)(2,1)S(1)}, bf16[512,384]{1,0:T(8,128)(2,1)S(1)}, u32[]{:S(2)}, u32[]{:S(2)}) collective-permute-start(bf16[512,384]{1,0:T(8,128)(2,1)S(1)} %get-tuple-element.32), channel_id=1, source_target_pairs={{0,1},{1,2},{2,3},{3,4},{4,5},{5,6},{6,7},{7,8},{8,9},{9,10},{10,1... | collective-permute-start | bytes 1179656 | tf_op jit(solution)/shard_map/ppermute | solution.py:364
  15.8 6.3 %copy-start.3 = (bf16[512,384]{1,0:T(8,128)(2,1)}, bf16[512,384]{1,0:T(8,128)(2,1)S(1)}, u32[]{:S(2)}) copy-start(bf16[512,384]{1,0:T(8,128)(2,1)S(1)} %collective-permute-done.1.b_ref) | copy-start | bytes 1179652
  22.1 0.7 copy-start.4
  46.3 27.9 %all-to-all-start.1 = ((bf16[32,64,384]{2,1,0:T(8,128)(2,1)}), bf16[32,64,384]{2,1,0:T(8,128)(2,1)S(1)}, u32[]{:S(2)}, u32[]{:S(2)}) async-start(bf16[32,64,384]{2,1,0:T(8,128)(2,1)} %block_a.3), calls=%async_computation.1 | async-start | bytes 3145728 | tf_op jit(solution)/shard_map/all_to_all | solution.py:355
  74.1 1.1 copy-start
  75.3 27.9 %all-to-all-start = ((bf16[32,64,384]{2,1,0:T(8,128)(2,1)}), bf16[32,64,384]{2,1,0:T(8,128)(2,1)S(1)}, u32[]{:S(2)}, u32[]{:S(2)}) async-start(bf16[32,64,384]{2,1,0:T(8,128)(2,1)} %block_a.2), calls=%async_computation | async-start | bytes 3145728 | tf_op jit(solution)/shard_map/all_to_all | solution.py:355
  103.2 1.1 copy-start.1
  137.5 31.3 %all-to-all-start.2 = ((bf16[32,64,384]{2,1,0:T(8,128)(2,1)}), bf16[32,64,384]{2,1,0:T(8,128)(2,1)S(1)}, u32[]{:S(2)}, u32[]{:S(2)}) async-start(bf16[32,64,384]{2,1,0:T(8,128)(2,1)} %block_b.2), calls=%async_computation.2 | async-start | bytes 3145728 | tf_op jit(solution)/shard_map/all_to_all | solution.py:355
  168.9 30.0 %copy-start.2 = (bf16[32,64,384]{2,1,0:T(8,128)(2,1)}, bf16[32,64,384]{2,1,0:T(8,128)(2,1)S(1)}, u32[]{:S(2)}) copy-start(bf16[32,64,384]{2,1,0:T(8,128)(2,1)S(1)} %all-to-all-done.2.refs_0_) | copy-start | bytes 4718596

commit v2 on v1

v2 whole, which is shorter than its diff:
```python
import functools

import jax
import jax.numpy as jnp
from jax import lax
from jax.experimental import pallas as pl
from jax.experimental.pallas import tpu as pltpu
from jax.sharding import PartitionSpec as P

D = 384
HEADS = 6
HEAD_DIM = 64
FF = 1536
PATCH = 1024
TILE = 128
TILES_DEV = 16
SLOTS = 24
PEERS = 32
PAIRS = HEADS // 2
CHUNKS = 2
PART = TILE // CHUNKS
PATCH_TILES = PATCH // TILE
UNIT_TILES = 4
HALF = PATCH // 2
HID = 256

norm_epsilon = 1e-05
masked_score = -1000000000.0
query_scale = HEAD_DIM ** (-0.5) * 1.4426950408889634
f32 = jnp.float32
bf16 = jnp.bfloat16


def norm_rows(values, gain_row):
    center = values - jnp.mean(values, axis=-1, keepdims=True)
    spread = jnp.mean(center * center, axis=-1, keepdims=True)
    return (center * lax.rsqrt(spread + norm_epsilon) * gain_row).astype(bf16)


def gelu(x):
    return (0.5 * x) * (1.0 + lax.erf(x * 0.5 ** 0.5))


def dot(a, b):
    return jnp.dot(a, b, preferred_element_type=f32)


def dot_t(a, b):
    return lax.dot_general(a, b, (((1,), (1,)), ((), ())), preferred_element_type=f32)


def dot_lead(a, b):
    return lax.dot_general(a, b, (((0,), (0,)), ((), ())), preferred_element_type=f32)


def dot_cross(a, b):
    return lax.dot_general(a, b, (((0,), (1,)), ((), ())), preferred_element_type=f32)


def whole(shape):
    zeros = (0,) * len(shape)
    return pl.BlockSpec(shape, lambda *_: zeros)


def layer_of(shape, layer):
    zeros = (0,) * len(shape)
    return pl.BlockSpec((None, *shape), lambda *_: (layer, *zeros))


def qkv_own_kernel(x_ref, gains_ref, w_ref, q_ref, k_ref, v_ref):
    normed = norm_rows(x_ref[...].astype(f32), gains_ref[0:1, :])
    out = dot(normed, w_ref[:, : 2 * D])
    q_ref[...] = (out[:, :D] * query_scale).astype(bf16)
    k_ref[...] = out[:, D:].astype(bf16)
    v_ref[...] = dot_cross(w_ref[:, 2 * D :], normed).astype(bf16)


def qkv_own(points, gains, qkv_weight):
    rows = points.shape[0]
    return pl.pallas_call(
        qkv_own_kernel,
        grid=(rows // HALF,),
        in_specs=[
            pl.BlockSpec((HALF, D), lambda i: (i, 0)),
            whole((4, D)),
            layer_of((D, 3 * D), 0),
        ],
        out_specs=[
            pl.BlockSpec((HALF, D), lambda i: (i, 0)),
            pl.BlockSpec((HALF, D), lambda i: (i + 1, 0)),
            pl.BlockSpec((D, HALF), lambda i: (0, i + 1)),
        ],
        out_shape=[
            jax.ShapeDtypeStruct((rows, D), bf16),
            jax.ShapeDtypeStruct((rows + PATCH, D), bf16),
            jax.ShapeDtypeStruct((D, rows + PATCH), bf16),
        ],
        name="qkv_own",
    )(points, gains, qkv_weight)


def qkv_halo_kernel(a_ref, b_ref, gains_ref, w_ref, k_in, v_in, k_ref, v_ref):
    first = pl.program_id(0) == 0
    rows = jnp.where(first, a_ref[...].astype(f32), b_ref[...].astype(f32))
    normed = norm_rows(rows, gains_ref[0:1, :])
    k_ref[...] = dot(normed, w_ref[:, D : 2 * D]).astype(bf16)
    v_ref[...] = dot_cross(w_ref[:, 2 * D :], normed).astype(bf16)


def qkv_halo(before, after, gains, qkv_weight, keys, values):
    last = keys.shape[0] // HALF - 1
    return pl.pallas_call(
        qkv_halo_kernel,
        grid=(2,),
        in_specs=[
            whole((HALF, D)),
            whole((HALF, D)),
            whole((4, D)),
            layer_of((D, 3 * D), 0),
            pl.BlockSpec(memory_space=pl.ANY),
            pl.BlockSpec(memory_space=pl.ANY),
        ],
        out_specs=[
            pl.BlockSpec((HALF, D), lambda i: (i * last, 0)),
            pl.BlockSpec((D, HALF), lambda i: (0, i * last)),
        ],
        out_shape=[
            jax.ShapeDtypeStruct(keys.shape, bf16),
            jax.ShapeDtypeStruct(values.shape, bf16),
        ],
        input_output_aliases={4: 0, 5: 1},
        name="qkv_halo",
    )(before, after, gains, qkv_weight, keys, values)


def qkv_owner_kernel(from_ref, part_ref, gains_ref, w_ref, x_ref, q_ref, k_ref, v_ref):
    step = pl.program_id(0)
    tiles = []
    for t in range(PATCH_TILES):
        source = from_ref[step * PATCH_TILES + t]
        tile = part_ref[jnp.maximum(source, 0)]
        tiles.append(jnp.where(source >= 0, tile.astype(f32), 0.0))
    rows = jnp.concatenate(tiles, axis=0)
    shape = (PATCH_TILES, PART, D)
    x_ref[...] = rows.astype(bf16).reshape(shape)
    normed = norm_rows(rows, gains_ref[2:3, :])
    out = dot(normed, w_ref[:, : 2 * D])
    q_ref[...] = (out[:, :D] * query_scale).astype(bf16).reshape(shape)
    k_ref[...] = out[:, D:].astype(bf16).reshape(shape)
    v_ref[...] = dot_cross(w_ref[:, 2 * D :], normed).astype(bf16)


def qkv_owner(owner_from, part, gains, qkv_weight):
    patches = SLOTS // PATCH_TILES
    count = PATCH_TILES * PART
    block = pl.BlockSpec((PATCH_TILES, PART, D), lambda i, *_: (i, 0, 0))
    shape = jax.ShapeDtypeStruct((SLOTS, PART, D), bf16)
    return pl.pallas_call(
        qkv_owner_kernel,
        grid_spec=pltpu.PrefetchScalarGridSpec(
            num_scalar_prefetch=1,
            grid=(patches,),
            in_specs=[
                pl.BlockSpec(memory_space=pltpu.VMEM),
                whole((4, D)),
                layer_of((D, 3 * D), 1),
            ],
            out_specs=[block] * 3 + [pl.BlockSpec((None, D, count), lambda i, *_: (i, 0, 0))],
        ),
        out_shape=[shape] * 3 + [jax.ShapeDtypeStruct((patches, D, count), bf16)],
        compiler_params=pltpu.CompilerParams(vmem_limit_bytes=24 << 20),
        name="qkv_owner",
    )(owner_from, part, gains, qkv_weight)


def block_kernel(units, masked, layer, pieces, table_ref, x_ref, q_ref, *refs):
    k_refs, refs = refs[:pieces], refs[pieces:]
    v_refs, refs = refs[:pieces], refs[pieces:]
    gains_ref, *sources, out_ref, mixed_ref, proj_ref, up_ref, down_ref, sems = refs
    step = pl.program_id(0)
    count = UNIT_TILES * PART
    rows = PATCH // pieces
    lanes = lax.broadcasted_iota(jnp.int32, (1, 128), 1)
    low = lanes < HEAD_DIM
    picks = [low.astype(f32).astype(bf16), (~low).astype(f32).astype(bf16)]
    fetches = [
        pltpu.make_async_copy(source.at[layer], target, sems.at[i])
        for i, (source, target) in enumerate(zip(sources, (proj_ref, up_ref, down_ref)))
    ]

    def attention_parts():
        queries = q_ref[...].reshape(count, D)
        ones = jnp.ones((16, rows), bf16)
        extra_q = extra_k = None
        if masked:
            base = (step * UNIT_TILES) // PATCH_TILES * PATCH_TILES
            extra_q = jnp.broadcast_to((lanes == 0).astype(f32).astype(bf16), (count, 128))
            marks = []
            for t in range(PATCH_TILES):
                mark = jnp.where(table_ref[base + t] >= 0, 0.0, masked_score)
                marks.append(jnp.full((rows // PATCH_TILES, 128), mark, f32).astype(bf16))
            extra_k = jnp.concatenate(marks, axis=0)

        def scores(h):
            cols = slice(128 * (h // 2), 128 * (h // 2) + 128)
            q = queries[:, cols] * picks[h % 2]
            if masked:
                q = jnp.concatenate([q, extra_q], axis=1)
            out = []
            for k_ref in k_refs:
                k = k_ref[...].reshape(rows, D)[:, cols]
                if masked:
                    k = jnp.concatenate([k, extra_k], axis=1)
                out.append(dot_t(k, q))
            return out

        def soften(parts):
            peak = functools.reduce(
                jnp.maximum, [jnp.max(s, axis=0, keepdims=True) for s in parts]
            )
            return [jnp.exp2(s - peak).astype(bf16) for s in parts]

        def mix(h, parts):
            cols = slice(HEAD_DIM * h, HEAD_DIM * (h + 1))
            total = None
            for p, v_ref in zip(parts, v_refs):
                one = dot(jnp.concatenate([v_ref[cols, :], ones], axis=0), p)
                total = one if total is None else total + one
            mixed_ref[cols, :] = (total[:HEAD_DIM] / total[HEAD_DIM : HEAD_DIM + 1]).astype(bf16)

        return scores, soften, mix

    def join(mixed):
        base = x_ref[...].reshape(count, D).astype(f32)
        inner = (base + dot_lead(mixed, proj_ref[...])).astype(bf16)
        gain = gains_ref[2 * layer + 1 : 2 * layer + 2, :]
        return inner, norm_rows(inner.astype(f32), gain)

    def hidden(normed, j):
        return gelu(dot(normed, up_ref[:, HID * j : HID * (j + 1)])).astype(bf16)

    def down(part, j):
        return dot(part, down_ref[HID * j : HID * (j + 1), :])

    def emit(inner, total):
        outer = (inner.astype(f32) + total).astype(bf16)
        for t in range(UNIT_TILES):
            slot = table_ref[(step - 1) * UNIT_TILES + t]

            @pl.when(slot >= 0)
            def _():
                out_ref[jnp.maximum(slot, 0)] = outer[t * PART : (t + 1) * PART]

    @pl.when(step == 0)
    def _():
        for fetch in fetches:
            fetch.start()
        scores, soften, mix = attention_parts()
        s = scores(0)
        for h in range(HEADS):
            later = scores(h + 1) if h + 1 < HEADS else None
            mix(h, soften(s))
            s = later
        for fetch in fetches:
            fetch.wait()

    @pl.when((step > 0) & (step < units))
    def _():
        mixed = mixed_ref[...]
        scores, soften, mix = attention_parts()
        s = scores(0)
        inner, normed = join(mixed)
        total = None
        for h in range(HEADS):
            later = scores(h + 1) if h + 1 < HEADS else None
            part = hidden(normed, h)
            mix(h, soften(s))
            one = down(part, h)
            total = one if total is None else total + one
            s = later
        emit(inner, total)

    @pl.when(step == units)
    def _():
        inner, normed = join(mixed_ref[...])
        total = None
        for h in range(HEADS):
            one = down(hidden(normed, h), h)
            total = one if total is None else total + one
        emit(inner, total)


def block(name, table, x, q, keys, values, specs, units, masked, layer, weights):
    gains, *matrices = weights
    pieces = len(keys)
    count = UNIT_TILES * PART
    x_spec, q_spec, key_spec, value_spec = specs
    return pl.pallas_call(
        functools.partial(block_kernel, units, masked, layer, pieces),
        grid_spec=pltpu.PrefetchScalarGridSpec(
            num_scalar_prefetch=1,
            grid=(units + 1,),
            in_specs=[x_spec, q_spec]
            + [key_spec] * pieces
            + [value_spec] * pieces
            + [whole((4, D))]
            + [pl.BlockSpec(memory_space=pl.ANY)] * len(matrices),
            out_specs=whole((PEERS, PART, D)),
            scratch_shapes=[
                pltpu.VMEM((D, count), bf16),
                pltpu.VMEM((D, D), bf16),
                pltpu.VMEM((D, FF), bf16),
                pltpu.VMEM((FF, D), bf16),
                pltpu.SemaphoreType.DMA((len(matrices),)),
            ],
        ),
        out_shape=jax.ShapeDtypeStruct((PEERS, PART, D), bf16),
        name=name,
    )(table, x, q, *keys, *values, gains, *matrices)


def now(i, units):
    return jnp.minimum(i, units - 1)


def prior(i):
    return jnp.maximum(i - 1, 0)


def block_a(chunk, table, x, q, keys, values, weights):
    units = TILES_DEV // UNIT_TILES
    shape = (UNIT_TILES, PART, D)
    specs = [
        pl.BlockSpec(shape, lambda i, *_: (prior(i), chunk, 0)),
        pl.BlockSpec(shape, lambda i, *_: (now(i, units), chunk, 0)),
        pl.BlockSpec((PATCH, D), lambda i, *_: ((now(i, units) + 1) // 2, 0)),
        pl.BlockSpec((D, PATCH), lambda i, *_: (0, (now(i, units) + 1) // 2)),
    ]
    return block("block_a", table, x, q, [keys], [values], specs, units, False, 0, weights)


def block_b(table, x, q, keys, values, weights):
    units = SLOTS // UNIT_TILES
    shape = (UNIT_TILES, PART, D)
    patch = (PATCH_TILES, PART, D)
    flat = (None, D, PATCH_TILES * PART)
    specs = [
        pl.BlockSpec(shape, lambda i, *_: (prior(i), 0, 0)),
        pl.BlockSpec(shape, lambda i, *_: (now(i, units), 0, 0)),
        pl.BlockSpec(patch, lambda i, *_: (now(i, units) // 2, 0, 0)),
        pl.BlockSpec(flat, lambda i, *_: (now(i, units) // 2, 0, 0)),
    ]
    return block("block_b", table, x, q, keys, values, specs, units, True, 1, weights)


def home_kernel(table_ref, *refs):
    parts, out_ref = refs[:CHUNKS], refs[CHUNKS]
    for t in range(TILES_DEV):
        for c, part_ref in enumerate(parts):
            out_ref[t, c * PART : (c + 1) * PART] = part_ref[table_ref[t]]


def home(table, parts):
    return pl.pallas_call(
        home_kernel,
        grid_spec=pltpu.PrefetchScalarGridSpec(
            num_scalar_prefetch=1,
            grid=(1,),
            in_specs=[pl.BlockSpec(memory_space=pltpu.VMEM)] * CHUNKS,
            out_specs=whole((TILES_DEV, TILE, D)),
        ),
        out_shape=jax.ShapeDtypeStruct((TILES_DEV, TILE, D), bf16),
        compiler_params=pltpu.CompilerParams(vmem_limit_bytes=12 << 20),
        name="home",
    )(table, *parts)


def exchange(part):
    return lax.all_to_all(part, "chain", split_axis=0, concat_axis=0, tiled=True)


def body(
    points, norm_gains, qkv_weight, proj_weight, up_weight, down_weight, dest_slot, owner_from
):
    rows = points.shape[0]
    axes = ("chain", "group")
    ring = lax.axis_size(axes)
    before = lax.ppermute(points[rows - HALF :], axes, [(i, (i + 1) % ring) for i in range(ring)])
    after = lax.ppermute(points[:HALF], axes, [((i + 1) % ring, i) for i in range(ring)])
    weights = (norm_gains, proj_weight, up_weight, down_weight)
    q, keys, values = qkv_own(points, norm_gains, qkv_weight)
    keys, values = qkv_halo(before, after, norm_gains, qkv_weight, keys, values)
    tiled = (TILES_DEV, TILE, D)
    x, q = points.reshape(tiled), q.reshape(tiled)
    sent = []
    for chunk in range(CHUNKS):
        packed = block_a(chunk, dest_slot, x, q, keys, values, weights)
        sent.append(exchange(packed))
    owned = [qkv_owner(owner_from, part, norm_gains, qkv_weight) for part in sent]
    owner_keys = [one[2] for one in owned]
    owner_values = [one[3] for one in owned]
    returned = []
    for chunk in range(CHUNKS):
        done = block_b(
            owner_from, owned[chunk][0], owned[chunk][1], owner_keys, owner_values, weights
        )
        returned.append(exchange(done))
    return home(dest_slot, returned).reshape(rows, D)


def solution(mesh):
    placed = (
        P(("chain", "group"), None),
        P(),
        P(),
        P(),
        P(),
        P(),
        P(("chain", "group")),
        P(("chain", "group")),
    )
    return jax.shard_map(
        body, mesh=mesh, in_specs=placed, out_specs=P(("chain", "group"), None), check_vma=False
    )
```

time: 251 us -> 202 us (0.80)
  Pallas kernels: 165 us -> 111 us
  local copies, waits for them, and re-layouts: 4.22 us -> 10.4 us
    pallas_call x1, Pallas kernels: 49.7 us -> 1.82 us  [home(): pl.pallas_call(home_kernel, grid_spec=pltpu.PrefetchScalarGridSpec(num_sc...]
    unnamed x10 -> x28, local copies, waits for them, and re-layouts: 3.03 us -> 9.16 us
    pallas_call x2, Pallas kernels: 12.4 us -> 8.41 us  [qkv_owner(): pl.pallas_call(qkv_owner_kernel, grid_spec=pltpu.PrefetchScalarGridSpec(n...]
    pallas_call x4, Pallas kernels: 93 us -> 90.4 us  [block(): pl.pallas_call(functools.partial(block_kernel, units, masked, layer, piec...]
  transfers between devices with their start and end apart: 5 -> 5, of which waited for: 3 -> 3; matrix products, arithmetic and copies ran while one was open for 0% -> 0% of each run, Pallas kernels for 24% -> 28%
where the time goes in v2:
time: 202 us; the launch traced here: 200 us
  Pallas kernels  111 us (55%)
  blocking collectives  30 us (15%)
  waiting for transfers between devices  27.3 us (14%)
  starting transfers between devices  21.6 us (11%)
  local copies, waits for them, and re-layouts  10.4 us (5%)
    pallas_call x4, Pallas kernels, block(): pl.pallas_call(functools.partial(block_kernel, units, masked, layer, piec...  90.4 us
    all_to_all x1, blocking collectives, exchange(): lax.all_to_all(part, 'chain', split_axis=0, concat_axis=0, tiled=True)  30 us
    all_to_all x3, waiting for transfers between devices, exchange(): lax.all_to_all(part, 'chain', split_axis=0, concat_axis=0, tiled=True)  21.1 us
    all_to_all x3, starting transfers between devices, exchange(): lax.all_to_all(part, 'chain', split_axis=0, concat_axis=0, tiled=True)  13.3 us
    unnamed x28, local copies, waits for them, and re-layouts  9.16 us
    pallas_call x2, Pallas kernels, qkv_owner(): pl.pallas_call(qkv_owner_kernel, grid_spec=pltpu.PrefetchScalarGridSpec(n...  8.41 us
    ppermute x1, starting transfers between devices, body(): lax.ppermute(points[:HALF], axes, [((i + 1) % ring, i) for i in range(rin...  8.31 us
    pallas_call x1, Pallas kernels, qkv_own(): pl.pallas_call(qkv_own_kernel, grid=(rows // HALF,), in_specs=[pl.BlockSp...  6.49 us
  transfers between devices with their start and end apart: 5, of which 3 were waited for; matrix products, arithmetic and copies ran while one was open for 0% of the time, Pallas kernels for 28%

profile of v2, /device:TPU:0, one launch (start us, length us, event | category | flops | bytes accessed | tf_op | source)
XLA Modules:
  0.0 200.4 jit_solution(15260814999923464994)
XLA Ops:
  0.0 1.2 fusion
  1.2 8.3 %collective-permute-start.1 = (bf16[512,384]{1,0:T(8,128)(2,1)S(1)}, bf16[512,384]{1,0:T(8,128)(2,1)S(1)}, u32[]{:S(2)}, u32[]{:S(2)}) collective-permute-start(bf16[512,384]{1,0:T(8,128)(2,1)S(1)} %get-tuple-element.31), channel_id=1, source_target_pairs={{1,0},{2,1},{3,2},{4,3},{5,4},{6,5},{7,6},{8,7},{9,8},{10,9},{11,1... | collective-permute-start | bytes 1179656 | tf_op jit(solution)/shard_map/ppermute | solution.py:389
  9.5 0.0 collective-permute-start
  9.5 6.5 %qkv_own.1 = (bf16[2048,384]{1,0:T(8,128)(2,1)}, bf16[3072,384]{1,0:T(8,128)(2,1)}, bf16[384,3072]{1,0:T(8,128)(2,1)}) custom-call(bf16[2048,384]{1,0:T(8,128)(2,1)} %x_ref.1, f32[4,384]{1,0:T(4,128)} %refs_4_.7, bf16[2,384,1152]{2,1,0:T(8,128)(2,1)} %w_ref.7), custom_call_target="tpu_custom_call" | custom-call | tf_op jit(solution)/shard_map/qkv_own/pallas_call | solution.py:80
  16.0 6.1 %collective-permute-done.a_ref = bf16[512,384]{1,0:T(8,128)(2,1)S(1)} collective-permute-done((bf16[512,384]{1,0:T(8,128)(2,1)S(1)}, bf16[512,384]{1,0:T(8,128)(2,1)S(1)}, u32[]{:S(2)}, u32[]{:S(2)}) %collective-permute-start) | collective-permute-done | bytes 393248 | tf_op jit(solution)/shard_map/ppermute | solution.py:388
  22.1 0.8 copy-done.13
  22.9 3.9 %qkv_halo.1 = (bf16[3072,384]{1,0:T(8,128)(2,1)}, bf16[384,3072]{1,0:T(8,128)(2,1)}) custom-call(bf16[512,384]{1,0:T(8,128)(2,1)} %copy-done.13, bf16[512,384]{1,0:T(8,128)(2,1)} %copy-done.12, f32[4,384]{1,0:T(4,128)} %refs_4_.7, bf16[2,384,1152]{2,1,0:T(8,128)(2,1)} %w_ref.7, ...), custom_call_target="tpu_custom_call", output_to_operand_aliasing={{0}: (4, {}), {1}: (5, {})} | custom-call | tf_op jit(solution)/shard_map/qkv_halo/pallas_call | solution.py:112
  26.8 18.5 %block_a.3 = bf16[32,64,384]{2,1,0:T(8,128)(2,1)} custom-call(s32[16]{0:T(128)} %table_ref.9, bf16[16,128,384]{2,1,0:T(8,128)(2,1)} %bitcast.3, bf16[16,128,384]{2,1,0:T(8,128)(2,1)} %bitcast.5, bf16[3072,384]{1,0:T(8,128)(2,1)} %get-tuple-element.21.refs_0_, bf16[384,3072]{1,0:T(8,128)(2,1)} %get-tuple-element.22.refs_1_, f32[4,384]{1,0:T(4,128)} %refs_4_.7, ...), custom_call_target="tpu_custom_call" | custom-call | tf_op jit(solution)/shard_map/block_a/pallas_call | solution.py:298
  45.3 4.2 %all-to-all-start.1 = ((bf16[32,64,384]{2,1,0:T(8,128)(2,1)}), bf16[32,64,384]{2,1,0:T(8,128)(2,1)S(1)}, u32[]{:S(2)}, u32[]{:S(2)}) async-start(bf16[32,64,384]{2,1,0:T(8,128)(2,1)} %block_a.3), calls=%async_computation.1 | async-start | bytes 3145728 | tf_op jit(solution)/shard_map/all_to_all | solution.py:379
  49.5 18.6 %block_a.2 = bf16[32,64,384]{2,1,0:T(8,128)(2,1)} custom-call(s32[16]{0:T(128)} %table_ref.9, bf16[16,128,384]{2,1,0:T(8,128)(2,1)} %bitcast.4, bf16[16,128,384]{2,1,0:T(8,128)(2,1)} %bitcast.6, bf16[3072,384]{1,0:T(8,128)(2,1)} %get-tuple-element.21.refs_0_, bf16[384,3072]{1,0:T(8,128)(2,1)} %get-tuple-element.22.refs_1_, f32[4,384]{1,0:T(4,128)} %refs_4_.7, ...), custom_call_target="tpu_custom_call" | custom-call | tf_op jit(solution)/shard_map/block_a/pallas_call | solution.py:298
  68.1 0.0 copy-start
  68.1 0.0 copy-start.9
  68.1 0.0 copy-start.10
  68.1 5.1 %all-to-all-done.1.part_ref = bf16[32,64,384]{2,1,0:T(8,128)(2,1)S(1)} async-done(((bf16[32,64,384]{2,1,0:T(8,128)(2,1)}), bf16[32,64,384]{2,1,0:T(8,128)(2,1)S(1)}, u32[]{:S(2)}, u32[]{:S(2)}) %all-to-all-start.1) | async-done | bytes 1572896 | tf_op jit(solution)/shard_map/all_to_all | solution.py:379
  73.2 4.9 %all-to-all-start = ((bf16[32,64,384]{2,1,0:T(8,128)(2,1)}), bf16[32,64,384]{2,1,0:T(8,128)(2,1)}, u32[]{:S(2)}, u32[]{:S(2)}) async-start(bf16[32,64,384]{2,1,0:T(8,128)(2,1)} %block_a.2), calls=%async_computation | async-start | bytes 3145728 | tf_op jit(solution)/shard_map/all_to_all | solution.py:379
  78.2 3.5 %qkv_owner.3 = (bf16[24,64,384]{2,1,0:T(8,128)(2,1)S(1)}, bf16[24,64,384]{2,1,0:T(8,128)(2,1)S(1)}, bf16[24,64,384]{2,1,0:T(8,128)(2,1)S(1)}, bf16[3,384,512]{2,1,0:T(8,128)(2,1)S(1)}) custom-call(s32[24]{0:T(128)S(1)} %copy-done.10, bf16[32,64,384]{2,1,0:T(8,128)(2,1)S(1)} %all-to-all-done.1.part_ref, f32[4,384]{1,0:T(4,128)S(1)} %copy-done.9, ...), custom_call_target="tpu_custom_call" | custom-call | tf_op jit(solution)/shard_map/qkv_owner/pallas_call | solution.py:158
  81.7 1.0 copy-done.1
  82.7 1.0 copy-done.2
  83.8 1.0 copy-done.5
  84.8 1.0 copy-done.6
  85.8 16.0 %all-to-all-done.part_ref = bf16[32,64,384]{2,1,0:T(8,128)(2,1)} async-done(((bf16[32,64,384]{2,1,0:T(8,128)(2,1)}), bf16[32,64,384]{2,1,0:T(8,128)(2,1)}, u32[]{:S(2)}, u32[]{:S(2)}) %all-to-all-start) | async-done | bytes 1572896 | tf_op jit(solution)/shard_map/all_to_all | solution.py:379
  101.8 4.9 %qkv_owner.2 = (bf16[24,64,384]{2,1,0:T(8,128)(2,1)S(1)}, bf16[24,64,384]{2,1,0:T(8,128)(2,1)S(1)}, bf16[24,64,384]{2,1,0:T(8,128)(2,1)S(1)}, bf16[3,384,512]{2,1,0:T(8,128)(2,1)S(1)}) custom-call(s32[24]{0:T(128)S(1)} %copy-done.10, bf16[32,64,384]{2,1,0:T(8,128)(2,1)} %all-to-all-done.part_ref, f32[4,384]{1,0:T(4,128)S(1)} %copy-done.9, ...), custom_call_target="tpu_custom_call" | custom-call | tf_op jit(solution)/shard_map/qkv_owner/pallas_call | solution.py:158
  106.8 1.0 copy-done.3
  107.8 1.0 copy-done.4
  108.8 1.1 copy-done.7
  109.9 1.1 copy-done.8
  111.0 26.6 %block_b.2 = bf16[32,64,384]{2,1,0:T(8,128)(2,1)} custom-call(s32[24]{0:T(128)} %table_ref.8, bf16[24,64,384]{2,1,0:T(8,128)(2,1)} %copy-done.7, bf16[24,64,384]{2,1,0:T(8,128)(2,1)} %copy-done.8, bf16[24,64,384]{2,1,0:T(8,128)(2,1)} %copy-done.3, bf16[24,64,384]{2,1,0:T(8,128)(2,1)} %copy-done.1, bf16[3,384,512]{2,1,0:T(8,128)(2,1)} %copy-done.4, ...), custom_call_target="tpu_custom_call" | custom-call | tf_op jit(solution)/shard_map/block_b/pallas_call | solution.py:298
  137.6 4.2 %all-to-all-start.2 = ((bf16[32,64,384]{2,1,0:T(8,128)(2,1)}), bf16[32,64,384]{2,1,0:T(8,128)(2,1)S(1)}, u32[]{:S(2)}, u32[]{:S(2)}) async-start(bf16[32,64,384]{2,1,0:T(8,128)(2,1)} %block_b.2), calls=%async_computation.2 | async-start | bytes 3145728 | tf_op jit(solution)/shard_map/all_to_all | solution.py:379
  141.9 26.7 %block_b.3 = bf16[32,64,384]{2,1,0:T(8,128)(2,1)} custom-call(s32[24]{0:T(128)} %table_ref.8, bf16[24,64,384]{2,1,0:T(8,128)(2,1)} %copy-done.5, bf16[24,64,384]{2,1,0:T(8,128)(2,1)} %copy-done.6, bf16[24,64,384]{2,1,0:T(8,128)(2,1)} %copy-done.3, bf16[24,64,384]{2,1,0:T(8,128)(2,1)} %copy-done.1, bf16[3,384,512]{2,1,0:T(8,128)(2,1)} %copy-done.4, ...), custom_call_target="tpu_custom_call" | custom-call | tf_op jit(solution)/shard_map/block_b/pallas_call | solution.py:298
  168.6 0.0 copy-start.11
  168.6 30.0 %all_to_all.20.refs_1_ = bf16[32,64,384]{2,1,0:T(8,128)(2,1)S(1)} all-to-all(bf16[32,64,384]{2,1,0:T(8,128)(2,1)} %block_b.3), channel_id=1, replica_groups=mesh['chain'=32,'group'=4] {'chain'}, dimensions={0} | all-to-all | bytes 3145728 | tf_op jit(solution)/shard_map/all_to_all | solution.py:379
  198.6 1.8 home.1
  (17 shorter events, 0.0 us)
Async XLA Ops:
  1.2 14.8 %collective-permute-start.1 = (bf16[512,384]{1,0:T(8,128)(2,1)S(1)}, bf16[512,384]{1,0:T(8,128)(2,1)S(1)}, u32[]{:S(2)}, u32[]{:S(2)}) collective-permute-start(bf16[512,384]{1,0:T(8,128)(2,1)S(1)} %get-tuple-element.31), channel_id=1, source_target_pairs={{1,0},{2,1},{3,2},{4,3},{5,4},{6,5},{7,6},{8,7},{9,8},{10,9},{11,1... | collective-permute-start | bytes 1179656 | tf_op jit(solution)/shard_map/ppermute | solution.py:389
  9.5 12.6 %collective-permute-start = (bf16[512,384]{1,0:T(8,128)(2,1)S(1)}, bf16[512,384]{1,0:T(8,128)(2,1)S(1)}, u32[]{:S(2)}, u32[]{:S(2)}) collective-permute-start(bf16[512,384]{1,0:T(8,128)(2,1)S(1)} %get-tuple-element.32), channel_id=1, source_target_pairs={{0,1},{1,2},{2,3},{3,4},{4,5},{5,6},{6,7},{7,8},{8,9},{9,10},{10,1... | collective-permute-start | bytes 1179656 | tf_op jit(solution)/shard_map/ppermute | solution.py:388
  16.0 6.1 %copy-start.12 = (bf16[512,384]{1,0:T(8,128)(2,1)}, bf16[512,384]{1,0:T(8,128)(2,1)S(1)}, u32[]{:S(2)}) copy-start(bf16[512,384]{1,0:T(8,128)(2,1)S(1)} %collective-permute-done.1.b_ref) | copy-start | bytes 1179652
  22.1 0.8 copy-start.13
  45.3 27.9 %all-to-all-start.1 = ((bf16[32,64,384]{2,1,0:T(8,128)(2,1)}), bf16[32,64,384]{2,1,0:T(8,128)(2,1)S(1)}, u32[]{:S(2)}, u32[]{:S(2)}) async-start(bf16[32,64,384]{2,1,0:T(8,128)(2,1)} %block_a.3), calls=%async_computation.1 | async-start | bytes 3145728 | tf_op jit(solution)/shard_map/all_to_all | solution.py:379
  68.1 10.1 %copy-start = (bf16[2,384,1152]{2,1,0:T(8,128)(2,1)S(1)}, bf16[2,384,1152]{2,1,0:T(8,128)(2,1)}, u32[]{:S(2)}) copy-start(bf16[2,384,1152]{2,1,0:T(8,128)(2,1)} %w_ref.7) | copy-start | bytes 5308420
  68.1 10.1 %copy-start.9 = (f32[4,384]{1,0:T(4,128)S(1)}, f32[4,384]{1,0:T(4,128)}, u32[]{:S(2)}) copy-start(f32[4,384]{1,0:T(4,128)} %refs_4_.7) | copy-start | bytes 18436
  68.1 10.1 %copy-start.10 = (s32[24]{0:T(128)S(1)}, s32[24]{0:T(128)}, u32[]{:S(2)}) copy-start(s32[24]{0:T(128)} %table_ref.8) | copy-start | bytes 292
  73.2 28.6 %all-to-all-start = ((bf16[32,64,384]{2,1,0:T(8,128)(2,1)}), bf16[32,64,384]{2,1,0:T(8,128)(2,1)}, u32[]{:S(2)}, u32[]{:S(2)}) async-start(bf16[32,64,384]{2,1,0:T(8,128)(2,1)} %block_a.2), calls=%async_computation | async-start | bytes 3145728 | tf_op jit(solution)/shard_map/all_to_all | solution.py:379
  81.7 1.1 copy-start.1
  82.7 1.0 copy-start.2
  83.8 1.0 copy-start.5
  84.8 1.0 copy-start.6
  106.8 1.0 copy-start.3
  107.8 1.0 copy-start.4
  108.8 1.1 copy-start.7
  109.9 1.1 copy-start.8
  137.6 31.0 %all-to-all-start.2 = ((bf16[32,64,384]{2,1,0:T(8,128)(2,1)}), bf16[32,64,384]{2,1,0:T(8,128)(2,1)S(1)}, u32[]{:S(2)}, u32[]{:S(2)}) async-start(bf16[32,64,384]{2,1,0:T(8,128)(2,1)} %block_b.2), calls=%async_computation.2 | async-start | bytes 3145728 | tf_op jit(solution)/shard_map/all_to_all | solution.py:379
  168.6 30.0 %copy-start.11 = (s32[16]{0:T(128)S(1)}, s32[16]{0:T(128)}, u32[]{:S(2)}) copy-start(s32[16]{0:T(128)} %table_ref.9) | copy-start | bytes 196

commit v3 on v2

--- a/solution.py
+++ b/solution.py
@@ -49,14 +49,6 @@
     return lax.dot_general(a, b, (((1,), (1,)), ((), ())), preferred_element_type=f32)
 
 
-def dot_lead(a, b):
-    return lax.dot_general(a, b, (((0,), (0,)), ((), ())), preferred_element_type=f32)
-
-
-def dot_cross(a, b):
-    return lax.dot_general(a, b, (((0,), (1,)), ((), ())), preferred_element_type=f32)
-
-
 def whole(shape):
     zeros = (0,) * len(shape)
     return pl.BlockSpec(shape, lambda *_: zeros)
@@ -67,107 +59,111 @@
     return pl.BlockSpec((None, *shape), lambda *_: (layer, *zeros))
 
 
+def qkv_rows(norms, w_ref, store):
+    normed = norms[0]()
+    for i in range(len(norms)):
+        later = norms[i + 1]() if i + 1 < len(norms) else None
+        store(i, dot(normed, w_ref[...]))
+        normed = later
+
+
 def qkv_own_kernel(x_ref, gains_ref, w_ref, q_ref, k_ref, v_ref):
-    normed = norm_rows(x_ref[...].astype(f32), gains_ref[0:1, :])
-    out = dot(normed, w_ref[:, : 2 * D])
-    q_ref[...] = (out[:, :D] * query_scale).astype(bf16)
-    k_ref[...] = out[:, D:].astype(bf16)
-    v_ref[...] = dot_cross(w_ref[:, 2 * D :], normed).astype(bf16)
+    spans = [slice(i * HALF, (i + 1) * HALF) for i in range(x_ref.shape[0] // HALF)]
+    norms = [lambda s=s: norm_rows(x_ref[s, :].astype(f32), gains_ref[0:1, :]) for s in spans]
+
+    def store(i, out):
+        q_ref[spans[i], :] = (out[:, :D] * query_scale).astype(bf16)
+        k_ref[spans[i], :] = out[:, D : 2 * D].astype(bf16)
+        v_ref[spans[i], :] = out[:, 2 * D :].astype(bf16)
+
+    qkv_rows(norms, w_ref, store)
 
 
 def qkv_own(points, gains, qkv_weight):
     rows = points.shape[0]
+    block = pl.BlockSpec((PATCH, D), lambda i: (i, 0))
     return pl.pallas_call(
         qkv_own_kernel,
-        grid=(rows // HALF,),
+        grid=(rows // PATCH,),
+        in_specs=[block, whole((4, D)), layer_of((D, 3 * D), 0)],
+        out_specs=[block] * 3,
+        out_shape=[pltpu.HBM((n, D), bf16) for n in (rows, rows + PATCH, rows + PATCH)],
+        name="qkv_own",
+    )(points, gains, qkv_weight)
+
+
+def qkv_halo_kernel(a_ref, b_ref, gains_ref, w_ref, k_in, v_in, k_ref, v_ref):
+    norms = [
+        lambda r=r: norm_rows(r[...].astype(f32), gains_ref[0:1, :]) for r in (a_ref, b_ref)
+    ]
+
+    def store(i, out):
+        span = slice(i * HALF, (i + 1) * HALF)
+        k_ref[span, :] = out[:, :D].astype(bf16)
+        v_ref[span, :] = out[:, D:].astype(bf16)
+
+    qkv_rows(norms, w_ref.at[:, D:], store)
+
+
+def qkv_halo(before, after, gains, qkv_weight, keys, values):
+    last = keys.shape[0] // PATCH - 1
+    ext = pltpu.HBM(keys.shape, bf16)
+    return pl.pallas_call(
+        qkv_halo_kernel,
+        grid=(1,),
         in_specs=[
-            pl.BlockSpec((HALF, D), lambda i: (i, 0)),
+            pl.BlockSpec(memory_space=pltpu.VMEM),
+            pl.BlockSpec(memory_space=pltpu.VMEM),
             whole((4, D)),
             layer_of((D, 3 * D), 0),
+            pl.BlockSpec(memory_space=pltpu.HBM),
+            pl.BlockSpec(memory_space=pltpu.HBM),
         ],
-        out_specs=[
-            pl.BlockSpec((HALF, D), lambda i: (i, 0)),
-            pl.BlockSpec((HALF, D), lambda i: (i + 1, 0)),
-            pl.BlockSpec((D, HALF), lambda i: (0, i + 1)),
-        ],
-        out_shape=[
-            jax.ShapeDtypeStruct((rows, D), bf16),
-            jax.ShapeDtypeStruct((rows + PATCH, D), bf16),
-            jax.ShapeDtypeStruct((D, rows + PATCH), bf16),
-        ],
-        name="qkv_own",
-    )(points, gains, qkv_weight)
-
-
-def qkv_halo_kernel(a_ref, b_ref, gains_ref, w_ref, k_in, v_in, k_ref, v_ref):
-    first = pl.program_id(0) == 0
-    rows = jnp.where(first, a_ref[...].astype(f32), b_ref[...].astype(f32))
-    normed = norm_rows(rows, gains_ref[0:1, :])
-    k_ref[...] = dot(normed, w_ref[:, D : 2 * D]).astype(bf16)
-    v_ref[...] = dot_cross(w_ref[:, 2 * D :], normed).astype(bf16)
-
-
-def qkv_halo(before, after, gains, qkv_weight, keys, values):
-    last = keys.shape[0] // HALF - 1
-    return pl.pallas_call(
-        qkv_halo_kernel,
-        grid=(2,),
-        in_specs=[
-            whole((HALF, D)),
-            whole((HALF, D)),
-            whole((4, D)),
-            layer_of((D, 3 * D), 0),
-            pl.BlockSpec(memory_space=pl.ANY),
-            pl.BlockSpec(memory_space=pl.ANY),
-        ],
-        out_specs=[
-            pl.BlockSpec((HALF, D), lambda i: (i * last, 0)),
-            pl.BlockSpec((D, HALF), lambda i: (0, i * last)),
-        ],
-        out_shape=[
-            jax.ShapeDtypeStruct(keys.shape, bf16),
-            jax.ShapeDtypeStruct(values.shape, bf16),
-        ],
+        out_specs=[pl.BlockSpec((PATCH, D), lambda i: (last, 0))] * 2,
+        out_shape=[ext, ext],
         input_output_aliases={4: 0, 5: 1},
+        compiler_params=pltpu.CompilerParams(vmem_limit_bytes=24 << 20),
         name="qkv_halo",
     )(before, after, gains, qkv_weight, keys, values)
 
 
-def qkv_owner_kernel(from_ref, part_ref, gains_ref, w_ref, x_ref, q_ref, k_ref, v_ref):
-    step = pl.program_id(0)
-    tiles = []
-    for t in range(PATCH_TILES):
-        source = from_ref[step * PATCH_TILES + t]
-        tile = part_ref[jnp.maximum(source, 0)]
-        tiles.append(jnp.where(source >= 0, tile.astype(f32), 0.0))
-    rows = jnp.concatenate(tiles, axis=0)
+def qkv_owner_kernel(from_ref, part_ref, gains_ref, w_ref, x_ref, q_ref, k_ref, v_ref, normed_ref):
+    patches = SLOTS // PATCH_TILES
     shape = (PATCH_TILES, PART, D)
-    x_ref[...] = rows.astype(bf16).reshape(shape)
-    normed = norm_rows(rows, gains_ref[2:3, :])
-    out = dot(normed, w_ref[:, : 2 * D])
-    q_ref[...] = (out[:, :D] * query_scale).astype(bf16).reshape(shape)
-    k_ref[...] = out[:, D:].astype(bf16).reshape(shape)
-    v_ref[...] = dot_cross(w_ref[:, 2 * D :], normed).astype(bf16)
+
+    def prepare(p):
+        tiles = []
+        for t in range(PATCH_TILES):
+            source = from_ref[p * PATCH_TILES + t]
+            tile = part_ref[jnp.maximum(source, 0)]
+            tiles.append(jnp.where(source >= 0, tile.astype(f32), 0.0))
+        rows = jnp.concatenate(tiles, axis=0)
+        x_ref[pl.ds(p * PATCH_TILES, PATCH_TILES)] = rows.astype(bf16).reshape(shape)
+        return norm_rows(rows, gains_ref[2:3, :])
+
+    normed_ref[0] = prepare(0)
+
+    @pl.loop(0, patches)
+    def _(p):
+        normed_ref[(p + 1) % 2] = prepare(jnp.minimum(p + 1, patches - 1))
+        out = dot(normed_ref[p % 2], w_ref[1])
+        tiles = pl.ds(p * PATCH_TILES, PATCH_TILES)
+        q_ref[tiles] = (out[:, :D] * query_scale).astype(bf16).reshape(shape)
+        k_ref[tiles] = out[:, D : 2 * D].astype(bf16).reshape(shape)
+        v_ref[tiles] = out[:, 2 * D :].astype(bf16).reshape(shape)
 
 
 def qkv_owner(owner_from, part, gains, qkv_weight):
-    patches = SLOTS // PATCH_TILES
-    count = PATCH_TILES * PART
-    block = pl.BlockSpec((PATCH_TILES, PART, D), lambda i, *_: (i, 0, 0))
-    shape = jax.ShapeDtypeStruct((SLOTS, PART, D), bf16)
     return pl.pallas_call(
         qkv_owner_kernel,
         grid_spec=pltpu.PrefetchScalarGridSpec(
             num_scalar_prefetch=1,
-            grid=(patches,),
-            in_specs=[
-                pl.BlockSpec(memory_space=pltpu.VMEM),
-                whole((4, D)),
-                layer_of((D, 3 * D), 1),
-            ],
-            out_specs=[block] * 3 + [pl.BlockSpec((None, D, count), lambda i, *_: (i, 0, 0))],
+            grid=(1,),
+            in_specs=[pl.BlockSpec(memory_space=pltpu.VMEM)] * 3,
+            out_specs=[whole((SLOTS, PART, D))] * 4,
+            scratch_shapes=[pltpu.VMEM((2, PATCH_TILES * PART, D), bf16)],
         ),
-        out_shape=[shape] * 3 + [jax.ShapeDtypeStruct((patches, D, count), bf16)],
+        out_shape=[pltpu.HBM((SLOTS, PART, D), bf16)] * 4,
         compiler_params=pltpu.CompilerParams(vmem_limit_bytes=24 << 20),
         name="qkv_owner",
     )(owner_from, part, gains, qkv_weight)
@@ -176,7 +172,8 @@
 def block_kernel(units, masked, layer, pieces, table_ref, x_ref, q_ref, *refs):
     k_refs, refs = refs[:pieces], refs[pieces:]
     v_refs, refs = refs[:pieces], refs[pieces:]
-    gains_ref, *sources, out_ref, mixed_ref, proj_ref, up_ref, down_ref, sems = refs
+    gains_ref, *sources, out_ref = refs[:5]
+    mixed_ref, normed_ref, rising_ref, total_ref, proj_ref, up_ref, down_ref, sems = refs[5:]
     step = pl.program_id(0)
     count = UNIT_TILES * PART
     rows = PATCH // pieces
@@ -190,7 +187,7 @@
 
     def attention_parts():
         queries = q_ref[...].reshape(count, D)
-        ones = jnp.ones((16, rows), bf16)
+        ones = jnp.ones((rows, 128), bf16)
         extra_q = extra_k = None
         if masked:
             base = (step * UNIT_TILES) // PATCH_TILES * PATCH_TILES
@@ -211,28 +208,32 @@
                 k = k_ref[...].reshape(rows, D)[:, cols]
                 if masked:
                     k = jnp.concatenate([k, extra_k], axis=1)
-                out.append(dot_t(k, q))
+                out.append(dot_t(q, k))
             return out
 
         def soften(parts):
             peak = functools.reduce(
-                jnp.maximum, [jnp.max(s, axis=0, keepdims=True) for s in parts]
+                jnp.maximum, [jnp.max(s, axis=-1, keepdims=True) for s in parts]
             )
             return [jnp.exp2(s - peak).astype(bf16) for s in parts]
 
         def mix(h, parts):
-            cols = slice(HEAD_DIM * h, HEAD_DIM * (h + 1))
+            cols = slice(128 * (h // 2), 128 * (h // 2) + 128)
             total = None
             for p, v_ref in zip(parts, v_refs):
-                one = dot(jnp.concatenate([v_ref[cols, :], ones], axis=0), p)
+                v = v_ref[...].reshape(rows, D)[:, cols]
+                one = dot(p, jnp.concatenate([v, ones], axis=1))
                 total = one if total is None else total + one
-            mixed_ref[cols, :] = (total[:HEAD_DIM] / total[HEAD_DIM : HEAD_DIM + 1]).astype(bf16)
+            own = (total[:, :128] / total[:, 128:]).astype(bf16) * picks[h % 2]
+            if h % 2:
+                own = own + mixed_ref[:, cols]
+            mixed_ref[:, cols] = own
 
         return scores, soften, mix
 
     def join(mixed):
         base = x_ref[...].reshape(count, D).astype(f32)
-        inner = (base + dot_lead(mixed, proj_ref[...])).astype(bf16)
+        inner = (base + dot(mixed, proj_ref[...])).astype(bf16)
         gain = gains_ref[2 * layer + 1 : 2 * layer + 2, :]
         return inner, norm_rows(inner.astype(f32), gain)
 
@@ -283,31 +284,38 @@
     @pl.when(step == units)
     def _():
         inner, normed = join(mixed_ref[...])
-        total = None
-        for h in range(HEADS):
-            one = down(hidden(normed, h), h)
-            total = one if total is None else total + one
-        emit(inner, total)
+        normed_ref[...] = normed
+        rising_ref[0] = dot(normed, up_ref[:, :HID])
+        total_ref[...] = jnp.zeros_like(total_ref)
+
+        @pl.loop(0, FF // HID)
+        def _(j):
+            after = pl.multiple_of(jnp.minimum(j + 1, FF // HID - 1) * HID, HID)
+            rising_ref[(j + 1) % 2] = dot(normed_ref[...], up_ref[:, pl.ds(after, HID)])
+            part = gelu(rising_ref[j % 2]).astype(bf16)
+            total_ref[...] += dot(part, down_ref[pl.ds(pl.multiple_of(j * HID, HID), HID), :])
+
+        emit(inner, total_ref[...])
 
 
 def block(name, table, x, q, keys, values, specs, units, masked, layer, weights):
     gains, *matrices = weights
     pieces = len(keys)
     count = UNIT_TILES * PART
-    x_spec, q_spec, key_spec, value_spec = specs
     return pl.pallas_call(
         functools.partial(block_kernel, units, masked, layer, pieces),
         grid_spec=pltpu.PrefetchScalarGridSpec(
             num_scalar_prefetch=1,
             grid=(units + 1,),
-            in_specs=[x_spec, q_spec]
-            + [key_spec] * pieces
-            + [value_spec] * pieces
+            in_specs=specs
             + [whole((4, D))]
             + [pl.BlockSpec(memory_space=pl.ANY)] * len(matrices),
             out_specs=whole((PEERS, PART, D)),
             scratch_shapes=[
-                pltpu.VMEM((D, count), bf16),
+                pltpu.VMEM((count, D), bf16),
+                pltpu.VMEM((count, D), bf16),
+                pltpu.VMEM((2, count, HID), f32),
+                pltpu.VMEM((count, D), f32),
                 pltpu.VMEM((D, D), bf16),
                 pltpu.VMEM((D, FF), bf16),
                 pltpu.VMEM((FF, D), bf16),
@@ -330,26 +338,37 @@
 def block_a(chunk, table, x, q, keys, values, weights):
     units = TILES_DEV // UNIT_TILES
     shape = (UNIT_TILES, PART, D)
+    own = TILES_DEV * TILE // HALF
+
+    def first(i, *_):
+        patch = (now(i, units) + 1) // 2
+        return patch + patch // 2, 0
+
+    def second(i, *_):
+        patch = (now(i, units) + 1) // 2
+        return jnp.where(patch == 1, 2, own + patch // 2), 0
+
+    key_specs = [pl.BlockSpec((HALF, D), first), pl.BlockSpec((HALF, D), second)]
     specs = [
         pl.BlockSpec(shape, lambda i, *_: (prior(i), chunk, 0)),
         pl.BlockSpec(shape, lambda i, *_: (now(i, units), chunk, 0)),
-        pl.BlockSpec((PATCH, D), lambda i, *_: ((now(i, units) + 1) // 2, 0)),
-        pl.BlockSpec((D, PATCH), lambda i, *_: (0, (now(i, units) + 1) // 2)),
+        *key_specs,
+        *key_specs,
     ]
-    return block("block_a", table, x, q, [keys], [values], specs, units, False, 0, weights)
+    return block(
+        "block_a", table, x, q, [keys] * 2, [values] * 2, specs, units, False, 0, weights
+    )
 
 
 def block_b(table, x, q, keys, values, weights):
     units = SLOTS // UNIT_TILES
     shape = (UNIT_TILES, PART, D)
     patch = (PATCH_TILES, PART, D)
-    flat = (None, D, PATCH_TILES * PART)
+    key_spec = pl.BlockSpec(patch, lambda i, *_: (now(i, units) // 2, 0, 0))
     specs = [
         pl.BlockSpec(shape, lambda i, *_: (prior(i), 0, 0)),
         pl.BlockSpec(shape, lambda i, *_: (now(i, units), 0, 0)),
-        pl.BlockSpec(patch, lambda i, *_: (now(i, units) // 2, 0, 0)),
-        pl.BlockSpec(flat, lambda i, *_: (now(i, units) // 2, 0, 0)),
-    ]
+    ] + [key_spec] * (2 * CHUNKS)
     return block("block_b", table, x, q, keys, values, specs, units, True, 1, weights)
 
 

time: 202 us -> 203 us (level)
  Pallas kernels: 111 us -> 121 us
  local copies, waits for them, and re-layouts: 10.4 us -> 1.22 us
    unnamed x28 -> x10, local copies, waits for them, and re-layouts: 9.16 us -> 0.03 us
    pallas_call x4, Pallas kernels: 90.4 us -> 98.2 us  [block(): pl.pallas_call(functools.partial(block_kernel, units, masked, layer, piec...]
    pallas_call x2, Pallas kernels: 8.41 us -> 12.7 us  [qkv_owner(): pl.pallas_call(qkv_owner_kernel, grid_spec=pltpu.PrefetchScalarGridSpec(n...]
  transfers between devices with their start and end apart: 5 -> 5, of which waited for: 3 -> 3; matrix products, arithmetic and copies ran while one was open for 0% -> 0% of each run, Pallas kernels for 28% -> 30%
where the time goes in v3:
time: 203 us; the launch traced here: 201 us
  Pallas kernels  121 us (60%)
  blocking collectives  30 us (15%)
  waiting for transfers between devices  27 us (13%)
  starting transfers between devices  21.8 us (11%)
    pallas_call x4, Pallas kernels, block(): pl.pallas_call(functools.partial(block_kernel, units, masked, layer, piec...  98.2 us
    all_to_all x1, blocking collectives, exchange(): lax.all_to_all(part, 'chain', split_axis=0, concat_axis=0, tiled=True)  30 us
    all_to_all x3, waiting for transfers between devices, exchange(): lax.all_to_all(part, 'chain', split_axis=0, concat_axis=0, tiled=True)  20.5 us
    all_to_all x3, starting transfers between devices, exchange(): lax.all_to_all(part, 'chain', split_axis=0, concat_axis=0, tiled=True)  13.5 us
    pallas_call x2, Pallas kernels, qkv_owner(): pl.pallas_call(qkv_owner_kernel, grid_spec=pltpu.PrefetchScalarGridSpec(n...  12.7 us
    ppermute x1, starting transfers between devices, body(): lax.ppermute(points[:HALF], axes, [((i + 1) % ring, i) for i in range(rin...  8.31 us
    ppermute x1, waiting for transfers between devices, body(): lax.ppermute(points[rows - HALF:], axes, [(i, (i + 1) % ring) for i in ra...  6.53 us
    pallas_call x1, Pallas kernels, qkv_own(): pl.pallas_call(qkv_own_kernel, grid=(rows // PATCH,), in_specs=[block, wh...  6.09 us
  transfers between devices with their start and end apart: 5, of which 3 were waited for; matrix products, arithmetic and copies ran while one was open for 0% of the time, Pallas kernels for 30%

profile of v3, /device:TPU:0, one launch (start us, length us, event | category | flops | bytes accessed | tf_op | source)
XLA Modules:
  0.0 201.4 jit_solution(16106070759152783372)
XLA Ops:
  0.0 1.2 fusion
  1.2 8.3 %collective-permute-start.1 = (bf16[512,384]{1,0:T(8,128)(2,1)S(1)}, bf16[512,384]{1,0:T(8,128)(2,1)S(1)}, u32[]{:S(2)}, u32[]{:S(2)}) collective-permute-start(bf16[512,384]{1,0:T(8,128)(2,1)S(1)} %get-tuple-element.31), channel_id=1, source_target_pairs={{1,0},{2,1},{3,2},{4,3},{5,4},{6,5},{7,6},{8,7},{9,8},{10,9},{11,1... | collective-permute-start | bytes 1179656 | tf_op jit(solution)/shard_map/ppermute | solution.py:408
  9.5 0.0 copy-start
  9.5 0.0 copy-start.1
  9.5 0.0 collective-permute-start
  9.5 6.1 %qkv_own.1 = (bf16[2048,384]{1,0:T(8,128)(2,1)}, bf16[3072,384]{1,0:T(8,128)(2,1)}, bf16[3072,384]{1,0:T(8,128)(2,1)}) custom-call(bf16[2048,384]{1,0:T(8,128)(2,1)} %x_ref.1, f32[4,384]{1,0:T(4,128)} %refs_4_.7, bf16[2,384,1152]{2,1,0:T(8,128)(2,1)} %w_ref.7), custom_call_target="tpu_custom_call" | custom-call | tf_op jit(solution)/shard_map/qkv_own/pallas_call | solution.py:85
  15.6 0.0 collective-permute-done.1.b_ref
  15.6 6.5 %collective-permute-done.a_ref = bf16[512,384]{1,0:T(8,128)(2,1)S(1)} collective-permute-done((bf16[512,384]{1,0:T(8,128)(2,1)S(1)}, bf16[512,384]{1,0:T(8,128)(2,1)S(1)}, u32[]{:S(2)}, u32[]{:S(2)}) %collective-permute-start) | collective-permute-done | bytes 393248 | tf_op jit(solution)/shard_map/ppermute | solution.py:407
  22.1 0.0 copy-done
  22.1 0.0 copy-done.1
  22.1 2.4 %qkv_halo.1 = (bf16[3072,384]{1,0:T(8,128)(2,1)}, bf16[3072,384]{1,0:T(8,128)(2,1)}) custom-call(bf16[512,384]{1,0:T(8,128)(2,1)S(1)} %collective-permute-done.a_ref, bf16[512,384]{1,0:T(8,128)(2,1)S(1)} %collective-permute-done.1.b_ref, f32[4,384]{1,0:T(4,128)S(1)} %copy-done.1, ...), custom_call_target="tpu_custom_call", output_to_operand_aliasing={{0}: (4, {}), {1}: (5, {})} | custom-call | tf_op jit(solution)/shard_map/qkv_halo/pallas_call | solution.py:111
  24.6 21.1 %block_a.3 = bf16[32,64,384]{2,1,0:T(8,128)(2,1)} custom-call(s32[16]{0:T(128)} %table_ref.9, bf16[16,128,384]{2,1,0:T(8,128)(2,1)} %bitcast.3, bf16[16,128,384]{2,1,0:T(8,128)(2,1)} %bitcast.5, bf16[3072,384]{1,0:T(8,128)(2,1)} %get-tuple-element.21.refs_0_.refs_1_, bf16[3072,384]{1,0:T(8,128)(2,1)} %get-tuple-element.21.refs_0_.refs_1_, ...), custom_call_target="tpu_custom_call" | custom-call | tf_op jit(solution)/shard_map/block_a/pallas_call | solution.py:305
  45.7 4.2 %all-to-all-start.1 = ((bf16[32,64,384]{2,1,0:T(8,128)(2,1)}), bf16[32,64,384]{2,1,0:T(8,128)(2,1)S(1)}, u32[]{:S(2)}, u32[]{:S(2)}) async-start(bf16[32,64,384]{2,1,0:T(8,128)(2,1)} %block_a.3), calls=%async_computation.1 | async-start | bytes 3145728 | tf_op jit(solution)/shard_map/all_to_all | solution.py:398
  49.9 21.2 %block_a.2 = bf16[32,64,384]{2,1,0:T(8,128)(2,1)} custom-call(s32[16]{0:T(128)} %table_ref.9, bf16[16,128,384]{2,1,0:T(8,128)(2,1)} %bitcast.4, bf16[16,128,384]{2,1,0:T(8,128)(2,1)} %bitcast.6, bf16[3072,384]{1,0:T(8,128)(2,1)} %get-tuple-element.21.refs_0_.refs_1_, bf16[3072,384]{1,0:T(8,128)(2,1)} %get-tuple-element.21.refs_0_.refs_1_, ...), custom_call_target="tpu_custom_call" | custom-call | tf_op jit(solution)/shard_map/block_a/pallas_call | solution.py:305
  71.1 0.0 copy-start.2
  71.1 0.0 copy-start.3
  71.1 2.5 %all-to-all-done.1.part_ref = bf16[32,64,384]{2,1,0:T(8,128)(2,1)S(1)} async-done(((bf16[32,64,384]{2,1,0:T(8,128)(2,1)}), bf16[32,64,384]{2,1,0:T(8,128)(2,1)S(1)}, u32[]{:S(2)}, u32[]{:S(2)}) %all-to-all-start.1) | async-done | bytes 1572896 | tf_op jit(solution)/shard_map/all_to_all | solution.py:398
  73.6 5.1 %all-to-all-start = ((bf16[32,64,384]{2,1,0:T(8,128)(2,1)}), bf16[32,64,384]{2,1,0:T(8,128)(2,1)}, u32[]{:S(2)}, u32[]{:S(2)}) async-start(bf16[32,64,384]{2,1,0:T(8,128)(2,1)} %block_a.2), calls=%async_computation | async-start | bytes 3145728 | tf_op jit(solution)/shard_map/all_to_all | solution.py:398
  78.7 0.0 copy-done.2
  78.7 0.0 copy-done.3
  78.7 5.7 %qkv_owner.3 = (bf16[24,64,384]{2,1,0:T(8,128)(2,1)}, bf16[24,64,384]{2,1,0:T(8,128)(2,1)}, bf16[24,64,384]{2,1,0:T(8,128)(2,1)}, bf16[24,64,384]{2,1,0:T(8,128)(2,1)}) custom-call(s32[24]{0:T(128)S(1)} %copy-done.3, bf16[32,64,384]{2,1,0:T(8,128)(2,1)S(1)} %all-to-all-done.1.part_ref, f32[4,384]{1,0:T(4,128)S(1)} %copy-done.2, bf16[2,384,1152]{2,1,0:T(8,128)(2,1)S(1)} %copy-done), custom_call_target="tpu_custom_call" | custom-call | tf_op jit(solution)/shard_map/qkv_owner/pallas_call | solution.py:157
  84.4 18.0 %all-to-all-done.part_ref = bf16[32,64,384]{2,1,0:T(8,128)(2,1)} async-done(((bf16[32,64,384]{2,1,0:T(8,128)(2,1)}), bf16[32,64,384]{2,1,0:T(8,128)(2,1)}, u32[]{:S(2)}, u32[]{:S(2)}) %all-to-all-start) | async-done | bytes 1572896 | tf_op jit(solution)/shard_map/all_to_all | solution.py:398
  102.4 7.1 %qkv_owner.2 = (bf16[24,64,384]{2,1,0:T(8,128)(2,1)}, bf16[24,64,384]{2,1,0:T(8,128)(2,1)}, bf16[24,64,384]{2,1,0:T(8,128)(2,1)}, bf16[24,64,384]{2,1,0:T(8,128)(2,1)}) custom-call(s32[24]{0:T(128)S(1)} %copy-done.3, bf16[32,64,384]{2,1,0:T(8,128)(2,1)} %all-to-all-done.part_ref, f32[4,384]{1,0:T(4,128)S(1)} %copy-done.2, bf16[2,384,1152]{2,1,0:T(8,128)(2,1)S(1)} %copy-done), custom_call_target="tpu_custom_call" | custom-call | tf_op jit(solution)/shard_map/qkv_owner/pallas_call | solution.py:157
  109.4 27.9 %block_b.2 = bf16[32,64,384]{2,1,0:T(8,128)(2,1)} custom-call(s32[24]{0:T(128)} %table_ref.8, bf16[24,64,384]{2,1,0:T(8,128)(2,1)} %get-tuple-element.23.x_ref, bf16[24,64,384]{2,1,0:T(8,128)(2,1)} %get-tuple-element.24.q_ref, bf16[24,64,384]{2,1,0:T(8,128)(2,1)} %get-tuple-element.25.refs_0_, bf16[24,64,384]{2,1,0:T(8,128)(2,1)} %get-tuple-element.26.refs_1_, ...), custom_call_target="tpu_custom_call" | custom-call | tf_op jit(solution)/shard_map/block_b/pallas_call | solution.py:305
  137.4 4.2 %all-to-all-start.2 = ((bf16[32,64,384]{2,1,0:T(8,128)(2,1)}), bf16[32,64,384]{2,1,0:T(8,128)(2,1)S(1)}, u32[]{:S(2)}, u32[]{:S(2)}) async-start(bf16[32,64,384]{2,1,0:T(8,128)(2,1)} %block_b.2), calls=%async_computation.2 | async-start | bytes 3145728 | tf_op jit(solution)/shard_map/all_to_all | solution.py:398
  141.6 27.9 %block_b.3 = bf16[32,64,384]{2,1,0:T(8,128)(2,1)} custom-call(s32[24]{0:T(128)} %table_ref.8, bf16[24,64,384]{2,1,0:T(8,128)(2,1)} %get-tuple-element.29.x_ref, bf16[24,64,384]{2,1,0:T(8,128)(2,1)} %get-tuple-element.30.q_ref, bf16[24,64,384]{2,1,0:T(8,128)(2,1)} %get-tuple-element.25.refs_0_, bf16[24,64,384]{2,1,0:T(8,128)(2,1)} %get-tuple-element.26.refs_1_, ...), custom_call_target="tpu_custom_call" | custom-call | tf_op jit(solution)/shard_map/block_b/pallas_call | solution.py:305
  169.6 0.0 copy-start.4
  169.6 0.0 all-to-all-done.2.refs_0_
  169.6 30.0 %all_to_all.20.refs_1_ = bf16[32,64,384]{2,1,0:T(8,128)(2,1)S(1)} all-to-all(bf16[32,64,384]{2,1,0:T(8,128)(2,1)} %block_b.3), channel_id=1, replica_groups=mesh['chain'=32,'group'=4] {'chain'}, dimensions={0} | all-to-all | bytes 3145728 | tf_op jit(solution)/shard_map/all_to_all | solution.py:398
  199.6 0.0 copy-done.4
  199.6 1.8 home.1
Async XLA Ops:
  1.2 14.4 %collective-permute-start.1 = (bf16[512,384]{1,0:T(8,128)(2,1)S(1)}, bf16[512,384]{1,0:T(8,128)(2,1)S(1)}, u32[]{:S(2)}, u32[]{:S(2)}) collective-permute-start(bf16[512,384]{1,0:T(8,128)(2,1)S(1)} %get-tuple-element.31), channel_id=1, source_target_pairs={{1,0},{2,1},{3,2},{4,3},{5,4},{6,5},{7,6},{8,7},{9,8},{10,9},{11,1... | collective-permute-start | bytes 1179656 | tf_op jit(solution)/shard_map/ppermute | solution.py:408
  9.5 12.6 %copy-start = (bf16[2,384,1152]{2,1,0:T(8,128)(2,1)S(1)}, bf16[2,384,1152]{2,1,0:T(8,128)(2,1)}, u32[]{:S(2)}) copy-start(bf16[2,384,1152]{2,1,0:T(8,128)(2,1)} %w_ref.7) | copy-start | bytes 5308420
  9.5 12.6 %copy-start.1 = (f32[4,384]{1,0:T(4,128)S(1)}, f32[4,384]{1,0:T(4,128)}, u32[]{:S(2)}) copy-start(f32[4,384]{1,0:T(4,128)} %refs_4_.7) | copy-start | bytes 18436
  9.5 12.6 %collective-permute-start = (bf16[512,384]{1,0:T(8,128)(2,1)S(1)}, bf16[512,384]{1,0:T(8,128)(2,1)S(1)}, u32[]{:S(2)}, u32[]{:S(2)}) collective-permute-start(bf16[512,384]{1,0:T(8,128)(2,1)S(1)} %get-tuple-element.32), channel_id=1, source_target_pairs={{0,1},{1,2},{2,3},{3,4},{4,5},{5,6},{6,7},{7,8},{8,9},{9,10},{10,1... | collective-permute-start | bytes 1179656 | tf_op jit(solution)/shard_map/ppermute | solution.py:407
  45.7 27.9 %all-to-all-start.1 = ((bf16[32,64,384]{2,1,0:T(8,128)(2,1)}), bf16[32,64,384]{2,1,0:T(8,128)(2,1)S(1)}, u32[]{:S(2)}, u32[]{:S(2)}) async-start(bf16[32,64,384]{2,1,0:T(8,128)(2,1)} %block_a.3), calls=%async_computation.1 | async-start | bytes 3145728 | tf_op jit(solution)/shard_map/all_to_all | solution.py:398
  71.1 7.6 %copy-start.2 = (f32[4,384]{1,0:T(4,128)S(1)}, f32[4,384]{1,0:T(4,128)}, u32[]{:S(2)}) copy-start(f32[4,384]{1,0:T(4,128)} %refs_4_.7) | copy-start | bytes 18436
  71.1 7.6 %copy-start.3 = (s32[24]{0:T(128)S(1)}, s32[24]{0:T(128)}, u32[]{:S(2)}) copy-start(s32[24]{0:T(128)} %table_ref.8) | copy-start | bytes 292
  73.6 28.8 %all-to-all-start = ((bf16[32,64,384]{2,1,0:T(8,128)(2,1)}), bf16[32,64,384]{2,1,0:T(8,128)(2,1)}, u32[]{:S(2)}, u32[]{:S(2)}) async-start(bf16[32,64,384]{2,1,0:T(8,128)(2,1)} %block_a.2), calls=%async_computation | async-start | bytes 3145728 | tf_op jit(solution)/shard_map/all_to_all | solution.py:398
  137.4 32.2 %all-to-all-start.2 = ((bf16[32,64,384]{2,1,0:T(8,128)(2,1)}), bf16[32,64,384]{2,1,0:T(8,128)(2,1)S(1)}, u32[]{:S(2)}, u32[]{:S(2)}) async-start(bf16[32,64,384]{2,1,0:T(8,128)(2,1)} %block_b.2), calls=%async_computation.2 | async-start | bytes 3145728 | tf_op jit(solution)/shard_map/all_to_all | solution.py:398
  169.6 30.0 %copy-start.4 = (s32[16]{0:T(128)S(1)}, s32[16]{0:T(128)}, u32[]{:S(2)}) copy-start(s32[16]{0:T(128)} %table_ref.9) | copy-start | bytes 196

commit v4 on v3

--- a/solution.py
+++ b/solution.py
@@ -65,6 +65,14 @@
         later = norms[i + 1]() if i + 1 < len(norms) else None
         store(i, dot(normed, w_ref[...]))
         normed = later
+
+
+def now(i, units):
+    return jnp.minimum(i, units - 1)
+
+
+def prior(i):
+    return jnp.maximum(i - 1, 0)
 
 
 def qkv_own_kernel(x_ref, gains_ref, w_ref, q_ref, k_ref, v_ref):
@@ -127,41 +135,35 @@
     )(before, after, gains, qkv_weight, keys, values)
 
 
-def qkv_owner_kernel(from_ref, part_ref, gains_ref, w_ref, x_ref, q_ref, k_ref, v_ref, normed_ref):
-    patches = SLOTS // PATCH_TILES
+def qkv_owner_kernel(from_ref, part_ref, gains_ref, w_ref, x_ref, q_ref, k_ref, v_ref):
+    patch = pl.program_id(0)
     shape = (PATCH_TILES, PART, D)
-
-    def prepare(p):
-        tiles = []
-        for t in range(PATCH_TILES):
-            source = from_ref[p * PATCH_TILES + t]
-            tile = part_ref[jnp.maximum(source, 0)]
-            tiles.append(jnp.where(source >= 0, tile.astype(f32), 0.0))
-        rows = jnp.concatenate(tiles, axis=0)
-        x_ref[pl.ds(p * PATCH_TILES, PATCH_TILES)] = rows.astype(bf16).reshape(shape)
-        return norm_rows(rows, gains_ref[2:3, :])
-
-    normed_ref[0] = prepare(0)
-
-    @pl.loop(0, patches)
-    def _(p):
-        normed_ref[(p + 1) % 2] = prepare(jnp.minimum(p + 1, patches - 1))
-        out = dot(normed_ref[p % 2], w_ref[1])
-        tiles = pl.ds(p * PATCH_TILES, PATCH_TILES)
-        q_ref[tiles] = (out[:, :D] * query_scale).astype(bf16).reshape(shape)
-        k_ref[tiles] = out[:, D : 2 * D].astype(bf16).reshape(shape)
-        v_ref[tiles] = out[:, 2 * D :].astype(bf16).reshape(shape)
+    tiles = []
+    for t in range(PATCH_TILES):
+        source = from_ref[patch * PATCH_TILES + t]
+        tile = part_ref[jnp.maximum(source, 0)]
+        tiles.append(jnp.where(source >= 0, tile.astype(f32), 0.0))
+    rows = jnp.concatenate(tiles, axis=0)
+    x_ref[...] = rows.astype(bf16).reshape(shape)
+    out = dot(norm_rows(rows, gains_ref[2:3, :]), w_ref[...])
+    q_ref[...] = (out[:, :D] * query_scale).astype(bf16).reshape(shape)
+    k_ref[...] = out[:, D : 2 * D].astype(bf16).reshape(shape)
+    v_ref[...] = out[:, 2 * D :].astype(bf16).reshape(shape)
 
 
 def qkv_owner(owner_from, part, gains, qkv_weight):
+    block = pl.BlockSpec((PATCH_TILES, PART, D), lambda i, *_: (i, 0, 0))
     return pl.pallas_call(
         qkv_owner_kernel,
         grid_spec=pltpu.PrefetchScalarGridSpec(
             num_scalar_prefetch=1,
-            grid=(1,),
-            in_specs=[pl.BlockSpec(memory_space=pltpu.VMEM)] * 3,
-            out_specs=[whole((SLOTS, PART, D))] * 4,
-            scratch_shapes=[pltpu.VMEM((2, PATCH_TILES * PART, D), bf16)],
+            grid=(SLOTS // PATCH_TILES,),
+            in_specs=[
+                pl.BlockSpec(memory_space=pltpu.VMEM),
+                whole((4, D)),
+                layer_of((D, 3 * D), 1),
+            ],
+            out_specs=[block] * 4,
         ),
         out_shape=[pltpu.HBM((SLOTS, PART, D), bf16)] * 4,
         compiler_params=pltpu.CompilerParams(vmem_limit_bytes=24 << 20),
@@ -172,8 +174,7 @@
 def block_kernel(units, masked, layer, pieces, table_ref, x_ref, q_ref, *refs):
     k_refs, refs = refs[:pieces], refs[pieces:]
     v_refs, refs = refs[:pieces], refs[pieces:]
-    gains_ref, *sources, out_ref = refs[:5]
-    mixed_ref, normed_ref, rising_ref, total_ref, proj_ref, up_ref, down_ref, sems = refs[5:]
+    gains_ref, *sources, out_ref, mixed_ref, proj_ref, up_ref, down_ref, sems = refs
     step = pl.program_id(0)
     count = UNIT_TILES * PART
     rows = PATCH // pieces
@@ -231,17 +232,56 @@
 
         return scores, soften, mix
 
-    def join(mixed):
+    def attention_steps():
+        scores, soften, mix = attention_parts()
+        s = scores(0)
+        yield
+        for h in range(HEADS):
+            later = None
+            if h + 1 < HEADS:
+                later = scores(h + 1)
+                yield
+            weights = soften(s)
+            yield
+            mix(h, weights)
+            yield
+            s = later
+
+    def forward_steps(mixed, result):
         base = x_ref[...].reshape(count, D).astype(f32)
+        gain = gains_ref[2 * layer + 1 : 2 * layer + 2, :]
         inner = (base + dot(mixed, proj_ref[...])).astype(bf16)
-        gain = gains_ref[2 * layer + 1 : 2 * layer + 2, :]
-        return inner, norm_rows(inner.astype(f32), gain)
-
-    def hidden(normed, j):
-        return gelu(dot(normed, up_ref[:, HID * j : HID * (j + 1)])).astype(bf16)
-
-    def down(part, j):
-        return dot(part, down_ref[HID * j : HID * (j + 1), :])
+        yield
+        normed = norm_rows(inner.astype(f32), gain)
+        yield
+
+        def rise(j):
+            return dot(normed, up_ref[:, HID * j : HID * (j + 1)])
+
+        total = None
+        up = rise(0)
+        yield
+        for j in range(FF // HID):
+            later = None
+            if j + 1 < FF // HID:
+                later = rise(j + 1)
+                yield
+            one = dot(gelu(up).astype(bf16), down_ref[HID * j : HID * (j + 1), :])
+            total = one if total is None else total + one
+            yield
+            up = later
+        result.extend((inner, total))
+
+    def weave(first, *others, delay=0):
+        done = object()
+        streams = [first]
+        for _ in range(delay):
+            next(first)
+        streams = [first, *others]
+        while streams:
+            for stream in list(streams):
+                if next(stream, done) is done:
+                    streams.remove(stream)
 
     def emit(inner, total):
         outer = (inner.astype(f32) + total).astype(bf16)
@@ -256,46 +296,21 @@
     def _():
         for fetch in fetches:
             fetch.start()
-        scores, soften, mix = attention_parts()
-        s = scores(0)
-        for h in range(HEADS):
-            later = scores(h + 1) if h + 1 < HEADS else None
-            mix(h, soften(s))
-            s = later
+        weave(attention_steps())
         for fetch in fetches:
             fetch.wait()
 
     @pl.when((step > 0) & (step < units))
     def _():
-        mixed = mixed_ref[...]
-        scores, soften, mix = attention_parts()
-        s = scores(0)
-        inner, normed = join(mixed)
-        total = None
-        for h in range(HEADS):
-            later = scores(h + 1) if h + 1 < HEADS else None
-            part = hidden(normed, h)
-            mix(h, soften(s))
-            one = down(part, h)
-            total = one if total is None else total + one
-            s = later
-        emit(inner, total)
+        result = []
+        weave(attention_steps(), forward_steps(mixed_ref[...], result), delay=0)
+        emit(*result)
 
     @pl.when(step == units)
     def _():
-        inner, normed = join(mixed_ref[...])
-        normed_ref[...] = normed
-        rising_ref[0] = dot(normed, up_ref[:, :HID])
-        total_ref[...] = jnp.zeros_like(total_ref)
-
-        @pl.loop(0, FF // HID)
-        def _(j):
-            after = pl.multiple_of(jnp.minimum(j + 1, FF // HID - 1) * HID, HID)
-            rising_ref[(j + 1) % 2] = dot(normed_ref[...], up_ref[:, pl.ds(after, HID)])
-            part = gelu(rising_ref[j % 2]).astype(bf16)
-            total_ref[...] += dot(part, down_ref[pl.ds(pl.multiple_of(j * HID, HID), HID), :])
-
-        emit(inner, total_ref[...])
+        result = []
+        weave(forward_steps(mixed_ref[...], result))
+        emit(*result)
 
 
 def block(name, table, x, q, keys, values, specs, units, masked, layer, weights):
@@ -313,9 +328,6 @@
             out_specs=whole((PEERS, PART, D)),
             scratch_shapes=[
                 pltpu.VMEM((count, D), bf16),
-                pltpu.VMEM((count, D), bf16),
-                pltpu.VMEM((2, count, HID), f32),
-                pltpu.VMEM((count, D), f32),
                 pltpu.VMEM((D, D), bf16),
                 pltpu.VMEM((D, FF), bf16),
                 pltpu.VMEM((FF, D), bf16),
@@ -325,14 +337,6 @@
         out_shape=jax.ShapeDtypeStruct((PEERS, PART, D), bf16),
         name=name,
     )(table, x, q, *keys, *values, gains, *matrices)
-
-
-def now(i, units):
-    return jnp.minimum(i, units - 1)
-
-
-def prior(i):
-    return jnp.maximum(i - 1, 0)
 
 
 def block_a(chunk, table, x, q, keys, values, weights):
@@ -374,7 +378,8 @@
 
 def home_kernel(table_ref, *refs):
     parts, out_ref = refs[:CHUNKS], refs[CHUNKS]
-    for t in range(TILES_DEV):
+    @pl.loop(0, TILES_DEV)
+    def _(t):
         for c, part_ref in enumerate(parts):
             out_ref[t, c * PART : (c + 1) * PART] = part_ref[table_ref[t]]
 

time: 203 us -> 188 us (0.926)
  Pallas kernels: 121 us -> 101 us
  waiting for transfers between devices: 27 us -> 32.7 us
    pallas_call x4, Pallas kernels: 98.2 us -> 80.6 us  [block(): pl.pallas_call(functools.partial(block_kernel, units, masked, layer, piec...]
    all_to_all x3, waiting for transfers between devices: 20.5 us -> 26.2 us  [exchange(): lax.all_to_all(part, 'chain', split_axis=0, concat_axis=0, tiled=True)]
    pallas_call x2, Pallas kernels: 12.7 us -> 10.2 us  [qkv_owner(): pl.pallas_call(qkv_owner_kernel, grid_spec=pltpu.PrefetchScalarGridSpec(n...]
  transfers between devices with their start and end apart: 5 -> 5, of which waited for: 3 -> 4; matrix products, arithmetic and copies ran while one was open for 0% -> 0% of each run, Pallas kernels for 30% -> 27%
where the time goes in v4:
time: 188 us; the launch traced here: 187 us
  Pallas kernels  101 us (54%)
  waiting for transfers between devices  32.7 us (17%)
  blocking collectives  29.7 us (16%)
  starting transfers between devices  21.6 us (11%)
    pallas_call x4, Pallas kernels, block(): pl.pallas_call(functools.partial(block_kernel, units, masked, layer, piec...  80.6 us
    all_to_all x1, blocking collectives, exchange(): lax.all_to_all(part, 'chain', split_axis=0, concat_axis=0, tiled=True)  29.7 us
    all_to_all x3, waiting for transfers between devices, exchange(): lax.all_to_all(part, 'chain', split_axis=0, concat_axis=0, tiled=True)  26.2 us
    all_to_all x3, starting transfers between devices, exchange(): lax.all_to_all(part, 'chain', split_axis=0, concat_axis=0, tiled=True)  13.3 us
    pallas_call x2, Pallas kernels, qkv_owner(): pl.pallas_call(qkv_owner_kernel, grid_spec=pltpu.PrefetchScalarGridSpec(n...  10.2 us
    ppermute x1, starting transfers between devices, body(): lax.ppermute(points[:HALF], axes, [((i + 1) % ring, i) for i in range(rin...  8.31 us
    ppermute x1, waiting for transfers between devices, body(): lax.ppermute(points[rows - HALF:], axes, [(i, (i + 1) % ring) for i in ra...  6.53 us
    pallas_call x1, Pallas kernels, qkv_own(): pl.pallas_call(qkv_own_kernel, grid=(rows // PATCH,), in_specs=[block, wh...  6.09 us
  transfers between devices with their start and end apart: 5, of which 4 were waited for; matrix products, arithmetic and copies ran while one was open for 0% of the time, Pallas kernels for 27%

profile of v4, /device:TPU:0, one launch (start us, length us, event | category | flops | bytes accessed | tf_op | source)
XLA Modules:
  0.0 186.7 jit_solution(14826074220876617080)
XLA Ops:
  0.0 1.2 fusion
  1.2 8.3 %collective-permute-start.1 = (bf16[512,384]{1,0:T(8,128)(2,1)S(1)}, bf16[512,384]{1,0:T(8,128)(2,1)S(1)}, u32[]{:S(2)}, u32[]{:S(2)}) collective-permute-start(bf16[512,384]{1,0:T(8,128)(2,1)S(1)} %get-tuple-element.31), channel_id=1, source_target_pairs={{1,0},{2,1},{3,2},{4,3},{5,4},{6,5},{7,6},{8,7},{9,8},{10,9},{11,1... | collective-permute-start | bytes 1179656 | tf_op jit(solution)/shard_map/ppermute | solution.py:413
  9.5 0.0 copy-start
  9.5 0.0 copy-start.1
  9.5 0.0 collective-permute-start
  9.5 6.1 %qkv_own.1 = (bf16[2048,384]{1,0:T(8,128)(2,1)}, bf16[3072,384]{1,0:T(8,128)(2,1)}, bf16[3072,384]{1,0:T(8,128)(2,1)}) custom-call(bf16[2048,384]{1,0:T(8,128)(2,1)} %x_ref.1, f32[4,384]{1,0:T(4,128)} %refs_4_.7, bf16[2,384,1152]{2,1,0:T(8,128)(2,1)} %w_ref.7), custom_call_target="tpu_custom_call" | custom-call | tf_op jit(solution)/shard_map/qkv_own/pallas_call | solution.py:93
  15.6 0.0 collective-permute-done.1.b_ref
  15.6 6.5 %collective-permute-done.a_ref = bf16[512,384]{1,0:T(8,128)(2,1)S(1)} collective-permute-done((bf16[512,384]{1,0:T(8,128)(2,1)S(1)}, bf16[512,384]{1,0:T(8,128)(2,1)S(1)}, u32[]{:S(2)}, u32[]{:S(2)}) %collective-permute-start) | collective-permute-done | bytes 393248 | tf_op jit(solution)/shard_map/ppermute | solution.py:412
  22.1 0.0 copy-done
  22.1 0.0 copy-done.1
  22.1 2.4 %qkv_halo.1 = (bf16[3072,384]{1,0:T(8,128)(2,1)}, bf16[3072,384]{1,0:T(8,128)(2,1)}) custom-call(bf16[512,384]{1,0:T(8,128)(2,1)S(1)} %collective-permute-done.a_ref, bf16[512,384]{1,0:T(8,128)(2,1)S(1)} %collective-permute-done.1.b_ref, f32[4,384]{1,0:T(4,128)S(1)} %copy-done.1, ...), custom_call_target="tpu_custom_call", output_to_operand_aliasing={{0}: (4, {}), {1}: (5, {})} | custom-call | tf_op jit(solution)/shard_map/qkv_halo/pallas_call | solution.py:119
  24.6 17.0 %block_a.3 = bf16[32,64,384]{2,1,0:T(8,128)(2,1)} custom-call(s32[16]{0:T(128)} %table_ref.9, bf16[16,128,384]{2,1,0:T(8,128)(2,1)} %bitcast.3, bf16[16,128,384]{2,1,0:T(8,128)(2,1)} %bitcast.5, bf16[3072,384]{1,0:T(8,128)(2,1)} %get-tuple-element.21.refs_0_.refs_1_, bf16[3072,384]{1,0:T(8,128)(2,1)} %get-tuple-element.21.refs_0_.refs_1_, ...), custom_call_target="tpu_custom_call" | custom-call | tf_op jit(solution)/shard_map/block_a/pallas_call | solution.py:320
  41.6 4.2 %all-to-all-start.1 = ((bf16[32,64,384]{2,1,0:T(8,128)(2,1)}), bf16[32,64,384]{2,1,0:T(8,128)(2,1)S(1)}, u32[]{:S(2)}, u32[]{:S(2)}) async-start(bf16[32,64,384]{2,1,0:T(8,128)(2,1)} %block_a.3), calls=%async_computation.1 | async-start | bytes 3145728 | tf_op jit(solution)/shard_map/all_to_all | solution.py:403
  45.7 17.0 %block_a.2 = bf16[32,64,384]{2,1,0:T(8,128)(2,1)} custom-call(s32[16]{0:T(128)} %table_ref.9, bf16[16,128,384]{2,1,0:T(8,128)(2,1)} %bitcast.4, bf16[16,128,384]{2,1,0:T(8,128)(2,1)} %bitcast.6, bf16[3072,384]{1,0:T(8,128)(2,1)} %get-tuple-element.21.refs_0_.refs_1_, bf16[3072,384]{1,0:T(8,128)(2,1)} %get-tuple-element.21.refs_0_.refs_1_, ...), custom_call_target="tpu_custom_call" | custom-call | tf_op jit(solution)/shard_map/block_a/pallas_call | solution.py:320
  62.8 0.0 copy-start.2
  62.8 0.0 copy-start.3
  62.8 6.7 %all-to-all-done.1.part_ref = bf16[32,64,384]{2,1,0:T(8,128)(2,1)S(1)} async-done(((bf16[32,64,384]{2,1,0:T(8,128)(2,1)}), bf16[32,64,384]{2,1,0:T(8,128)(2,1)S(1)}, u32[]{:S(2)}, u32[]{:S(2)}) %all-to-all-start.1) | async-done | bytes 1572896 | tf_op jit(solution)/shard_map/all_to_all | solution.py:403
  69.5 4.9 %all-to-all-start = ((bf16[32,64,384]{2,1,0:T(8,128)(2,1)}), bf16[32,64,384]{2,1,0:T(8,128)(2,1)}, u32[]{:S(2)}, u32[]{:S(2)}) async-start(bf16[32,64,384]{2,1,0:T(8,128)(2,1)} %block_a.2), calls=%async_computation | async-start | bytes 3145728 | tf_op jit(solution)/shard_map/all_to_all | solution.py:403
  74.4 0.0 copy-done.2
  74.4 0.0 copy-done.3
  74.4 4.4 %qkv_owner.3 = (bf16[24,64,384]{2,1,0:T(8,128)(2,1)}, bf16[24,64,384]{2,1,0:T(8,128)(2,1)}, bf16[24,64,384]{2,1,0:T(8,128)(2,1)}, bf16[24,64,384]{2,1,0:T(8,128)(2,1)}) custom-call(s32[24]{0:T(128)S(1)} %copy-done.3, bf16[32,64,384]{2,1,0:T(8,128)(2,1)S(1)} %all-to-all-done.1.part_ref, f32[4,384]{1,0:T(4,128)S(1)} %copy-done.2, bf16[2,384,1152]{2,1,0:T(8,128)(2,1)S(1)} %copy-done), custom_call_target="tpu_custom_call" | custom-call | tf_op jit(solution)/shard_map/qkv_owner/pallas_call | solution.py:156
  78.8 19.2 %all-to-all-done.part_ref = bf16[32,64,384]{2,1,0:T(8,128)(2,1)} async-done(((bf16[32,64,384]{2,1,0:T(8,128)(2,1)}), bf16[32,64,384]{2,1,0:T(8,128)(2,1)}, u32[]{:S(2)}, u32[]{:S(2)}) %all-to-all-start) | async-done | bytes 1572896 | tf_op jit(solution)/shard_map/all_to_all | solution.py:403
  98.1 5.8 %qkv_owner.2 = (bf16[24,64,384]{2,1,0:T(8,128)(2,1)}, bf16[24,64,384]{2,1,0:T(8,128)(2,1)}, bf16[24,64,384]{2,1,0:T(8,128)(2,1)}, bf16[24,64,384]{2,1,0:T(8,128)(2,1)}) custom-call(s32[24]{0:T(128)S(1)} %copy-done.3, bf16[32,64,384]{2,1,0:T(8,128)(2,1)} %all-to-all-done.part_ref, f32[4,384]{1,0:T(4,128)S(1)} %copy-done.2, bf16[2,384,1152]{2,1,0:T(8,128)(2,1)S(1)} %copy-done), custom_call_target="tpu_custom_call" | custom-call | tf_op jit(solution)/shard_map/qkv_owner/pallas_call | solution.py:156
  103.9 23.3 %block_b.2 = bf16[32,64,384]{2,1,0:T(8,128)(2,1)} custom-call(s32[24]{0:T(128)} %table_ref.8, bf16[24,64,384]{2,1,0:T(8,128)(2,1)} %get-tuple-element.23.x_ref, bf16[24,64,384]{2,1,0:T(8,128)(2,1)} %get-tuple-element.24.q_ref, bf16[24,64,384]{2,1,0:T(8,128)(2,1)} %get-tuple-element.25.refs_0_, bf16[24,64,384]{2,1,0:T(8,128)(2,1)} %get-tuple-element.26.refs_1_, ...), custom_call_target="tpu_custom_call" | custom-call | tf_op jit(solution)/shard_map/block_b/pallas_call | solution.py:320
  127.1 4.2 %all-to-all-start.2 = ((bf16[32,64,384]{2,1,0:T(8,128)(2,1)}), bf16[32,64,384]{2,1,0:T(8,128)(2,1)S(1)}, u32[]{:S(2)}, u32[]{:S(2)}) async-start(bf16[32,64,384]{2,1,0:T(8,128)(2,1)} %block_b.2), calls=%async_computation.2 | async-start | bytes 3145728 | tf_op jit(solution)/shard_map/all_to_all | solution.py:403
  131.4 23.3 %block_b.3 = bf16[32,64,384]{2,1,0:T(8,128)(2,1)} custom-call(s32[24]{0:T(128)} %table_ref.8, bf16[24,64,384]{2,1,0:T(8,128)(2,1)} %get-tuple-element.29.x_ref, bf16[24,64,384]{2,1,0:T(8,128)(2,1)} %get-tuple-element.30.q_ref, bf16[24,64,384]{2,1,0:T(8,128)(2,1)} %get-tuple-element.25.refs_0_, bf16[24,64,384]{2,1,0:T(8,128)(2,1)} %get-tuple-element.26.refs_1_, ...), custom_call_target="tpu_custom_call" | custom-call | tf_op jit(solution)/shard_map/block_b/pallas_call | solution.py:320
  154.7 0.0 copy-start.4
  154.7 0.3 all-to-all-done.2.refs_0_
  155.1 29.7 %all_to_all.20.refs_1_ = bf16[32,64,384]{2,1,0:T(8,128)(2,1)S(1)} all-to-all(bf16[32,64,384]{2,1,0:T(8,128)(2,1)} %block_b.3), channel_id=1, replica_groups=mesh['chain'=32,'group'=4] {'chain'}, dimensions={0} | all-to-all | bytes 3145728 | tf_op jit(solution)/shard_map/all_to_all | solution.py:403
  184.7 0.0 copy-done.4
  184.7 1.9 %home.1 = bf16[16,128,384]{2,1,0:T(8,128)(2,1)} custom-call(s32[16]{0:T(128)S(1)} %copy-done.4, bf16[32,64,384]{2,1,0:T(8,128)(2,1)S(1)} %all-to-all-done.2.refs_0_, bf16[32,64,384]{2,1,0:T(8,128)(2,1)S(1)} %all_to_all.20.refs_1_), custom_call_target="tpu_custom_call" | custom-call | tf_op jit(solution)/shard_map/home/pallas_call | solution.py:388
Async XLA Ops:
  1.2 14.4 %collective-permute-start.1 = (bf16[512,384]{1,0:T(8,128)(2,1)S(1)}, bf16[512,384]{1,0:T(8,128)(2,1)S(1)}, u32[]{:S(2)}, u32[]{:S(2)}) collective-permute-start(bf16[512,384]{1,0:T(8,128)(2,1)S(1)} %get-tuple-element.31), channel_id=1, source_target_pairs={{1,0},{2,1},{3,2},{4,3},{5,4},{6,5},{7,6},{8,7},{9,8},{10,9},{11,1... | collective-permute-start | bytes 1179656 | tf_op jit(solution)/shard_map/ppermute | solution.py:413
  9.5 12.6 %copy-start = (bf16[2,384,1152]{2,1,0:T(8,128)(2,1)S(1)}, bf16[2,384,1152]{2,1,0:T(8,128)(2,1)}, u32[]{:S(2)}) copy-start(bf16[2,384,1152]{2,1,0:T(8,128)(2,1)} %w_ref.7) | copy-start | bytes 5308420
  9.5 12.6 %copy-start.1 = (f32[4,384]{1,0:T(4,128)S(1)}, f32[4,384]{1,0:T(4,128)}, u32[]{:S(2)}) copy-start(f32[4,384]{1,0:T(4,128)} %refs_4_.7) | copy-start | bytes 18436
  9.5 12.6 %collective-permute-start = (bf16[512,384]{1,0:T(8,128)(2,1)S(1)}, bf16[512,384]{1,0:T(8,128)(2,1)S(1)}, u32[]{:S(2)}, u32[]{:S(2)}) collective-permute-start(bf16[512,384]{1,0:T(8,128)(2,1)S(1)} %get-tuple-element.32), channel_id=1, source_target_pairs={{0,1},{1,2},{2,3},{3,4},{4,5},{5,6},{6,7},{7,8},{8,9},{9,10},{10,1... | collective-permute-start | bytes 1179656 | tf_op jit(solution)/shard_map/ppermute | solution.py:412
  41.6 27.9 %all-to-all-start.1 = ((bf16[32,64,384]{2,1,0:T(8,128)(2,1)}), bf16[32,64,384]{2,1,0:T(8,128)(2,1)S(1)}, u32[]{:S(2)}, u32[]{:S(2)}) async-start(bf16[32,64,384]{2,1,0:T(8,128)(2,1)} %block_a.3), calls=%async_computation.1 | async-start | bytes 3145728 | tf_op jit(solution)/shard_map/all_to_all | solution.py:403
  62.8 11.6 %copy-start.2 = (f32[4,384]{1,0:T(4,128)S(1)}, f32[4,384]{1,0:T(4,128)}, u32[]{:S(2)}) copy-start(f32[4,384]{1,0:T(4,128)} %refs_4_.7) | copy-start | bytes 18436
  62.8 11.6 %copy-start.3 = (s32[24]{0:T(128)S(1)}, s32[24]{0:T(128)}, u32[]{:S(2)}) copy-start(s32[24]{0:T(128)} %table_ref.8) | copy-start | bytes 292
  69.5 28.6 %all-to-all-start = ((bf16[32,64,384]{2,1,0:T(8,128)(2,1)}), bf16[32,64,384]{2,1,0:T(8,128)(2,1)}, u32[]{:S(2)}, u32[]{:S(2)}) async-start(bf16[32,64,384]{2,1,0:T(8,128)(2,1)} %block_a.2), calls=%async_computation | async-start | bytes 3145728 | tf_op jit(solution)/shard_map/all_to_all | solution.py:403
  127.1 27.9 %all-to-all-start.2 = ((bf16[32,64,384]{2,1,0:T(8,128)(2,1)}), bf16[32,64,384]{2,1,0:T(8,128)(2,1)S(1)}, u32[]{:S(2)}, u32[]{:S(2)}) async-start(bf16[32,64,384]{2,1,0:T(8,128)(2,1)} %block_b.2), calls=%async_computation.2 | async-start | bytes 3145728 | tf_op jit(solution)/shard_map/all_to_all | solution.py:403
  154.7 30.0 %copy-start.4 = (s32[16]{0:T(128)S(1)}, s32[16]{0:T(128)}, u32[]{:S(2)}) copy-start(s32[16]{0:T(128)} %table_ref.9) | copy-start | bytes 196

commit v5 on v4

--- a/solution.py
+++ b/solution.py
@@ -100,7 +100,7 @@
     )(points, gains, qkv_weight)
 
 
-def qkv_halo_kernel(a_ref, b_ref, gains_ref, w_ref, k_in, v_in, k_ref, v_ref):
+def qkv_halo_kernel(a_ref, b_ref, gains_ref, w_ref, k_in, v_in, after_in, k_ref, v_ref):
     norms = [
         lambda r=r: norm_rows(r[...].astype(f32), gains_ref[0:1, :]) for r in (a_ref, b_ref)
     ]
@@ -113,7 +113,7 @@
     qkv_rows(norms, w_ref.at[:, D:], store)
 
 
-def qkv_halo(before, after, gains, qkv_weight, keys, values):
+def qkv_halo(before, after, gains, qkv_weight, keys, values, earlier):
     last = keys.shape[0] // PATCH - 1
     ext = pltpu.HBM(keys.shape, bf16)
     return pl.pallas_call(
@@ -126,13 +126,14 @@
             layer_of((D, 3 * D), 0),
             pl.BlockSpec(memory_space=pltpu.HBM),
             pl.BlockSpec(memory_space=pltpu.HBM),
+            pl.BlockSpec(memory_space=pl.ANY),
         ],
         out_specs=[pl.BlockSpec((PATCH, D), lambda i: (last, 0))] * 2,
         out_shape=[ext, ext],
         input_output_aliases={4: 0, 5: 1},
         compiler_params=pltpu.CompilerParams(vmem_limit_bytes=24 << 20),
         name="qkv_halo",
-    )(before, after, gains, qkv_weight, keys, values)
+    )(before, after, gains, qkv_weight, keys, values, earlier)
 
 
 def qkv_owner_kernel(from_ref, part_ref, gains_ref, w_ref, x_ref, q_ref, k_ref, v_ref):
@@ -171,69 +172,130 @@
     )(owner_from, part, gains, qkv_weight)
 
 
+def forward_rows(inner, normed, up_ref, down_ref):
+    def rise(j):
+        return dot(normed, up_ref[:, HID * j : HID * (j + 1)])
+
+    total = None
+    up = rise(0)
+    for j in range(FF // HID):
+        later = rise(j + 1) if j + 1 < FF // HID else None
+        one = dot(gelu(up).astype(bf16), down_ref[HID * j : HID * (j + 1), :])
+        total = one if total is None else total + one
+        up = later
+    return (inner.astype(f32) + total).astype(bf16)
+
+
+def forward_owner_kernel(
+    from_ref, part_ref, gains_ref, up_ref, down_ref, w_ref, x_ref, q_ref, k_ref, v_ref
+):
+    unit = pl.program_id(0)
+    shape = (UNIT_TILES, PART, D)
+    tiles = []
+    for t in range(UNIT_TILES):
+        source = from_ref[unit * UNIT_TILES + t]
+        tile = part_ref[jnp.maximum(source, 0)]
+        tiles.append(jnp.where(source >= 0, tile.astype(f32), 0.0))
+    rows = jnp.concatenate(tiles, axis=0)
+    outer = forward_rows(rows, norm_rows(rows, gains_ref[1:2, :]), up_ref, down_ref)
+    x_ref[...] = outer.reshape(shape)
+    out = dot(norm_rows(outer.astype(f32), gains_ref[2:3, :]), w_ref[...])
+    q_ref[...] = (out[:, :D] * query_scale).astype(bf16).reshape(shape)
+    k_ref[...] = out[:, D : 2 * D].astype(bf16).reshape(shape)
+    v_ref[...] = out[:, 2 * D :].astype(bf16).reshape(shape)
+
+
+def forward_owner(owner_from, part, weights, qkv_weight):
+    gains, _, up_weight, down_weight = weights
+    block = pl.BlockSpec((UNIT_TILES, PART, D), lambda i, *_: (i, 0, 0))
+    return pl.pallas_call(
+        forward_owner_kernel,
+        grid_spec=pltpu.PrefetchScalarGridSpec(
+            num_scalar_prefetch=1,
+            grid=(SLOTS // UNIT_TILES,),
+            in_specs=[
+                pl.BlockSpec(memory_space=pltpu.VMEM),
+                whole((4, D)),
+                layer_of((D, FF), 0),
+                layer_of((FF, D), 0),
+                layer_of((D, 3 * D), 1),
+            ],
+            out_specs=[block] * 4,
+        ),
+        out_shape=[pltpu.HBM((SLOTS, PART, D), bf16)] * 4,
+        compiler_params=pltpu.CompilerParams(vmem_limit_bytes=30 << 20),
+        name="forward_owner",
+    )(owner_from, part, gains, up_weight, down_weight, qkv_weight)
+
+
+def attention_parts(masked, first_tile, table_ref, q_ref, k_refs, v_refs, mixed_ref):
+    pieces = len(k_refs)
+    count = UNIT_TILES * PART
+    rows = PATCH // pieces
+    lanes = lax.broadcasted_iota(jnp.int32, (1, 128), 1)
+    low = lanes < HEAD_DIM
+    picks = [low.astype(f32).astype(bf16), (~low).astype(f32).astype(bf16)]
+    queries = q_ref[...].reshape(count, D)
+    ones = jnp.ones((rows, 128), bf16)
+    extra_q = extra_k = None
+    if masked:
+        base = first_tile // PATCH_TILES * PATCH_TILES
+        extra_q = jnp.broadcast_to((lanes == 0).astype(f32).astype(bf16), (count, 128))
+        marks = []
+        for t in range(PATCH_TILES):
+            mark = jnp.where(table_ref[base + t] >= 0, 0.0, masked_score)
+            marks.append(jnp.full((rows // PATCH_TILES, 128), mark, f32).astype(bf16))
+        extra_k = jnp.concatenate(marks, axis=0)
+
+    def scores(h):
+        cols = slice(128 * (h // 2), 128 * (h // 2) + 128)
+        q = queries[:, cols] * picks[h % 2]
+        if masked:
+            q = jnp.concatenate([q, extra_q], axis=1)
+        out = []
+        for k_ref in k_refs:
+            k = k_ref[...].reshape(rows, D)[:, cols]
+            if masked:
+                k = jnp.concatenate([k, extra_k], axis=1)
+            out.append(dot_t(q, k))
+        return out
+
+    def soften(parts):
+        peak = functools.reduce(
+            jnp.maximum, [jnp.max(s, axis=-1, keepdims=True) for s in parts]
+        )
+        return [jnp.exp2(s - peak).astype(bf16) for s in parts]
+
+    def mix(h, parts):
+        cols = slice(128 * (h // 2), 128 * (h // 2) + 128)
+        total = None
+        for p, v_ref in zip(parts, v_refs):
+            v = v_ref[...].reshape(rows, D)[:, cols]
+            one = dot(p, jnp.concatenate([v, ones], axis=1))
+            total = one if total is None else total + one
+        own = (total[:, :128] / total[:, 128:]).astype(bf16) * picks[h % 2]
+        if h % 2:
+            own = own + mixed_ref[:, cols]
+        mixed_ref[:, cols] = own
+
+    return scores, soften, mix
+
+
 def block_kernel(units, masked, layer, pieces, table_ref, x_ref, q_ref, *refs):
     k_refs, refs = refs[:pieces], refs[pieces:]
     v_refs, refs = refs[:pieces], refs[pieces:]
     gains_ref, *sources, out_ref, mixed_ref, proj_ref, up_ref, down_ref, sems = refs
     step = pl.program_id(0)
     count = UNIT_TILES * PART
-    rows = PATCH // pieces
-    lanes = lax.broadcasted_iota(jnp.int32, (1, 128), 1)
-    low = lanes < HEAD_DIM
-    picks = [low.astype(f32).astype(bf16), (~low).astype(f32).astype(bf16)]
     fetches = [
         pltpu.make_async_copy(source.at[layer], target, sems.at[i])
         for i, (source, target) in enumerate(zip(sources, (proj_ref, up_ref, down_ref)))
     ]
 
-    def attention_parts():
-        queries = q_ref[...].reshape(count, D)
-        ones = jnp.ones((rows, 128), bf16)
-        extra_q = extra_k = None
-        if masked:
-            base = (step * UNIT_TILES) // PATCH_TILES * PATCH_TILES
-            extra_q = jnp.broadcast_to((lanes == 0).astype(f32).astype(bf16), (count, 128))
-            marks = []
-            for t in range(PATCH_TILES):
-                mark = jnp.where(table_ref[base + t] >= 0, 0.0, masked_score)
-                marks.append(jnp.full((rows // PATCH_TILES, 128), mark, f32).astype(bf16))
-            extra_k = jnp.concatenate(marks, axis=0)
-
-        def scores(h):
-            cols = slice(128 * (h // 2), 128 * (h // 2) + 128)
-            q = queries[:, cols] * picks[h % 2]
-            if masked:
-                q = jnp.concatenate([q, extra_q], axis=1)
-            out = []
-            for k_ref in k_refs:
-                k = k_ref[...].reshape(rows, D)[:, cols]
-                if masked:
-                    k = jnp.concatenate([k, extra_k], axis=1)
-                out.append(dot_t(q, k))
-            return out
-
-        def soften(parts):
-            peak = functools.reduce(
-                jnp.maximum, [jnp.max(s, axis=-1, keepdims=True) for s in parts]
-            )
-            return [jnp.exp2(s - peak).astype(bf16) for s in parts]
-
-        def mix(h, parts):
-            cols = slice(128 * (h // 2), 128 * (h // 2) + 128)
-            total = None
-            for p, v_ref in zip(parts, v_refs):
-                v = v_ref[...].reshape(rows, D)[:, cols]
-                one = dot(p, jnp.concatenate([v, ones], axis=1))
-                total = one if total is None else total + one
-            own = (total[:, :128] / total[:, 128:]).astype(bf16) * picks[h % 2]
-            if h % 2:
-                own = own + mixed_ref[:, cols]
-            mixed_ref[:, cols] = own
-
-        return scores, soften, mix
-
     def attention_steps():
-        scores, soften, mix = attention_parts()
+        scores, soften, mix = attention_parts(
+            masked, step * UNIT_TILES, table_ref, q_ref, k_refs, v_refs, mixed_ref
+        )
         s = scores(0)
         yield
         for h in range(HEADS):
@@ -311,6 +373,77 @@
         result = []
         weave(forward_steps(mixed_ref[...], result))
         emit(*result)
+
+
+def attention_kernel(place, masked, pieces, table_ref, x_ref, q_ref, *refs):
+    k_refs, refs = refs[:pieces], refs[pieces:]
+    v_refs, refs = refs[:pieces], refs[pieces:]
+    proj_ref, out_ref, mixed_ref, tiles_ref, sems = refs[0], *refs[-4:]
+    step = pl.program_id(0)
+    units = pl.num_programs(0)
+    count = UNIT_TILES * PART
+    first_tile = place(step) * UNIT_TILES
+    scores, soften, mix = attention_parts(
+        masked, first_tile, table_ref, q_ref, k_refs, v_refs, mixed_ref
+    )
+    s = scores(0)
+    for h in range(HEADS):
+        later = scores(h + 1) if h + 1 < HEADS else None
+        mix(h, soften(s))
+        s = later
+    base = x_ref[...].reshape(count, D).astype(f32)
+    inner = (base + dot(mixed_ref[...], proj_ref[...])).astype(bf16)
+    tiles_ref[pl.ds(step * UNIT_TILES, UNIT_TILES)] = inner.reshape(UNIT_TILES, PART, D)
+
+    def copy_of(unit, t, act):
+        slot = table_ref[place(unit) * UNIT_TILES + t]
+
+        @pl.when(slot >= 0)
+        def _():
+            i = unit * UNIT_TILES + t
+            act(
+                pltpu.make_async_copy(
+                    tiles_ref.at[i], out_ref.at[jnp.maximum(slot, 0)], sems.at[i]
+                )
+            )
+
+    for t in range(UNIT_TILES):
+        copy_of(step, t, lambda copy: copy.start())
+
+    @pl.when(step == units - 1)
+    def _():
+        @pl.loop(0, units)
+        def _(unit):
+            for t in range(UNIT_TILES):
+                copy_of(unit, t, lambda copy: copy.wait())
+
+
+def attention(name, table, x, q, keys, values, specs, units, place, masked, layer, proj, packed):
+    pieces = len(keys)
+    args = [table, x, q, *keys, *values, proj]
+    specs = [*specs, layer_of((D, D), layer)]
+    aliases = {}
+    if packed is not None:
+        aliases = {len(args): 0}
+        args.append(packed)
+        specs.append(pl.BlockSpec(memory_space=pltpu.HBM))
+    return pl.pallas_call(
+        functools.partial(attention_kernel, place, masked, pieces),
+        grid_spec=pltpu.PrefetchScalarGridSpec(
+            num_scalar_prefetch=1,
+            grid=(units,),
+            in_specs=specs,
+            out_specs=pl.BlockSpec(memory_space=pltpu.HBM),
+            scratch_shapes=[
+                pltpu.VMEM((UNIT_TILES * PART, D), bf16),
+                pltpu.VMEM((units * UNIT_TILES, PART, D), bf16),
+                pltpu.SemaphoreType.DMA((units * UNIT_TILES,)),
+            ],
+        ),
+        out_shape=pltpu.HBM((PEERS, PART, D), bf16),
+        input_output_aliases=aliases,
+        name=name,
+    )(*args)
 
 
 def block(name, table, x, q, keys, values, specs, units, masked, layer, weights):
@@ -339,64 +472,123 @@
     )(table, x, q, *keys, *values, gains, *matrices)
 
 
-def block_a(chunk, table, x, q, keys, values, weights):
-    units = TILES_DEV // UNIT_TILES
+def specs_a(chunk, x_place, place):
     shape = (UNIT_TILES, PART, D)
     own = TILES_DEV * TILE // HALF
 
     def first(i, *_):
-        patch = (now(i, units) + 1) // 2
+        patch = (place(i) + 1) // 2
         return patch + patch // 2, 0
 
     def second(i, *_):
-        patch = (now(i, units) + 1) // 2
+        patch = (place(i) + 1) // 2
         return jnp.where(patch == 1, 2, own + patch // 2), 0
 
     key_specs = [pl.BlockSpec((HALF, D), first), pl.BlockSpec((HALF, D), second)]
-    specs = [
-        pl.BlockSpec(shape, lambda i, *_: (prior(i), chunk, 0)),
-        pl.BlockSpec(shape, lambda i, *_: (now(i, units), chunk, 0)),
+    return [
+        pl.BlockSpec(shape, lambda i, *_: (x_place(i), chunk, 0)),
+        pl.BlockSpec(shape, lambda i, *_: (place(i), chunk, 0)),
         *key_specs,
         *key_specs,
     ]
+
+
+def attention_a(name, chunk, place, table, x, q, keys, values, proj, packed):
+    specs = specs_a(chunk, place, place)
+    return attention(
+        name, table, x, q, [keys] * 2, [values] * 2, specs, 2, place, False, 0, proj, packed
+    )
+
+
+def block_a(chunk, table, x, q, keys, values, weights):
+    units = TILES_DEV // UNIT_TILES
+    specs = specs_a(chunk, prior, lambda i: now(i, units))
     return block(
         "block_a", table, x, q, [keys] * 2, [values] * 2, specs, units, False, 0, weights
     )
 
 
+def specs_b(x_place, place):
+    shape = (UNIT_TILES, PART, D)
+    patch = (PATCH_TILES, PART, D)
+    key_spec = pl.BlockSpec(patch, lambda i, *_: (place(i) // 2, 0, 0))
+    return [
+        pl.BlockSpec(shape, lambda i, *_: (x_place(i), 0, 0)),
+        pl.BlockSpec(shape, lambda i, *_: (place(i), 0, 0)),
+    ] + [key_spec] * (2 * CHUNKS)
+
+
+def attention_b(table, x, q, keys, values, proj):
+    units = SLOTS // UNIT_TILES
+
+    def place(i):
+        return i
+
+    specs = specs_b(place, place)
+    return attention(
+        "attention_b", table, x, q, keys, values, specs, units, place, True, 1, proj, None
+    )
+
+
 def block_b(table, x, q, keys, values, weights):
     units = SLOTS // UNIT_TILES
-    shape = (UNIT_TILES, PART, D)
-    patch = (PATCH_TILES, PART, D)
-    key_spec = pl.BlockSpec(patch, lambda i, *_: (now(i, units) // 2, 0, 0))
-    specs = [
-        pl.BlockSpec(shape, lambda i, *_: (prior(i), 0, 0)),
-        pl.BlockSpec(shape, lambda i, *_: (now(i, units), 0, 0)),
-    ] + [key_spec] * (2 * CHUNKS)
-    return block("block_b", table, x, q, keys, values, specs, units, True, 1, weights)
-
-
-def home_kernel(table_ref, *refs):
-    parts, out_ref = refs[:CHUNKS], refs[CHUNKS]
-    @pl.loop(0, TILES_DEV)
-    def _(t):
-        for c, part_ref in enumerate(parts):
-            out_ref[t, c * PART : (c + 1) * PART] = part_ref[table_ref[t]]
-
-
-def home(table, parts):
+    specs = specs_b(prior, lambda i: now(i, units))
+    return block(
+        "block_b", table, x, q, keys, values, specs, units, True, 1, weights
+    )
+
+
+def forward_home_kernel(table_ref, part_ref, gains_ref, up_ref, down_ref, out_ref):
+    step = pl.program_id(0)
+    tiles = [part_ref[table_ref[step * UNIT_TILES + t]] for t in range(UNIT_TILES)]
+    rows = jnp.concatenate(tiles, axis=0)
+    normed = norm_rows(rows.astype(f32), gains_ref[3:4, :])
+    out_ref[...] = forward_rows(rows, normed, up_ref, down_ref).reshape(UNIT_TILES, PART, D)
+
+
+def forward_home(table, part, weights):
+    gains, _, up_weight, down_weight = weights
+    return pl.pallas_call(
+        forward_home_kernel,
+        grid_spec=pltpu.PrefetchScalarGridSpec(
+            num_scalar_prefetch=1,
+            grid=(TILES_DEV // UNIT_TILES,),
+            in_specs=[
+                pl.BlockSpec(memory_space=pltpu.VMEM),
+                whole((4, D)),
+                layer_of((D, FF), 1),
+                layer_of((FF, D), 1),
+            ],
+            out_specs=pl.BlockSpec((UNIT_TILES, PART, D), lambda i, *_: (i, 0, 0)),
+        ),
+        out_shape=pltpu.HBM((TILES_DEV, TILE, D), bf16),
+        compiler_params=pltpu.CompilerParams(vmem_limit_bytes=30 << 20),
+        name="forward_home",
+    )(table, part, gains, up_weight, down_weight)
+
+
+def home_kernel(table_ref, part_ref, done_in, out_ref):
+    for t in range(TILES_DEV):
+        out_ref[t] = part_ref[table_ref[t]]
+
+
+def home(table, part, done):
     return pl.pallas_call(
         home_kernel,
         grid_spec=pltpu.PrefetchScalarGridSpec(
             num_scalar_prefetch=1,
             grid=(1,),
-            in_specs=[pl.BlockSpec(memory_space=pltpu.VMEM)] * CHUNKS,
-            out_specs=whole((TILES_DEV, TILE, D)),
+            in_specs=[
+                pl.BlockSpec(memory_space=pltpu.VMEM),
+                pl.BlockSpec(memory_space=pltpu.HBM),
+            ],
+            out_specs=pl.BlockSpec((TILES_DEV, PART, D), lambda i, *_: (0, 1, 0)),
         ),
-        out_shape=jax.ShapeDtypeStruct((TILES_DEV, TILE, D), bf16),
+        out_shape=pltpu.HBM((TILES_DEV, TILE, D), bf16),
+        input_output_aliases={2: 0},
         compiler_params=pltpu.CompilerParams(vmem_limit_bytes=12 << 20),
         name="home",
-    )(table, *parts)
+    )(table, part, done)
 
 
 def exchange(part):
@@ -412,24 +604,30 @@
     before = lax.ppermute(points[rows - HALF :], axes, [(i, (i + 1) % ring) for i in range(ring)])
     after = lax.ppermute(points[:HALF], axes, [((i + 1) % ring, i) for i in range(ring)])
     weights = (norm_gains, proj_weight, up_weight, down_weight)
+    tiled = (TILES_DEV, TILE, D)
+    x = points.reshape(tiled)
     q, keys, values = qkv_own(points, norm_gains, qkv_weight)
-    keys, values = qkv_halo(before, after, norm_gains, qkv_weight, keys, values)
-    tiled = (TILES_DEV, TILE, D)
-    x, q = points.reshape(tiled), q.reshape(tiled)
-    sent = []
-    for chunk in range(CHUNKS):
-        packed = block_a(chunk, dest_slot, x, q, keys, values, weights)
-        sent.append(exchange(packed))
-    owned = [qkv_owner(owner_from, part, norm_gains, qkv_weight) for part in sent]
-    owner_keys = [one[2] for one in owned]
-    owner_values = [one[3] for one in owned]
-    returned = []
-    for chunk in range(CHUNKS):
-        done = block_b(
-            owner_from, owned[chunk][0], owned[chunk][1], owner_keys, owner_values, weights
-        )
-        returned.append(exchange(done))
-    return home(dest_slot, returned).reshape(rows, D)
+    q = q.reshape(tiled)
+    packed = attention_a(
+        "attention_a_middle", 0, lambda i: i + 1, dest_slot, x, q, keys, values, proj_weight, None
+    )
+    keys, values = qkv_halo(before, after, norm_gains, qkv_weight, keys, values, packed)
+    packed = attention_a(
+        "attention_a_edges", 0, lambda i: 3 * i, dest_slot, x, q, keys, values, proj_weight, packed
+    )
+    early = exchange(packed)
+    late = exchange(block_a(1, dest_slot, x, q, keys, values, weights))
+    owned = [
+        forward_owner(owner_from, early, weights, qkv_weight),
+        qkv_owner(owner_from, late, norm_gains, qkv_weight),
+    ]
+    xs, qs, owner_keys, owner_values = zip(*owned)
+    early = exchange(
+        attention_b(owner_from, xs[0], qs[0], owner_keys, owner_values, proj_weight)
+    )
+    late = exchange(block_b(owner_from, xs[1], qs[1], owner_keys, owner_values, weights))
+    done = forward_home(dest_slot, early, weights)
+    return home(dest_slot, late, done).reshape(rows, D)
 
 
 def solution(mesh):

time: 188 us -> 182 us (0.968)
  blocking collectives: 29.7 us -> 0 us
  Pallas kernels: 101 us -> 112 us
  starting transfers between devices: 21.6 us -> 29.8 us
  local copies, waits for them, and re-layouts: 1.22 us -> 8.91 us
  waiting for transfers between devices: 32.7 us -> 28.2 us
    pallas_call x0 -> x5, Pallas kernels: none -> 54.5 us  [the longest x3 32.6 us: attention(): pl.pallas_call(functools.partial(attention_kernel, place, masked, pieces)...]
    pallas_call x4 -> x2, Pallas kernels: 80.6 us -> 40.3 us  [block(): pl.pallas_call(functools.partial(block_kernel, units, masked, layer, piec...]
    all_to_all x1 -> x0, blocking collectives: 29.7 us -> none  [exchange(): lax.all_to_all(part, 'chain', split_axis=0, concat_axis=0, tiled=True)]
    all_to_all x3 -> x4, starting transfers between devices: 13.3 us -> 21.5 us  [exchange(): lax.all_to_all(part, 'chain', split_axis=0, concat_axis=0, tiled=True)]
    unnamed x10 -> x26, local copies, waits for them, and re-layouts: 0.03 us -> 7.72 us
    ppermute x1, waiting for transfers between devices: 6.53 us -> 0.01 us  [body(): lax.ppermute(points[rows - HALF:], axes, [(i, (i + 1) % ring) for i in ra...]
    pallas_call x2 -> x1, Pallas kernels: 10.2 us -> 5.79 us  [qkv_owner(): pl.pallas_call(qkv_owner_kernel, grid_spec=pltpu.PrefetchScalarGridSpec(n...]
    all_to_all x3 -> x4, waiting for transfers between devices: 26.2 us -> 28.2 us  [exchange(): lax.all_to_all(part, 'chain', split_axis=0, concat_axis=0, tiled=True)]
  transfers between devices with their start and end apart: 5 -> 6, of which waited for: 4 -> 4; matrix products, arithmetic and copies ran while one was open for 0% -> 0% of each run, Pallas kernels for 27% -> 42%
where the time goes in v5:
time: 182 us; the launch traced here: 179 us
  Pallas kernels  112 us (62%)
  starting transfers between devices  29.8 us (16%)
  waiting for transfers between devices  28.2 us (15%)
  local copies, waits for them, and re-layouts  8.91 us (5%)
    pallas_call x2, Pallas kernels, block(): pl.pallas_call(functools.partial(block_kernel, units, masked, layer, piec...  40.3 us
    pallas_call x3, Pallas kernels, attention(): pl.pallas_call(functools.partial(attention_kernel, place, masked, pieces)...  32.6 us
    all_to_all x4, waiting for transfers between devices, exchange(): lax.all_to_all(part, 'chain', split_axis=0, concat_axis=0, tiled=True)  28.2 us
    all_to_all x4, starting transfers between devices, exchange(): lax.all_to_all(part, 'chain', split_axis=0, concat_axis=0, tiled=True)  21.5 us
    pallas_call x1, Pallas kernels, forward_owner(): pl.pallas_call(forward_owner_kernel, grid_spec=pltpu.PrefetchScalarGridSp...  14.3 us
    ppermute x1, starting transfers between devices, body(): lax.ppermute(points[:HALF], axes, [((i + 1) % ring, i) for i in range(rin...  8.31 us
    unnamed x26, local copies, waits for them, and re-layouts  7.72 us
    pallas_call x1, Pallas kernels, forward_home(): pl.pallas_call(forward_home_kernel, grid_spec=pltpu.PrefetchScalarGridSpe...  7.69 us
  transfers between devices with their start and end apart: 6, of which 4 were waited for; matrix products, arithmetic and copies ran while one was open for 0% of the time, Pallas kernels for 42%

profile of v5, /device:TPU:0, one launch (start us, length us, event | category | flops | bytes accessed | tf_op | source)
XLA Modules:
  0.0 179.1 jit_solution(8760801698079365867)
XLA Ops:
  0.0 1.2 fusion
  1.2 8.3 %collective-permute-start.1 = (bf16[512,384]{1,0:T(8,128)(2,1)S(1)}, bf16[512,384]{1,0:T(8,128)(2,1)S(1)}, u32[]{:S(2)}, u32[]{:S(2)}) collective-permute-start(bf16[512,384]{1,0:T(8,128)(2,1)S(1)} %get-tuple-element.31), channel_id=1, source_target_pairs={{1,0},{2,1},{3,2},{4,3},{5,4},{6,5},{7,6},{8,7},{9,8},{10,9},{11,1... | collective-permute-start | bytes 1179656 | tf_op jit(solution)/shard_map/ppermute | solution.py:605
  9.5 6.0 %qkv_own.1 = (bf16[2048,384]{1,0:T(8,128)(2,1)}, bf16[3072,384]{1,0:T(8,128)(2,1)}, bf16[3072,384]{1,0:T(8,128)(2,1)}) custom-call(bf16[2048,384]{1,0:T(8,128)(2,1)} %x_ref.1, f32[4,384]{1,0:T(4,128)} %gains_ref.9, bf16[2,384,1152]{2,1,0:T(8,128)(2,1)} %w_ref.7), custom_call_target="tpu_custom_call" | custom-call | tf_op jit(solution)/shard_map/qkv_own/pallas_call | solution.py:93
  15.5 7.8 %attention_a_middle.1.after_in.refs_5_ = bf16[32,64,384]{2,1,0:T(8,128)(2,1)} custom-call(s32[16]{0:T(128)} %table_ref.13, bf16[16,128,384]{2,1,0:T(8,128)(2,1)} %bitcast.3, bf16[16,128,384]{2,1,0:T(8,128)(2,1)} %bitcast.6, bf16[3072,384]{1,0:T(8,128)(2,1)} %get-tuple-element.19.refs_0_.refs_1_.k_in, ...), custom_call_target="tpu_custom_call" | custom-call | tf_op jit(solution)/shard_map/attention_a_middle/pallas_call | solution.py:430
  23.3 1.4 copy-done.7
  24.7 2.4 %qkv_halo.1 = (bf16[3072,384]{1,0:T(8,128)(2,1)}, bf16[3072,384]{1,0:T(8,128)(2,1)}) custom-call(bf16[512,384]{1,0:T(8,128)(2,1)S(1)} %collective-permute-done.a_ref, bf16[512,384]{1,0:T(8,128)(2,1)S(1)} %collective-permute-done.1.b_ref, f32[4,384]{1,0:T(4,128)S(1)} %copy-done.8, ...), custom_call_target="tpu_custom_call", output_to_operand_aliasing={{0}: (4, {}), {1}: (5, {})} | custom-call | tf_op jit(solution)/shard_map/qkv_halo/pallas_call | solution.py:119
  27.1 7.6 %attention_a_edges.1 = bf16[32,64,384]{2,1,0:T(8,128)(2,1)} custom-call(s32[16]{0:T(128)} %table_ref.13, bf16[16,128,384]{2,1,0:T(8,128)(2,1)} %bitcast.4, bf16[16,128,384]{2,1,0:T(8,128)(2,1)} %bitcast.7, bf16[3072,384]{1,0:T(8,128)(2,1)} %get-tuple-element.21.refs_0_.refs_1_, ...), custom_call_target="tpu_custom_call", output_to_operand_aliasing={{}: (8, {})} | custom-call | tf_op jit(solution)/shard_map/attention_a_edges/pallas_call | solution.py:430
  34.8 4.9 %all-to-all-start.1 = ((bf16[32,64,384]{2,1,0:T(8,128)(2,1)}), bf16[32,64,384]{2,1,0:T(8,128)(2,1)}, u32[]{:S(2)}, u32[]{:S(2)}) async-start(bf16[32,64,384]{2,1,0:T(8,128)(2,1)} %attention_a_edges.1), calls=%async_computation.1 | async-start | bytes 3145728 | tf_op jit(solution)/shard_map/all_to_all | solution.py:595
  39.7 17.0 %block_a.1 = bf16[32,64,384]{2,1,0:T(8,128)(2,1)} custom-call(s32[16]{0:T(128)} %table_ref.13, bf16[16,128,384]{2,1,0:T(8,128)(2,1)} %bitcast.5, bf16[16,128,384]{2,1,0:T(8,128)(2,1)} %bitcast.8, bf16[3072,384]{1,0:T(8,128)(2,1)} %get-tuple-element.21.refs_0_.refs_1_, bf16[3072,384]{1,0:T(8,128)(2,1)} %get-tuple-element.21.refs_0_.refs_1_, ...), custom_call_target="tpu_custom_call" | custom-call | tf_op jit(solution)/shard_map/block_a/pallas_call | solution.py:453
  56.7 0.0 copy-start
  56.7 0.0 copy-start.9
  56.7 0.0 copy-start.12
  56.7 6.7 %all-to-all-done.1.part_ref = bf16[32,64,384]{2,1,0:T(8,128)(2,1)} async-done(((bf16[32,64,384]{2,1,0:T(8,128)(2,1)}), bf16[32,64,384]{2,1,0:T(8,128)(2,1)}, u32[]{:S(2)}, u32[]{:S(2)}) %all-to-all-start.1) | async-done | bytes 1572896 | tf_op jit(solution)/shard_map/all_to_all | solution.py:595
  63.4 4.7 %all-to-all-start = ((bf16[32,64,384]{2,1,0:T(8,128)(2,1)}), bf16[32,64,384]{2,1,0:T(8,128)(2,1)}, u32[]{:S(2)}, u32[]{:S(2)}) async-start(bf16[32,64,384]{2,1,0:T(8,128)(2,1)} %block_a.1), calls=%async_computation | async-start | bytes 3145728 | tf_op jit(solution)/shard_map/all_to_all | solution.py:595
  68.1 0.0 copy-start.2
  68.1 1.7 copy-done.2
  69.8 1.5 copy-done.5
  71.3 14.3 %forward_owner.1 = (bf16[24,64,384]{2,1,0:T(8,128)(2,1)}, bf16[24,64,384]{2,1,0:T(8,128)(2,1)}, bf16[24,64,384]{2,1,0:T(8,128)(2,1)}, bf16[24,64,384]{2,1,0:T(8,128)(2,1)}) custom-call(s32[24]{0:T(128)S(1)} %copy-done.12, bf16[32,64,384]{2,1,0:T(8,128)(2,1)} %all-to-all-done.1.part_ref, f32[4,384]{1,0:T(4,128)S(1)} %copy-done.9, ...), custom_call_target="tpu_custom_call" | custom-call | tf_op jit(solution)/shard_map/forward_owner/pallas_call | solution.py:211
  85.6 6.4 %all-to-all-done.part_ref = bf16[32,64,384]{2,1,0:T(8,128)(2,1)} async-done(((bf16[32,64,384]{2,1,0:T(8,128)(2,1)}), bf16[32,64,384]{2,1,0:T(8,128)(2,1)}, u32[]{:S(2)}, u32[]{:S(2)}) %all-to-all-start) | async-done | bytes 1572896 | tf_op jit(solution)/shard_map/all_to_all | solution.py:595
  92.0 1.5 copy-done.6
  93.5 5.8 %qkv_owner.1 = (bf16[24,64,384]{2,1,0:T(8,128)(2,1)}, bf16[24,64,384]{2,1,0:T(8,128)(2,1)}, bf16[24,64,384]{2,1,0:T(8,128)(2,1)}, bf16[24,64,384]{2,1,0:T(8,128)(2,1)}) custom-call(s32[24]{0:T(128)S(1)} %copy-done.12, bf16[32,64,384]{2,1,0:T(8,128)(2,1)} %all-to-all-done.part_ref, f32[4,384]{1,0:T(4,128)S(1)} %copy-done.9, bf16[2,384,1152]{2,1,0:T(8,128)(2,1)S(1)} %copy-done.6), custom_call_target="tpu_custom_call" | custom-call | tf_op jit(solution)/shard_map/qkv_owner/pallas_call | solution.py:157
  99.3 17.2 %attention_b.1 = bf16[32,64,384]{2,1,0:T(8,128)(2,1)} custom-call(s32[24]{0:T(128)} %table_ref.11, bf16[24,64,384]{2,1,0:T(8,128)(2,1)} %get-tuple-element.29.x_ref, bf16[24,64,384]{2,1,0:T(8,128)(2,1)} %get-tuple-element.30.q_ref, bf16[24,64,384]{2,1,0:T(8,128)(2,1)} %get-tuple-element.25.refs_0_, bf16[24,64,384]{2,1,0:T(8,128)(2,1)} %get-tuple-element.26.refs_1_, ...), custom_call_target="tpu_custom_call" | custom-call | tf_op jit(solution)/shard_map/attention_b/pallas_call | solution.py:430
  116.4 4.9 %all-to-all-start.3 = ((bf16[32,64,384]{2,1,0:T(8,128)(2,1)}), bf16[32,64,384]{2,1,0:T(8,128)(2,1)}, u32[]{:S(2)}, u32[]{:S(2)}) async-start(bf16[32,64,384]{2,1,0:T(8,128)(2,1)} %attention_b.1), calls=%async_computation.3 | async-start | bytes 3145728 | tf_op jit(solution)/shard_map/all_to_all | solution.py:595
  121.4 23.3 %block_b.1 = bf16[32,64,384]{2,1,0:T(8,128)(2,1)} custom-call(s32[24]{0:T(128)} %table_ref.11, bf16[24,64,384]{2,1,0:T(8,128)(2,1)} %get-tuple-element.23.x_ref, bf16[24,64,384]{2,1,0:T(8,128)(2,1)} %get-tuple-element.24.q_ref, bf16[24,64,384]{2,1,0:T(8,128)(2,1)} %get-tuple-element.25.refs_0_, bf16[24,64,384]{2,1,0:T(8,128)(2,1)} %get-tuple-element.26.refs_1_, ...), custom_call_target="tpu_custom_call" | custom-call | tf_op jit(solution)/shard_map/block_b/pallas_call | solution.py:453
  144.7 0.0 copy-start.10
  144.7 0.0 copy-start.11
  144.7 0.5 all-to-all-done.3.part_ref
  145.3 7.0 %all-to-all-start.2 = ((bf16[32,64,384]{2,1,0:T(8,128)(2,1)}), bf16[32,64,384]{2,1,0:T(8,128)(2,1)}, u32[]{:S(2)}, u32[]{:S(2)}) async-start(bf16[32,64,384]{2,1,0:T(8,128)(2,1)} %block_b.1), calls=%async_computation.2 | async-start | bytes 3145728 | tf_op jit(solution)/shard_map/all_to_all | solution.py:595
  152.3 1.7 copy-done.3
  154.0 7.7 %forward_home.1.done_in = bf16[16,128,384]{2,1,0:T(8,128)(2,1)} custom-call(s32[16]{0:T(128)S(1)} %copy-done.11, bf16[32,64,384]{2,1,0:T(8,128)(2,1)} %all-to-all-done.3.part_ref, f32[4,384]{1,0:T(4,128)S(1)} %copy-done.10, bf16[2,384,1536]{2,1,0:T(8,128)(2,1)S(1)} %copy-done.1, bf16[2,1536,384]{2,1,0:T(8,128)(2,1)S(1)} %copy-done.3), custom_call_target="tpu_custom_call" | custom-call | tf_op jit(solution)/shard_map/forward_home/pallas_call | solution.py:551
  161.7 14.5 %all-to-all-done.2.part_ref = bf16[32,64,384]{2,1,0:T(8,128)(2,1)} async-done(((bf16[32,64,384]{2,1,0:T(8,128)(2,1)}), bf16[32,64,384]{2,1,0:T(8,128)(2,1)}, u32[]{:S(2)}, u32[]{:S(2)}) %all-to-all-start.2) | async-done | bytes 1572896 | tf_op jit(solution)/shard_map/all_to_all | solution.py:595
  176.2 2.9 %home.1 = bf16[16,128,384]{2,1,0:T(8,128)(2,1)} custom-call(s32[16]{0:T(128)S(1)} %copy-done.11, bf16[32,64,384]{2,1,0:T(8,128)(2,1)} %all-to-all-done.2.part_ref, bf16[16,128,384]{2,1,0:T(8,128)(2,1)} %forward_home.1.done_in), custom_call_target="tpu_custom_call", output_to_operand_aliasing={{}: (2, {})} | custom-call | tf_op jit(solution)/shard_map/home/pallas_call | solution.py:576
  (18 shorter events, 0.0 us)
Async XLA Ops:
  1.2 22.1 %collective-permute-start.1 = (bf16[512,384]{1,0:T(8,128)(2,1)S(1)}, bf16[512,384]{1,0:T(8,128)(2,1)S(1)}, u32[]{:S(2)}, u32[]{:S(2)}) collective-permute-start(bf16[512,384]{1,0:T(8,128)(2,1)S(1)} %get-tuple-element.31), channel_id=1, source_target_pairs={{1,0},{2,1},{3,2},{4,3},{5,4},{6,5},{7,6},{8,7},{9,8},{10,9},{11,1... | collective-permute-start | bytes 1179656 | tf_op jit(solution)/shard_map/ppermute | solution.py:605
  9.5 13.8 %collective-permute-start = (bf16[512,384]{1,0:T(8,128)(2,1)S(1)}, bf16[512,384]{1,0:T(8,128)(2,1)S(1)}, u32[]{:S(2)}, u32[]{:S(2)}) collective-permute-start(bf16[512,384]{1,0:T(8,128)(2,1)S(1)} %get-tuple-element.32), channel_id=1, source_target_pairs={{0,1},{1,2},{2,3},{3,4},{4,5},{5,6},{6,7},{7,8},{8,9},{9,10},{10,1... | collective-permute-start | bytes 1179656 | tf_op jit(solution)/shard_map/ppermute | solution.py:604
  15.5 7.8 %copy-start.4 = (bf16[2,384,1152]{2,1,0:T(8,128)(2,1)S(1)}, bf16[2,384,1152]{2,1,0:T(8,128)(2,1)}, u32[]{:S(2)}) copy-start(bf16[2,384,1152]{2,1,0:T(8,128)(2,1)} %w_ref.7) | copy-start | bytes 5308420
  15.5 7.8 %copy-start.8 = (f32[4,384]{1,0:T(4,128)S(1)}, f32[4,384]{1,0:T(4,128)}, u32[]{:S(2)}) copy-start(f32[4,384]{1,0:T(4,128)} %gains_ref.9) | copy-start | bytes 18436
  23.3 1.4 copy-start.7
  34.8 28.6 %all-to-all-start.1 = ((bf16[32,64,384]{2,1,0:T(8,128)(2,1)}), bf16[32,64,384]{2,1,0:T(8,128)(2,1)}, u32[]{:S(2)}, u32[]{:S(2)}) async-start(bf16[32,64,384]{2,1,0:T(8,128)(2,1)} %attention_a_edges.1), calls=%async_computation.1 | async-start | bytes 3145728 | tf_op jit(solution)/shard_map/all_to_all | solution.py:595
  56.7 11.4 %copy-start = (bf16[2,384,1536]{2,1,0:T(8,128)(2,1)S(1)}, bf16[2,384,1536]{2,1,0:T(8,128)(2,1)}, u32[]{:S(2)}) copy-start(bf16[2,384,1536]{2,1,0:T(8,128)(2,1)} %up_ref.3) | copy-start | bytes 7077892
  56.7 11.4 %copy-start.9 = (f32[4,384]{1,0:T(4,128)S(1)}, f32[4,384]{1,0:T(4,128)}, u32[]{:S(2)}) copy-start(f32[4,384]{1,0:T(4,128)} %gains_ref.9) | copy-start | bytes 18436
  56.7 11.4 %copy-start.12 = (s32[24]{0:T(128)S(1)}, s32[24]{0:T(128)}, u32[]{:S(2)}) copy-start(s32[24]{0:T(128)} %table_ref.11) | copy-start | bytes 292
  63.4 28.6 %all-to-all-start = ((bf16[32,64,384]{2,1,0:T(8,128)(2,1)}), bf16[32,64,384]{2,1,0:T(8,128)(2,1)}, u32[]{:S(2)}, u32[]{:S(2)}) async-start(bf16[32,64,384]{2,1,0:T(8,128)(2,1)} %block_a.1), calls=%async_computation | async-start | bytes 3145728 | tf_op jit(solution)/shard_map/all_to_all | solution.py:595
  68.1 1.7 copy-start.2
  69.8 1.5 copy-start.5
  92.0 1.5 copy-start.6
  116.4 28.8 %all-to-all-start.3 = ((bf16[32,64,384]{2,1,0:T(8,128)(2,1)}), bf16[32,64,384]{2,1,0:T(8,128)(2,1)}, u32[]{:S(2)}, u32[]{:S(2)}) async-start(bf16[32,64,384]{2,1,0:T(8,128)(2,1)} %attention_b.1), calls=%async_computation.3 | async-start | bytes 3145728 | tf_op jit(solution)/shard_map/all_to_all | solution.py:595
  144.7 7.6 %copy-start.1 = (bf16[2,384,1536]{2,1,0:T(8,128)(2,1)S(1)}, bf16[2,384,1536]{2,1,0:T(8,128)(2,1)}, u32[]{:S(2)}) copy-start(bf16[2,384,1536]{2,1,0:T(8,128)(2,1)} %up_ref.3) | copy-start | bytes 7077892
  144.7 7.6 %copy-start.10 = (f32[4,384]{1,0:T(4,128)S(1)}, f32[4,384]{1,0:T(4,128)}, u32[]{:S(2)}) copy-start(f32[4,384]{1,0:T(4,128)} %gains_ref.9) | copy-start | bytes 18436
  144.7 7.6 %copy-start.11 = (s32[16]{0:T(128)S(1)}, s32[16]{0:T(128)}, u32[]{:S(2)}) copy-start(s32[16]{0:T(128)} %table_ref.13) | copy-start | bytes 196
  145.3 30.9 %all-to-all-start.2 = ((bf16[32,64,384]{2,1,0:T(8,128)(2,1)}), bf16[32,64,384]{2,1,0:T(8,128)(2,1)}, u32[]{:S(2)}, u32[]{:S(2)}) async-start(bf16[32,64,384]{2,1,0:T(8,128)(2,1)} %block_b.1), calls=%async_computation.2 | async-start | bytes 3145728 | tf_op jit(solution)/shard_map/all_to_all | solution.py:595
  152.3 1.7 copy-start.3

commit v6 on v5

--- a/solution.py
+++ b/solution.py
@@ -23,6 +23,7 @@
 UNIT_TILES = 4
 HALF = PATCH // 2
 HID = 256
+FULL_VMEM = 65000 << 10
 
 norm_epsilon = 1e-05
 masked_score = -1000000000.0
@@ -126,7 +127,7 @@
             layer_of((D, 3 * D), 0),
             pl.BlockSpec(memory_space=pltpu.HBM),
             pl.BlockSpec(memory_space=pltpu.HBM),
-            pl.BlockSpec(memory_space=pl.ANY),
+            pl.BlockSpec(memory_space=pltpu.HBM),
         ],
         out_specs=[pl.BlockSpec((PATCH, D), lambda i: (last, 0))] * 2,
         out_shape=[ext, ext],
@@ -136,15 +137,28 @@
     )(before, after, gains, qkv_weight, keys, values, earlier)
 
 
-def qkv_owner_kernel(from_ref, part_ref, gains_ref, w_ref, x_ref, q_ref, k_ref, v_ref):
-    patch = pl.program_id(0)
+def gather_specs(count):
+    def spec(t):
+        return pl.BlockSpec(
+            (None, PART, D), lambda i, table: (jnp.maximum(table[i * count + t], 0), 0, 0)
+        )
+
+    return [spec(t) for t in range(count)]
+
+
+def live_rows(table_ref, step, tile_refs):
+    tiles = []
+    for t, tile_ref in enumerate(tile_refs):
+        live = table_ref[step * len(tile_refs) + t] >= 0
+        tiles.append(jnp.where(live, tile_ref[...].astype(f32), 0.0))
+    return jnp.concatenate(tiles, axis=0)
+
+
+def qkv_owner_kernel(from_ref, *refs):
+    part_refs, refs = refs[:PATCH_TILES], refs[PATCH_TILES:]
+    gains_ref, w_ref, x_ref, q_ref, k_ref, v_ref = refs
     shape = (PATCH_TILES, PART, D)
-    tiles = []
-    for t in range(PATCH_TILES):
-        source = from_ref[patch * PATCH_TILES + t]
-        tile = part_ref[jnp.maximum(source, 0)]
-        tiles.append(jnp.where(source >= 0, tile.astype(f32), 0.0))
-    rows = jnp.concatenate(tiles, axis=0)
+    rows = live_rows(from_ref, pl.program_id(0), part_refs)
     x_ref[...] = rows.astype(bf16).reshape(shape)
     out = dot(norm_rows(rows, gains_ref[2:3, :]), w_ref[...])
     q_ref[...] = (out[:, :D] * query_scale).astype(bf16).reshape(shape)
@@ -159,17 +173,12 @@
         grid_spec=pltpu.PrefetchScalarGridSpec(
             num_scalar_prefetch=1,
             grid=(SLOTS // PATCH_TILES,),
-            in_specs=[
-                pl.BlockSpec(memory_space=pltpu.VMEM),
-                whole((4, D)),
-                layer_of((D, 3 * D), 1),
-            ],
+            in_specs=gather_specs(PATCH_TILES) + [whole((4, D)), layer_of((D, 3 * D), 1)],
             out_specs=[block] * 4,
         ),
         out_shape=[pltpu.HBM((SLOTS, PART, D), bf16)] * 4,
-        compiler_params=pltpu.CompilerParams(vmem_limit_bytes=24 << 20),
         name="qkv_owner",
-    )(owner_from, part, gains, qkv_weight)
+    )(owner_from, *[part] * PATCH_TILES, gains, qkv_weight)
 
 
 def forward_rows(inner, normed, up_ref, down_ref):
@@ -186,17 +195,11 @@
     return (inner.astype(f32) + total).astype(bf16)
 
 
-def forward_owner_kernel(
-    from_ref, part_ref, gains_ref, up_ref, down_ref, w_ref, x_ref, q_ref, k_ref, v_ref
-):
-    unit = pl.program_id(0)
+def forward_owner_kernel(from_ref, *refs):
+    part_refs, refs = refs[:UNIT_TILES], refs[UNIT_TILES:]
+    gains_ref, up_ref, down_ref, w_ref, x_ref, q_ref, k_ref, v_ref = refs
     shape = (UNIT_TILES, PART, D)
-    tiles = []
-    for t in range(UNIT_TILES):
-        source = from_ref[unit * UNIT_TILES + t]
-        tile = part_ref[jnp.maximum(source, 0)]
-        tiles.append(jnp.where(source >= 0, tile.astype(f32), 0.0))
-    rows = jnp.concatenate(tiles, axis=0)
+    rows = live_rows(from_ref, pl.program_id(0), part_refs)
     outer = forward_rows(rows, norm_rows(rows, gains_ref[1:2, :]), up_ref, down_ref)
     x_ref[...] = outer.reshape(shape)
     out = dot(norm_rows(outer.astype(f32), gains_ref[2:3, :]), w_ref[...])
@@ -213,8 +216,8 @@
         grid_spec=pltpu.PrefetchScalarGridSpec(
             num_scalar_prefetch=1,
             grid=(SLOTS // UNIT_TILES,),
-            in_specs=[
-                pl.BlockSpec(memory_space=pltpu.VMEM),
+            in_specs=gather_specs(UNIT_TILES)
+            + [
                 whole((4, D)),
                 layer_of((D, FF), 0),
                 layer_of((FF, D), 0),
@@ -223,9 +226,9 @@
             out_specs=[block] * 4,
         ),
         out_shape=[pltpu.HBM((SLOTS, PART, D), bf16)] * 4,
-        compiler_params=pltpu.CompilerParams(vmem_limit_bytes=30 << 20),
+        compiler_params=pltpu.CompilerParams(vmem_limit_bytes=FULL_VMEM),
         name="forward_owner",
-    )(owner_from, part, gains, up_weight, down_weight, qkv_weight)
+    )(owner_from, *[part] * UNIT_TILES, gains, up_weight, down_weight, qkv_weight)
 
 
 def attention_parts(masked, first_tile, table_ref, q_ref, k_refs, v_refs, mixed_ref):
@@ -281,10 +284,10 @@
     return scores, soften, mix
 
 
-def block_kernel(units, masked, layer, pieces, table_ref, x_ref, q_ref, *refs):
+def block_kernel(units, masked, whole_units, layer, pieces, table_ref, x_ref, q_ref, *refs):
     k_refs, refs = refs[:pieces], refs[pieces:]
     v_refs, refs = refs[:pieces], refs[pieces:]
-    gains_ref, *sources, out_ref, mixed_ref, proj_ref, up_ref, down_ref, sems = refs
+    gains_ref, _, *sources, out_ref, mixed_ref, proj_ref, up_ref, down_ref, sems = refs
     step = pl.program_id(0)
     count = UNIT_TILES * PART
     fetches = [
@@ -345,14 +348,33 @@
                 if next(stream, done) is done:
                     streams.remove(stream)
 
-    def emit(inner, total):
+    def emit(inner, total, unit):
         outer = (inner.astype(f32) + total).astype(bf16)
         for t in range(UNIT_TILES):
-            slot = table_ref[(step - 1) * UNIT_TILES + t]
+            slot = table_ref[unit * UNIT_TILES + t]
 
             @pl.when(slot >= 0)
             def _():
                 out_ref[jnp.maximum(slot, 0)] = outer[t * PART : (t + 1) * PART]
+
+    if whole_units:
+
+        @pl.when(step == 0)
+        def _():
+            for fetch in fetches:
+                fetch.start()
+
+        weave(attention_steps())
+
+        @pl.when(step == 0)
+        def _():
+            for fetch in fetches:
+                fetch.wait()
+
+        result = []
+        weave(forward_steps(mixed_ref[...], result))
+        emit(*result, step)
+        return
 
     @pl.when(step == 0)
     def _():
@@ -365,98 +387,126 @@
     @pl.when((step > 0) & (step < units))
     def _():
         result = []
-        weave(attention_steps(), forward_steps(mixed_ref[...], result), delay=0)
-        emit(*result)
+        weave(attention_steps(), forward_steps(mixed_ref[...], result))
+        emit(*result, step - 1)
 
     @pl.when(step == units)
     def _():
         result = []
         weave(forward_steps(mixed_ref[...], result))
-        emit(*result)
-
-
-def attention_kernel(place, masked, pieces, table_ref, x_ref, q_ref, *refs):
-    k_refs, refs = refs[:pieces], refs[pieces:]
-    v_refs, refs = refs[:pieces], refs[pieces:]
-    proj_ref, out_ref, mixed_ref, tiles_ref, sems = refs[0], *refs[-4:]
+        emit(*result, step - 1)
+
+
+def attention_kernel(place, masked, sets, pieces, table_ref, *refs):
+    x_refs, q_refs, refs = refs[:2], refs[2:4], refs[4:]
+    key_sets, refs = refs[: 2 * pieces * sets], refs[2 * pieces * sets :]
+    proj_ref, out_ref, token_ref, mixed_ref, tiles_ref, sems = refs[0], *refs[-5:]
+    token_ref[...] = jnp.zeros_like(token_ref)
     step = pl.program_id(0)
-    units = pl.num_programs(0)
+    steps = pl.num_programs(0)
     count = UNIT_TILES * PART
-    first_tile = place(step) * UNIT_TILES
-    scores, soften, mix = attention_parts(
-        masked, first_tile, table_ref, q_ref, k_refs, v_refs, mixed_ref
-    )
-    s = scores(0)
-    for h in range(HEADS):
-        later = scores(h + 1) if h + 1 < HEADS else None
-        mix(h, soften(s))
-        s = later
-    base = x_ref[...].reshape(count, D).astype(f32)
-    inner = (base + dot(mixed_ref[...], proj_ref[...])).astype(bf16)
-    tiles_ref[pl.ds(step * UNIT_TILES, UNIT_TILES)] = inner.reshape(UNIT_TILES, PART, D)
-
-    def copy_of(unit, t, act):
-        slot = table_ref[place(unit) * UNIT_TILES + t]
+    units = []
+    for n in range(2):
+        own = key_sets[2 * pieces * (n % sets) : 2 * pieces * (n % sets + 1)]
+        units.append(
+            attention_parts(
+                masked,
+                place(step, n) * UNIT_TILES,
+                table_ref,
+                q_refs[n],
+                own[:pieces],
+                own[pieces:],
+                mixed_ref.at[n],
+            )
+        )
+
+    def copy_of(at, n, t, act):
+        slot = table_ref[place(at, n) * UNIT_TILES + t]
 
         @pl.when(slot >= 0)
         def _():
-            i = unit * UNIT_TILES + t
+            i = (2 * at + n) * UNIT_TILES + t
             act(
                 pltpu.make_async_copy(
                     tiles_ref.at[i], out_ref.at[jnp.maximum(slot, 0)], sems.at[i]
                 )
             )
 
-    for t in range(UNIT_TILES):
-        copy_of(step, t, lambda copy: copy.start())
-
-    @pl.when(step == units - 1)
+    def join(n):
+        base = x_refs[n][...].reshape(count, D).astype(f32)
+        inner = (base + dot(mixed_ref[n], proj_ref[...])).astype(bf16)
+        tiles_ref[pl.ds((2 * step + n) * UNIT_TILES, UNIT_TILES)] = inner.reshape(
+            UNIT_TILES, PART, D
+        )
+
+    jobs = [(n, h) for n in range(2) for h in range(HEADS)]
+    s = units[0][0](0)
+    for i, (n, h) in enumerate(jobs):
+        later = None
+        if i + 1 < len(jobs):
+            after, head = jobs[i + 1]
+            later = units[after][0](head)
+        units[n][2](h, units[n][1](s))
+        s = later
+        if (n, h) == (1, 1):
+            join(0)
+    join(1)
+    for n in range(2):
+        for t in range(UNIT_TILES):
+            copy_of(step, n, t, lambda copy: copy.start())
+
+    @pl.when(step == steps - 1)
     def _():
-        @pl.loop(0, units)
-        def _(unit):
-            for t in range(UNIT_TILES):
-                copy_of(unit, t, lambda copy: copy.wait())
-
-
-def attention(name, table, x, q, keys, values, specs, units, place, masked, layer, proj, packed):
-    pieces = len(keys)
-    args = [table, x, q, *keys, *values, proj]
+        @pl.loop(0, steps)
+        def _(at):
+            for n in range(2):
+                for t in range(UNIT_TILES):
+                    copy_of(at, n, t, lambda copy: copy.wait())
+
+
+def attention(name, table, x, q, key_sets, specs, steps, place, masked, layer, proj, packed):
+    pieces = len(key_sets[0]) // 2
+    args = [table, x, x, q, q]
+    for one in key_sets:
+        args += one
+    args.append(proj)
     specs = [*specs, layer_of((D, D), layer)]
     aliases = {}
     if packed is not None:
         aliases = {len(args): 0}
         args.append(packed)
         specs.append(pl.BlockSpec(memory_space=pltpu.HBM))
+    tiles = 2 * steps * UNIT_TILES
     return pl.pallas_call(
-        functools.partial(attention_kernel, place, masked, pieces),
+        functools.partial(attention_kernel, place, masked, len(key_sets), pieces),
         grid_spec=pltpu.PrefetchScalarGridSpec(
             num_scalar_prefetch=1,
-            grid=(units,),
+            grid=(steps,),
             in_specs=specs,
-            out_specs=pl.BlockSpec(memory_space=pltpu.HBM),
+            out_specs=[pl.BlockSpec(memory_space=pltpu.HBM), whole((8, 128))],
             scratch_shapes=[
-                pltpu.VMEM((UNIT_TILES * PART, D), bf16),
-                pltpu.VMEM((units * UNIT_TILES, PART, D), bf16),
-                pltpu.SemaphoreType.DMA((units * UNIT_TILES,)),
+                pltpu.VMEM((2, UNIT_TILES * PART, D), bf16),
+                pltpu.VMEM((tiles, PART, D), bf16),
+                pltpu.SemaphoreType.DMA((tiles,)),
             ],
         ),
-        out_shape=pltpu.HBM((PEERS, PART, D), bf16),
+        out_shape=[pltpu.HBM((PEERS, PART, D), bf16), jax.ShapeDtypeStruct((8, 128), f32)],
         input_output_aliases=aliases,
         name=name,
     )(*args)
 
 
-def block(name, table, x, q, keys, values, specs, units, masked, layer, weights):
+def block(name, table, x, q, keys, values, specs, units, masked, whole_units, layer, weights, token):
     gains, *matrices = weights
     pieces = len(keys)
     count = UNIT_TILES * PART
     return pl.pallas_call(
-        functools.partial(block_kernel, units, masked, layer, pieces),
+        functools.partial(block_kernel, units, masked, whole_units, layer, pieces),
         grid_spec=pltpu.PrefetchScalarGridSpec(
             num_scalar_prefetch=1,
-            grid=(units + 1,),
+            grid=(units if whole_units else units + 1,),
             in_specs=specs
-            + [whole((4, D))]
+            + [whole((4, D)), whole((8, 128))]
             + [pl.BlockSpec(memory_space=pl.ANY)] * len(matrices),
             out_specs=whole((PEERS, PART, D)),
             scratch_shapes=[
@@ -468,8 +518,9 @@
             ],
         ),
         out_shape=jax.ShapeDtypeStruct((PEERS, PART, D), bf16),
+        compiler_params=pltpu.CompilerParams(vmem_limit_bytes=FULL_VMEM),
         name=name,
-    )(table, x, q, *keys, *values, gains, *matrices)
+    )(table, x, q, *keys, *values, gains, token, *matrices)
 
 
 def specs_a(chunk, x_place, place):
@@ -493,18 +544,27 @@
     ]
 
 
-def attention_a(name, chunk, place, table, x, q, keys, values, proj, packed):
-    specs = specs_a(chunk, place, place)
+def attention_a(name, chunk, places, table, x, q, keys, values, proj, packed):
+    first, second = [specs_a(chunk, lambda i, n=n: n, lambda i, n=n: n) for n in places]
+    shared = (places[0] + 1) // 2 == (places[1] + 1) // 2
+    key_sets = [[keys, keys, values, values]] * (1 if shared else 2)
+    specs = [first[0], second[0], first[1], second[1], *first[2:]]
+    if not shared:
+        specs += second[2:]
+
+    def place(i, n):
+        return places[n]
+
     return attention(
-        name, table, x, q, [keys] * 2, [values] * 2, specs, 2, place, False, 0, proj, packed
+        name, table, x, q, key_sets, specs, 1, place, False, 0, proj, packed
     )
 
 
-def block_a(chunk, table, x, q, keys, values, weights):
+def block_a(chunk, table, x, q, keys, values, weights, token):
     units = TILES_DEV // UNIT_TILES
-    specs = specs_a(chunk, prior, lambda i: now(i, units))
+    specs = specs_a(chunk, lambda i: i, lambda i: i)
     return block(
-        "block_a", table, x, q, [keys] * 2, [values] * 2, specs, units, False, 0, weights
+        "block_a", table, x, q, [keys] * 2, [values] * 2, specs, units, False, True, 0, weights, token
     )
 
 
@@ -519,30 +579,40 @@
 
 
 def attention_b(table, x, q, keys, values, proj):
-    units = SLOTS // UNIT_TILES
-
-    def place(i):
-        return i
-
-    specs = specs_b(place, place)
+    def place(i, n):
+        return 2 * i + n
+
+    first, second = [specs_b(lambda i, n=n: place(i, n), lambda i, n=n: place(i, n)) for n in (0, 1)]
+    specs = [first[0], second[0], first[1], second[1], *first[2:]]
     return attention(
-        "attention_b", table, x, q, keys, values, specs, units, place, True, 1, proj, None
+        "attention_b",
+        table,
+        x,
+        q,
+        [[*keys, *values]],
+        specs,
+        SLOTS // PATCH_TILES,
+        place,
+        True,
+        1,
+        proj,
+        None,
     )
 
 
-def block_b(table, x, q, keys, values, weights):
+def block_b(table, x, q, keys, values, weights, token):
     units = SLOTS // UNIT_TILES
     specs = specs_b(prior, lambda i: now(i, units))
     return block(
-        "block_b", table, x, q, keys, values, specs, units, True, 1, weights
+        "block_b", table, x, q, keys, values, specs, units, True, False, 1, weights, token
     )
 
 
-def forward_home_kernel(table_ref, part_ref, gains_ref, up_ref, down_ref, out_ref):
-    step = pl.program_id(0)
-    tiles = [part_ref[table_ref[step * UNIT_TILES + t]] for t in range(UNIT_TILES)]
-    rows = jnp.concatenate(tiles, axis=0)
-    normed = norm_rows(rows.astype(f32), gains_ref[3:4, :])
+def forward_home_kernel(table_ref, *refs):
+    part_refs, refs = refs[:UNIT_TILES], refs[UNIT_TILES:]
+    gains_ref, up_ref, down_ref, out_ref = refs
+    rows = live_rows(table_ref, pl.program_id(0), part_refs)
+    normed = norm_rows(rows, gains_ref[3:4, :])
     out_ref[...] = forward_rows(rows, normed, up_ref, down_ref).reshape(UNIT_TILES, PART, D)
 
 
@@ -553,40 +623,53 @@
         grid_spec=pltpu.PrefetchScalarGridSpec(
             num_scalar_prefetch=1,
             grid=(TILES_DEV // UNIT_TILES,),
-            in_specs=[
-                pl.BlockSpec(memory_space=pltpu.VMEM),
-                whole((4, D)),
-                layer_of((D, FF), 1),
-                layer_of((FF, D), 1),
-            ],
+            in_specs=gather_specs(UNIT_TILES)
+            + [whole((4, D)), layer_of((D, FF), 1), layer_of((FF, D), 1)],
             out_specs=pl.BlockSpec((UNIT_TILES, PART, D), lambda i, *_: (i, 0, 0)),
         ),
         out_shape=pltpu.HBM((TILES_DEV, TILE, D), bf16),
-        compiler_params=pltpu.CompilerParams(vmem_limit_bytes=30 << 20),
+        compiler_params=pltpu.CompilerParams(vmem_limit_bytes=FULL_VMEM),
         name="forward_home",
-    )(table, part, gains, up_weight, down_weight)
-
-
-def home_kernel(table_ref, part_ref, done_in, out_ref):
-    for t in range(TILES_DEV):
-        out_ref[t] = part_ref[table_ref[t]]
+    )(table, *[part] * UNIT_TILES, gains, up_weight, down_weight)
+
+
+def home_kernel(table_ref, part_ref, done_in, out_ref, tiles_ref, in_sems, out_sems):
+    arriving = [
+        pltpu.make_async_copy(part_ref.at[table_ref[t]], tiles_ref.at[t], in_sems.at[t])
+        for t in range(TILES_DEV)
+    ]
+    leaving = [
+        pltpu.make_async_copy(
+            tiles_ref.at[t], out_ref.at[t, pl.ds(PART, PART)], out_sems.at[t]
+        )
+        for t in range(TILES_DEV)
+    ]
+    for copy in arriving:
+        copy.start()
+    for copy, onward in zip(arriving, leaving):
+        copy.wait()
+        onward.start()
+    for onward in leaving:
+        onward.wait()
 
 
 def home(table, part, done):
+    hbm = pl.BlockSpec(memory_space=pltpu.HBM)
     return pl.pallas_call(
         home_kernel,
         grid_spec=pltpu.PrefetchScalarGridSpec(
             num_scalar_prefetch=1,
             grid=(1,),
-            in_specs=[
-                pl.BlockSpec(memory_space=pltpu.VMEM),
-                pl.BlockSpec(memory_space=pltpu.HBM),
+            in_specs=[hbm, hbm],
+            out_specs=hbm,
+            scratch_shapes=[
+                pltpu.VMEM((TILES_DEV, PART, D), bf16),
+                pltpu.SemaphoreType.DMA((TILES_DEV,)),
+                pltpu.SemaphoreType.DMA((TILES_DEV,)),
             ],
-            out_specs=pl.BlockSpec((TILES_DEV, PART, D), lambda i, *_: (0, 1, 0)),
         ),
         out_shape=pltpu.HBM((TILES_DEV, TILE, D), bf16),
         input_output_aliases={2: 0},
-        compiler_params=pltpu.CompilerParams(vmem_limit_bytes=12 << 20),
         name="home",
     )(table, part, done)
 
@@ -608,24 +691,23 @@
     x = points.reshape(tiled)
     q, keys, values = qkv_own(points, norm_gains, qkv_weight)
     q = q.reshape(tiled)
-    packed = attention_a(
-        "attention_a_middle", 0, lambda i: i + 1, dest_slot, x, q, keys, values, proj_weight, None
+    packed, token = attention_a(
+        "attention_a_middle", 0, (1, 2), dest_slot, x, q, keys, values, proj_weight, None
     )
-    keys, values = qkv_halo(before, after, norm_gains, qkv_weight, keys, values, packed)
-    packed = attention_a(
-        "attention_a_edges", 0, lambda i: 3 * i, dest_slot, x, q, keys, values, proj_weight, packed
+    keys, values = qkv_halo(before, after, norm_gains, qkv_weight, keys, values, token)
+    packed, token = attention_a(
+        "attention_a_edges", 0, (0, 3), dest_slot, x, q, keys, values, proj_weight, packed
     )
     early = exchange(packed)
-    late = exchange(block_a(1, dest_slot, x, q, keys, values, weights))
+    late = exchange(block_a(1, dest_slot, x, q, keys, values, weights, token))
     owned = [
         forward_owner(owner_from, early, weights, qkv_weight),
         qkv_owner(owner_from, late, norm_gains, qkv_weight),
     ]
     xs, qs, owner_keys, owner_values = zip(*owned)
-    early = exchange(
-        attention_b(owner_from, xs[0], qs[0], owner_keys, owner_values, proj_weight)
-    )
-    late = exchange(block_b(owner_from, xs[1], qs[1], owner_keys, owner_values, weights))
+    packed, token = attention_b(owner_from, xs[0], qs[0], owner_keys, owner_values, proj_weight)
+    early = exchange(packed)
+    late = exchange(block_b(owner_from, xs[1], qs[1], owner_keys, owner_values, weights, token))
     done = forward_home(dest_slot, early, weights)
     return home(dest_slot, late, done).reshape(rows, D)
 

time: 182 us -> 180 us (0.989)
  local copies, waits for them, and re-layouts: 8.91 us -> 1.87 us
  Pallas kernels: 112 us -> 116 us
    unnamed x26 -> x6, local copies, waits for them, and re-layouts: 7.72 us -> 0.67 us
  transfers between devices with their start and end apart: 6 -> 6, of which waited for: 4 -> 4; matrix products, arithmetic and copies ran while one was open for 0% -> 0% of each run, Pallas kernels for 42% -> 45%
where the time goes in v6:
time: 180 us; the launch traced here: 177 us
  Pallas kernels  116 us (64%)
  starting transfers between devices  29.7 us (16%)
  waiting for transfers between devices  29.5 us (16%)
  local copies, waits for them, and re-layouts  1.87 us (1%)
    pallas_call x2, Pallas kernels, block(): pl.pallas_call(functools.partial(block_kernel, units, masked, whole_units...  42 us
    pallas_call x3, Pallas kernels, attention(): pl.pallas_call(functools.partial(attention_kernel, place, masked, len(key...  32.6 us
    all_to_all x4, waiting for transfers between devices, exchange(): lax.all_to_all(part, 'chain', split_axis=0, concat_axis=0, tiled=True)  29.5 us
    all_to_all x4, starting transfers between devices, exchange(): lax.all_to_all(part, 'chain', split_axis=0, concat_axis=0, tiled=True)  21.4 us
    pallas_call x1, Pallas kernels, forward_owner(): pl.pallas_call(forward_owner_kernel, grid_spec=pltpu.PrefetchScalarGridSp...  15.4 us
    pallas_call x1, Pallas kernels, forward_home(): pl.pallas_call(forward_home_kernel, grid_spec=pltpu.PrefetchScalarGridSpe...  8.41 us
    ppermute x1, starting transfers between devices, body(): lax.ppermute(points[:HALF], axes, [((i + 1) % ring, i) for i in range(rin...  8.31 us
    pallas_call x1, Pallas kernels, qkv_owner(): pl.pallas_call(qkv_owner_kernel, grid_spec=pltpu.PrefetchScalarGridSpec(n...  6.24 us
  transfers between devices with their start and end apart: 6, of which 4 were waited for; matrix products, arithmetic and copies ran while one was open for 0% of the time, Pallas kernels for 45%

profile of v6, /device:TPU:0, one launch (start us, length us, event | category | flops | bytes accessed | tf_op | source)
XLA Modules:
  0.0 177.2 jit_solution(13313396077879486284)
XLA Ops:
  0.0 1.2 fusion
  1.2 8.3 %collective-permute-start.1 = (bf16[512,384]{1,0:T(8,128)(2,1)S(1)}, bf16[512,384]{1,0:T(8,128)(2,1)S(1)}, u32[]{:S(2)}, u32[]{:S(2)}) collective-permute-start(bf16[512,384]{1,0:T(8,128)(2,1)S(1)} %get-tuple-element.43), channel_id=1, source_target_pairs={{1,0},{2,1},{3,2},{4,3},{5,4},{6,5},{7,6},{8,7},{9,8},{10,9},{11,1... | collective-permute-start | bytes 1179656 | tf_op jit(solution)/shard_map/ppermute | solution.py:688
  9.5 0.0 collective-permute-start
  9.5 6.0 %qkv_own.1 = (bf16[2048,384]{1,0:T(8,128)(2,1)}, bf16[3072,384]{1,0:T(8,128)(2,1)}, bf16[3072,384]{1,0:T(8,128)(2,1)}) custom-call(bf16[2048,384]{1,0:T(8,128)(2,1)} %x_ref.1, f32[4,384]{1,0:T(4,128)} %refs_4_.7, bf16[2,384,1152]{2,1,0:T(8,128)(2,1)} %refs_7_.4), custom_call_target="tpu_custom_call" | custom-call | tf_op jit(solution)/shard_map/qkv_own/pallas_call | solution.py:94
  15.5 0.0 copy-start
  15.5 0.0 copy-start.1
  15.5 8.1 %attention_a_middle.1 = (bf16[32,64,384]{2,1,0:T(8,128)(2,1)}, f32[8,128]{1,0:T(8,128)}) custom-call(s32[16]{0:T(128)} %table_ref.13, bf16[16,128,384]{2,1,0:T(8,128)(2,1)} %bitcast.3, bf16[16,128,384]{2,1,0:T(8,128)(2,1)} %bitcast.4, bf16[16,128,384]{2,1,0:T(8,128)(2,1)} %bitcast.8, bf16[16,128,384]{2,1,0:T(8,128)(2,1)} %bitcast.9, ...), custom_call_target="tpu_custom_call" | custom-call | tf_op jit(solution)/shard_map/attention_a_middle/pallas_call | solution.py:480
  23.6 0.0 collective-permute-done.1.b_ref
  23.6 0.0 collective-permute-done.a_ref
  23.6 0.0 copy-done
  23.6 0.0 copy-done.1
  23.6 0.0 copy-start.2
  23.6 0.7 copy-done.2
  24.3 2.4 %qkv_halo.1 = (bf16[3072,384]{1,0:T(8,128)(2,1)}, bf16[3072,384]{1,0:T(8,128)(2,1)}) custom-call(bf16[512,384]{1,0:T(8,128)(2,1)S(1)} %collective-permute-done.a_ref, bf16[512,384]{1,0:T(8,128)(2,1)S(1)} %collective-permute-done.1.b_ref, f32[4,384]{1,0:T(4,128)S(1)} %copy-done.1, ...), custom_call_target="tpu_custom_call", output_to_operand_aliasing={{0}: (4, {}), {1}: (5, {})} | custom-call | tf_op jit(solution)/shard_map/qkv_halo/pallas_call | solution.py:120
  26.7 8.5 %attention_a_edges.1 = (bf16[32,64,384]{2,1,0:T(8,128)(2,1)}, f32[8,128]{1,0:T(8,128)}) custom-call(s32[16]{0:T(128)} %table_ref.13, bf16[16,128,384]{2,1,0:T(8,128)(2,1)} %bitcast.5, bf16[16,128,384]{2,1,0:T(8,128)(2,1)} %bitcast.6, bf16[16,128,384]{2,1,0:T(8,128)(2,1)} %bitcast.10, ...), custom_call_target="tpu_custom_call", output_to_operand_aliasing={{0}: (14, {})} | custom-call | tf_op jit(solution)/shard_map/attention_a_edges/pallas_call | solution.py:480
  35.2 4.9 %all-to-all-start.1 = ((bf16[32,64,384]{2,1,0:T(8,128)(2,1)}), bf16[32,64,384]{2,1,0:T(8,128)(2,1)}, u32[]{:S(2)}, u32[]{:S(2)}) async-start(bf16[32,64,384]{2,1,0:T(8,128)(2,1)} %get-tuple-element.34), calls=%async_computation.1 | async-start | bytes 3145728 | tf_op jit(solution)/shard_map/all_to_all | solution.py:678
  40.1 18.8 %block_a.1 = bf16[32,64,384]{2,1,0:T(8,128)(2,1)} custom-call(s32[16]{0:T(128)} %table_ref.13, bf16[16,128,384]{2,1,0:T(8,128)(2,1)} %bitcast.7, bf16[16,128,384]{2,1,0:T(8,128)(2,1)} %bitcast.12, bf16[3072,384]{1,0:T(8,128)(2,1)} %get-tuple-element.28.refs_4_.refs_5_.refs_8_.refs_9_.refs_0_.refs_1_, ...), custom_call_target="tpu_custom_call" | custom-call | tf_op jit(solution)/shard_map/block_a/pallas_call | solution.py:503
  58.9 5.1 %all-to-all-done.1.refs_0_.refs_1_.refs_2_.refs_3_ = bf16[32,64,384]{2,1,0:T(8,128)(2,1)} async-done(((bf16[32,64,384]{2,1,0:T(8,128)(2,1)}), bf16[32,64,384]{2,1,0:T(8,128)(2,1)}, u32[]{:S(2)}, u32[]{:S(2)}) %all-to-all-start.1) | async-done | bytes 1572896 | tf_op jit(solution)/shard_map/all_to_all | solution.py:678
  64.0 4.7 %all-to-all-start = ((bf16[32,64,384]{2,1,0:T(8,128)(2,1)}), bf16[32,64,384]{2,1,0:T(8,128)(2,1)}, u32[]{:S(2)}, u32[]{:S(2)}) async-start(bf16[32,64,384]{2,1,0:T(8,128)(2,1)} %block_a.1), calls=%async_computation | async-start | bytes 3145728 | tf_op jit(solution)/shard_map/all_to_all | solution.py:678
  68.7 15.4 %forward_owner.1 = (bf16[24,64,384]{2,1,0:T(8,128)(2,1)}, bf16[24,64,384]{2,1,0:T(8,128)(2,1)}, bf16[24,64,384]{2,1,0:T(8,128)(2,1)}, bf16[24,64,384]{2,1,0:T(8,128)(2,1)}) custom-call(s32[24]{0:T(128)} %table_ref.11, bf16[32,64,384]{2,1,0:T(8,128)(2,1)} %all-to-all-done.1.refs_0_.refs_1_.refs_2_.refs_3_, ...), custom_call_target="tpu_custom_call" | custom-call | tf_op jit(solution)/shard_map/forward_owner/pallas_call | solution.py:214
  84.1 8.5 %all-to-all-done.refs_0_.refs_1_.refs_2_.refs_3_.refs_4_.refs_5_.refs_6_.refs_7_ = bf16[32,64,384]{2,1,0:T(8,128)(2,1)} async-done(((bf16[32,64,384]{2,1,0:T(8,128)(2,1)}), bf16[32,64,384]{2,1,0:T(8,128)(2,1)}, u32[]{:S(2)}, u32[]{:S(2)}) %all-to-all-start) | async-done | bytes 1572896 | tf_op jit(solution)/shard_map/all_to_all | solution.py:678
  92.6 6.2 %qkv_owner.1 = (bf16[24,64,384]{2,1,0:T(8,128)(2,1)}, bf16[24,64,384]{2,1,0:T(8,128)(2,1)}, bf16[24,64,384]{2,1,0:T(8,128)(2,1)}, bf16[24,64,384]{2,1,0:T(8,128)(2,1)}) custom-call(s32[24]{0:T(128)} %table_ref.11, bf16[32,64,384]{2,1,0:T(8,128)(2,1)} %all-to-all-done.refs_0_.refs_1_.refs_2_.refs_3_.refs_4_.refs_5_.refs_6_.refs_7_, ...), custom_call_target="tpu_custom_call" | custom-call | tf_op jit(solution)/shard_map/qkv_owner/pallas_call | solution.py:171
  98.8 16.1 %attention_b.1 = (bf16[32,64,384]{2,1,0:T(8,128)(2,1)}, f32[8,128]{1,0:T(8,128)}) custom-call(s32[24]{0:T(128)} %table_ref.11, bf16[24,64,384]{2,1,0:T(8,128)(2,1)} %get-tuple-element.39.refs_0_.refs_1_, bf16[24,64,384]{2,1,0:T(8,128)(2,1)} %get-tuple-element.39.refs_0_.refs_1_, bf16[24,64,384]{2,1,0:T(8,128)(2,1)} %get-tuple-element.40.refs_2_.refs_3_, ...), custom_call_target="tpu_custom_call" | custom-call | tf_op jit(solution)/shard_map/attention_b/pallas_call | solution.py:480
  114.9 4.9 %all-to-all-start.3 = ((bf16[32,64,384]{2,1,0:T(8,128)(2,1)}), bf16[32,64,384]{2,1,0:T(8,128)(2,1)}, u32[]{:S(2)}, u32[]{:S(2)}) async-start(bf16[32,64,384]{2,1,0:T(8,128)(2,1)} %get-tuple-element.42), calls=%async_computation.3 | async-start | bytes 3145728 | tf_op jit(solution)/shard_map/all_to_all | solution.py:678
  119.9 23.2 %block_b.1 = bf16[32,64,384]{2,1,0:T(8,128)(2,1)} custom-call(s32[24]{0:T(128)} %table_ref.11, bf16[24,64,384]{2,1,0:T(8,128)(2,1)} %get-tuple-element.32.x_ref, bf16[24,64,384]{2,1,0:T(8,128)(2,1)} %get-tuple-element.33.q_ref, bf16[24,64,384]{2,1,0:T(8,128)(2,1)} %get-tuple-element.35.refs_4_.refs_0_, ...), custom_call_target="tpu_custom_call" | custom-call | tf_op jit(solution)/shard_map/block_b/pallas_call | solution.py:503
  143.1 0.4 all-to-all-done.3.refs_0_.refs_1_.refs_2_.refs_3_
  143.5 6.9 %all-to-all-start.2 = ((bf16[32,64,384]{2,1,0:T(8,128)(2,1)}), bf16[32,64,384]{2,1,0:T(8,128)(2,1)}, u32[]{:S(2)}, u32[]{:S(2)}) async-start(bf16[32,64,384]{2,1,0:T(8,128)(2,1)} %block_b.1), calls=%async_computation.2 | async-start | bytes 3145728 | tf_op jit(solution)/shard_map/all_to_all | solution.py:678
  150.4 8.4 %forward_home.1.done_in = bf16[16,128,384]{2,1,0:T(8,128)(2,1)} custom-call(s32[16]{0:T(128)} %table_ref.13, bf16[32,64,384]{2,1,0:T(8,128)(2,1)} %all-to-all-done.3.refs_0_.refs_1_.refs_2_.refs_3_, bf16[32,64,384]{2,1,0:T(8,128)(2,1)} %all-to-all-done.3.refs_0_.refs_1_.refs_2_.refs_3_, bf16[32,64,384]{2,1,0:T(8,128)(2,1)} %all-to-all-done.3.refs_0_.refs_1_.refs_2_.refs_3_, ...), custom_call_target="tpu_custom_call" | custom-call | tf_op jit(solution)/shard_map/forward_home/pallas_call | solution.py:621
  158.9 15.5 %all-to-all-done.2.part_ref = bf16[32,64,384]{2,1,0:T(8,128)(2,1)} async-done(((bf16[32,64,384]{2,1,0:T(8,128)(2,1)}), bf16[32,64,384]{2,1,0:T(8,128)(2,1)}, u32[]{:S(2)}, u32[]{:S(2)}) %all-to-all-start.2) | async-done | bytes 1572896 | tf_op jit(solution)/shard_map/all_to_all | solution.py:678
  174.3 2.7 %home.1 = bf16[16,128,384]{2,1,0:T(8,128)(2,1)} custom-call(s32[16]{0:T(128)} %table_ref.13, bf16[32,64,384]{2,1,0:T(8,128)(2,1)} %all-to-all-done.2.part_ref, bf16[16,128,384]{2,1,0:T(8,128)(2,1)} %forward_home.1.done_in), custom_call_target="tpu_custom_call", output_to_operand_aliasing={{}: (2, {})} | custom-call | tf_op jit(solution)/shard_map/home/pallas_call | solution.py:658
Async XLA Ops:
  1.2 22.4 %collective-permute-start.1 = (bf16[512,384]{1,0:T(8,128)(2,1)S(1)}, bf16[512,384]{1,0:T(8,128)(2,1)S(1)}, u32[]{:S(2)}, u32[]{:S(2)}) collective-permute-start(bf16[512,384]{1,0:T(8,128)(2,1)S(1)} %get-tuple-element.43), channel_id=1, source_target_pairs={{1,0},{2,1},{3,2},{4,3},{5,4},{6,5},{7,6},{8,7},{9,8},{10,9},{11,1... | collective-permute-start | bytes 1179656 | tf_op jit(solution)/shard_map/ppermute | solution.py:688
  9.5 14.1 %collective-permute-start = (bf16[512,384]{1,0:T(8,128)(2,1)S(1)}, bf16[512,384]{1,0:T(8,128)(2,1)S(1)}, u32[]{:S(2)}, u32[]{:S(2)}) collective-permute-start(bf16[512,384]{1,0:T(8,128)(2,1)S(1)} %get-tuple-element.44), channel_id=1, source_target_pairs={{0,1},{1,2},{2,3},{3,4},{4,5},{5,6},{6,7},{7,8},{8,9},{9,10},{10,1... | collective-permute-start | bytes 1179656 | tf_op jit(solution)/shard_map/ppermute | solution.py:687
  15.5 8.1 %copy-start = (bf16[2,384,1152]{2,1,0:T(8,128)(2,1)S(1)}, bf16[2,384,1152]{2,1,0:T(8,128)(2,1)}, u32[]{:S(2)}) copy-start(bf16[2,384,1152]{2,1,0:T(8,128)(2,1)} %refs_7_.4) | copy-start | bytes 5308420
  15.5 8.1 %copy-start.1 = (f32[4,384]{1,0:T(4,128)S(1)}, f32[4,384]{1,0:T(4,128)}, u32[]{:S(2)}) copy-start(f32[4,384]{1,0:T(4,128)} %refs_4_.7) | copy-start | bytes 18436
  23.6 0.7 copy-start.2
  35.2 28.8 %all-to-all-start.1 = ((bf16[32,64,384]{2,1,0:T(8,128)(2,1)}), bf16[32,64,384]{2,1,0:T(8,128)(2,1)}, u32[]{:S(2)}, u32[]{:S(2)}) async-start(bf16[32,64,384]{2,1,0:T(8,128)(2,1)} %get-tuple-element.34), calls=%async_computation.1 | async-start | bytes 3145728 | tf_op jit(solution)/shard_map/all_to_all | solution.py:678
  64.0 28.6 %all-to-all-start = ((bf16[32,64,384]{2,1,0:T(8,128)(2,1)}), bf16[32,64,384]{2,1,0:T(8,128)(2,1)}, u32[]{:S(2)}, u32[]{:S(2)}) async-start(bf16[32,64,384]{2,1,0:T(8,128)(2,1)} %block_a.1), calls=%async_computation | async-start | bytes 3145728 | tf_op jit(solution)/shard_map/all_to_all | solution.py:678
  114.9 28.6 %all-to-all-start.3 = ((bf16[32,64,384]{2,1,0:T(8,128)(2,1)}), bf16[32,64,384]{2,1,0:T(8,128)(2,1)}, u32[]{:S(2)}, u32[]{:S(2)}) async-start(bf16[32,64,384]{2,1,0:T(8,128)(2,1)} %get-tuple-element.42), calls=%async_computation.3 | async-start | bytes 3145728 | tf_op jit(solution)/shard_map/all_to_all | solution.py:678
  143.5 30.8 %all-to-all-start.2 = ((bf16[32,64,384]{2,1,0:T(8,128)(2,1)}), bf16[32,64,384]{2,1,0:T(8,128)(2,1)}, u32[]{:S(2)}, u32[]{:S(2)}) async-start(bf16[32,64,384]{2,1,0:T(8,128)(2,1)} %block_b.1), calls=%async_computation.2 | async-start | bytes 3145728 | tf_op jit(solution)/shard_map/all_to_all | solution.py:678

commit v7 on v6

--- a/solution.py
+++ b/solution.py
@@ -137,10 +137,11 @@
     )(before, after, gains, qkv_weight, keys, values, earlier)
 
 
-def gather_specs(count):
+def gather_specs(count, repeat=1):
     def spec(t):
         return pl.BlockSpec(
-            (None, PART, D), lambda i, table: (jnp.maximum(table[i * count + t], 0), 0, 0)
+            (None, PART, D),
+            lambda i, table: (jnp.maximum(table[i // repeat * count + t], 0), 0, 0),
         )
 
     return [spec(t) for t in range(count)]
@@ -152,33 +153,6 @@
         live = table_ref[step * len(tile_refs) + t] >= 0
         tiles.append(jnp.where(live, tile_ref[...].astype(f32), 0.0))
     return jnp.concatenate(tiles, axis=0)
-
-
-def qkv_owner_kernel(from_ref, *refs):
-    part_refs, refs = refs[:PATCH_TILES], refs[PATCH_TILES:]
-    gains_ref, w_ref, x_ref, q_ref, k_ref, v_ref = refs
-    shape = (PATCH_TILES, PART, D)
-    rows = live_rows(from_ref, pl.program_id(0), part_refs)
-    x_ref[...] = rows.astype(bf16).reshape(shape)
-    out = dot(norm_rows(rows, gains_ref[2:3, :]), w_ref[...])
-    q_ref[...] = (out[:, :D] * query_scale).astype(bf16).reshape(shape)
-    k_ref[...] = out[:, D : 2 * D].astype(bf16).reshape(shape)
-    v_ref[...] = out[:, 2 * D :].astype(bf16).reshape(shape)
-
-
-def qkv_owner(owner_from, part, gains, qkv_weight):
-    block = pl.BlockSpec((PATCH_TILES, PART, D), lambda i, *_: (i, 0, 0))
-    return pl.pallas_call(
-        qkv_owner_kernel,
-        grid_spec=pltpu.PrefetchScalarGridSpec(
-            num_scalar_prefetch=1,
-            grid=(SLOTS // PATCH_TILES,),
-            in_specs=gather_specs(PATCH_TILES) + [whole((4, D)), layer_of((D, 3 * D), 1)],
-            out_specs=[block] * 4,
-        ),
-        out_shape=[pltpu.HBM((SLOTS, PART, D), bf16)] * 4,
-        name="qkv_owner",
-    )(owner_from, *[part] * PATCH_TILES, gains, qkv_weight)
 
 
 def forward_rows(inner, normed, up_ref, down_ref):
@@ -397,100 +371,95 @@
         emit(*result, step - 1)
 
 
-def attention_kernel(place, masked, sets, pieces, table_ref, *refs):
-    x_refs, q_refs, refs = refs[:2], refs[2:4], refs[4:]
-    key_sets, refs = refs[: 2 * pieces * sets], refs[2 * pieces * sets :]
-    proj_ref, out_ref, token_ref, mixed_ref, tiles_ref, sems = refs[0], *refs[-5:]
+def attention_kernel(place, masked, arriving, table_ref, x_ref, q_ref, k_ref, *refs):
+    if arriving:
+        v_ref, *refs = refs
+        part_refs, refs = refs[:PATCH_TILES], refs[PATCH_TILES:]
+        gains_ref, w_ref, proj_ref, *refs = refs
+        out_ref, token_ref, x1_ref, q1_ref, k1_ref, v1_ref, mixed_ref, tiles_ref, sems = refs
+        k_refs, v_refs = [k_ref, k1_ref], [v_ref, v1_ref]
+    else:
+        k_refs, v_refs = [k_ref, refs[0]], refs[1:3]
+        proj_ref = refs[3]
+        out_ref, token_ref, mixed_ref, tiles_ref, sems = refs[-5:]
     token_ref[...] = jnp.zeros_like(token_ref)
     step = pl.program_id(0)
-    steps = pl.num_programs(0)
+    units = pl.num_programs(0)
     count = UNIT_TILES * PART
-    units = []
-    for n in range(2):
-        own = key_sets[2 * pieces * (n % sets) : 2 * pieces * (n % sets + 1)]
-        units.append(
-            attention_parts(
-                masked,
-                place(step, n) * UNIT_TILES,
-                table_ref,
-                q_refs[n],
-                own[:pieces],
-                own[pieces:],
-                mixed_ref.at[n],
-            )
-        )
-
-    def copy_of(at, n, t, act):
-        slot = table_ref[place(at, n) * UNIT_TILES + t]
+
+    if arriving:
+
+        @pl.when(step % 2 == 0)
+        def _():
+            shape = (PATCH_TILES, PART, D)
+            rows = live_rows(table_ref, step // 2, part_refs)
+            x1_ref[...] = rows.astype(bf16).reshape(shape)
+            out = dot(norm_rows(rows, gains_ref[2:3, :]), w_ref[...])
+            q1_ref[...] = (out[:, :D] * query_scale).astype(bf16).reshape(shape)
+            k1_ref[...] = out[:, D : 2 * D].astype(bf16).reshape(shape)
+            v1_ref[...] = out[:, 2 * D :].astype(bf16).reshape(shape)
+
+    scores, soften, mix = attention_parts(
+        masked, place(step) * UNIT_TILES, table_ref, q_ref, k_refs, v_refs, mixed_ref
+    )
+    s = scores(0)
+    for h in range(HEADS):
+        later = scores(h + 1) if h + 1 < HEADS else None
+        mix(h, soften(s))
+        s = later
+    base = x_ref[...].reshape(count, D).astype(f32)
+    inner = (base + dot(mixed_ref[...], proj_ref[...])).astype(bf16)
+    tiles_ref[pl.ds(step * UNIT_TILES, UNIT_TILES)] = inner.reshape(UNIT_TILES, PART, D)
+
+    def copy_of(unit, t, act):
+        slot = table_ref[place(unit) * UNIT_TILES + t]
 
         @pl.when(slot >= 0)
         def _():
-            i = (2 * at + n) * UNIT_TILES + t
+            i = unit * UNIT_TILES + t
             act(
                 pltpu.make_async_copy(
                     tiles_ref.at[i], out_ref.at[jnp.maximum(slot, 0)], sems.at[i]
                 )
             )
 
-    def join(n):
-        base = x_refs[n][...].reshape(count, D).astype(f32)
-        inner = (base + dot(mixed_ref[n], proj_ref[...])).astype(bf16)
-        tiles_ref[pl.ds((2 * step + n) * UNIT_TILES, UNIT_TILES)] = inner.reshape(
-            UNIT_TILES, PART, D
-        )
-
-    jobs = [(n, h) for n in range(2) for h in range(HEADS)]
-    s = units[0][0](0)
-    for i, (n, h) in enumerate(jobs):
-        later = None
-        if i + 1 < len(jobs):
-            after, head = jobs[i + 1]
-            later = units[after][0](head)
-        units[n][2](h, units[n][1](s))
-        s = later
-        if (n, h) == (1, 1):
-            join(0)
-    join(1)
-    for n in range(2):
-        for t in range(UNIT_TILES):
-            copy_of(step, n, t, lambda copy: copy.start())
-
-    @pl.when(step == steps - 1)
+    for t in range(UNIT_TILES):
+        copy_of(step, t, lambda copy: copy.start())
+
+    @pl.when(step == units - 1)
     def _():
-        @pl.loop(0, steps)
-        def _(at):
-            for n in range(2):
-                for t in range(UNIT_TILES):
-                    copy_of(at, n, t, lambda copy: copy.wait())
-
-
-def attention(name, table, x, q, key_sets, specs, steps, place, masked, layer, proj, packed):
-    pieces = len(key_sets[0]) // 2
-    args = [table, x, x, q, q]
-    for one in key_sets:
-        args += one
-    args.append(proj)
-    specs = [*specs, layer_of((D, D), layer)]
+        @pl.loop(0, units)
+        def _(unit):
+            for t in range(UNIT_TILES):
+                copy_of(unit, t, lambda copy: copy.wait())
+
+
+def attention(name, args, specs, units, place, masked, arriving, packed):
+    hbm = pl.BlockSpec(memory_space=pltpu.HBM)
     aliases = {}
     if packed is not None:
         aliases = {len(args): 0}
-        args.append(packed)
-        specs.append(pl.BlockSpec(memory_space=pltpu.HBM))
-    tiles = 2 * steps * UNIT_TILES
+        args = [*args, packed]
+        specs = [*specs, hbm]
+    out_specs = [hbm, whole((8, 128))]
+    out_shape = [pltpu.HBM((PEERS, PART, D), bf16), jax.ShapeDtypeStruct((8, 128), f32)]
+    if arriving:
+        out_specs += [pl.BlockSpec((PATCH_TILES, PART, D), lambda i, *_: (i // 2, 0, 0))] * 4
+        out_shape += [pltpu.HBM((SLOTS, PART, D), bf16)] * 4
     return pl.pallas_call(
-        functools.partial(attention_kernel, place, masked, len(key_sets), pieces),
+        functools.partial(attention_kernel, place, masked, arriving),
         grid_spec=pltpu.PrefetchScalarGridSpec(
             num_scalar_prefetch=1,
-            grid=(steps,),
+            grid=(units,),
             in_specs=specs,
-            out_specs=[pl.BlockSpec(memory_space=pltpu.HBM), whole((8, 128))],
+            out_specs=out_specs,
             scratch_shapes=[
-                pltpu.VMEM((2, UNIT_TILES * PART, D), bf16),
-                pltpu.VMEM((tiles, PART, D), bf16),
-                pltpu.SemaphoreType.DMA((tiles,)),
+                pltpu.VMEM((UNIT_TILES * PART, D), bf16),
+                pltpu.VMEM((units * UNIT_TILES, PART, D), bf16),
+                pltpu.SemaphoreType.DMA((units * UNIT_TILES,)),
             ],
         ),
-        out_shape=[pltpu.HBM((PEERS, PART, D), bf16), jax.ShapeDtypeStruct((8, 128), f32)],
+        out_shape=out_shape,
         input_output_aliases=aliases,
         name=name,
     )(*args)
@@ -544,27 +513,17 @@
     ]
 
 
-def attention_a(name, chunk, places, table, x, q, keys, values, proj, packed):
-    first, second = [specs_a(chunk, lambda i, n=n: n, lambda i, n=n: n) for n in places]
-    shared = (places[0] + 1) // 2 == (places[1] + 1) // 2
-    key_sets = [[keys, keys, values, values]] * (1 if shared else 2)
-    specs = [first[0], second[0], first[1], second[1], *first[2:]]
-    if not shared:
-        specs += second[2:]
-
-    def place(i, n):
-        return places[n]
-
-    return attention(
-        name, table, x, q, key_sets, specs, 1, place, False, 0, proj, packed
-    )
+def attention_a(name, chunk, place, table, x, q, keys, values, proj, packed):
+    args = [table, x, q, keys, keys, values, values, proj]
+    specs = [*specs_a(chunk, place, place), layer_of((D, D), 0)]
+    return attention(name, args, specs, 2, place, False, False, packed)
 
 
 def block_a(chunk, table, x, q, keys, values, weights, token):
     units = TILES_DEV // UNIT_TILES
-    specs = specs_a(chunk, lambda i: i, lambda i: i)
+    specs = specs_a(chunk, prior, lambda i: now(i, units))
     return block(
-        "block_a", table, x, q, [keys] * 2, [values] * 2, specs, units, False, True, 0, weights, token
+        "block_a", table, x, q, [keys] * 2, [values] * 2, specs, units, False, False, 0, weights, token
     )
 
 
@@ -578,26 +537,16 @@
     ] + [key_spec] * (2 * CHUNKS)
 
 
-def attention_b(table, x, q, keys, values, proj):
-    def place(i, n):
-        return 2 * i + n
-
-    first, second = [specs_b(lambda i, n=n: place(i, n), lambda i, n=n: place(i, n)) for n in (0, 1)]
-    specs = [first[0], second[0], first[1], second[1], *first[2:]]
-    return attention(
-        "attention_b",
-        table,
-        x,
-        q,
-        [[*keys, *values]],
-        specs,
-        SLOTS // PATCH_TILES,
-        place,
-        True,
-        1,
-        proj,
-        None,
-    )
+def attention_b(table, x, q, keys, values, part, gains, qkv_weight, proj):
+    def place(i):
+        return i
+
+    x_spec, q_spec, key_spec = specs_b(place, place)[:3]
+    specs = [x_spec, q_spec, key_spec, key_spec, *gather_specs(PATCH_TILES, 2)]
+    specs += [whole((4, D)), layer_of((D, 3 * D), 1), layer_of((D, D), 1)]
+    args = [table, x, q, keys, values, *[part] * PATCH_TILES, gains, qkv_weight, proj]
+    units = SLOTS // UNIT_TILES
+    return attention("attention_b", args, specs, units, place, True, True, None)
 
 
 def block_b(table, x, q, keys, values, weights, token):
@@ -692,22 +641,20 @@
     q, keys, values = qkv_own(points, norm_gains, qkv_weight)
     q = q.reshape(tiled)
     packed, token = attention_a(
-        "attention_a_middle", 0, (1, 2), dest_slot, x, q, keys, values, proj_weight, None
+        "attention_a_middle", 0, lambda i: i + 1, dest_slot, x, q, keys, values, proj_weight, None
     )
     keys, values = qkv_halo(before, after, norm_gains, qkv_weight, keys, values, token)
     packed, token = attention_a(
-        "attention_a_edges", 0, (0, 3), dest_slot, x, q, keys, values, proj_weight, packed
+        "attention_a_edges", 0, lambda i: 3 * i, dest_slot, x, q, keys, values, proj_weight, packed
     )
     early = exchange(packed)
     late = exchange(block_a(1, dest_slot, x, q, keys, values, weights, token))
-    owned = [
-        forward_owner(owner_from, early, weights, qkv_weight),
-        qkv_owner(owner_from, late, norm_gains, qkv_weight),
-    ]
-    xs, qs, owner_keys, owner_values = zip(*owned)
-    packed, token = attention_b(owner_from, xs[0], qs[0], owner_keys, owner_values, proj_weight)
+    x0, q0, k0, v0 = forward_owner(owner_from, early, weights, qkv_weight)
+    packed, token, x1, q1, k1, v1 = attention_b(
+        owner_from, x0, q0, k0, v0, late, norm_gains, qkv_weight, proj_weight
+    )
     early = exchange(packed)
-    late = exchange(block_b(owner_from, xs[1], qs[1], owner_keys, owner_values, weights, token))
+    late = exchange(block_b(owner_from, x1, q1, [k0, k1], [v0, v1], weights, token))
     done = forward_home(dest_slot, early, weights)
     return home(dest_slot, late, done).reshape(rows, D)
 

time: 180 us -> 180 us (level)
    pallas_call x4 -> x3, Pallas kernels: 38.9 us -> 39.2 us  [attention(): pl.pallas_call(functools.partial(attention_kernel, place, masked, arrivin...]
  transfers between devices with their start and end apart: 6 -> 6, of which waited for: 4 -> 4; matrix products, arithmetic and copies ran while one was open for 0% -> 0% of each run, Pallas kernels for 45% -> 44%
where the time goes in v7:
time: 180 us; the launch traced here: 178 us
  Pallas kernels  115 us (64%)
  waiting for transfers between devices  31.2 us (17%)
  starting transfers between devices  29.8 us (17%)
  local copies, waits for them, and re-layouts  1.87 us (1%)
    pallas_call x2, Pallas kernels, block(): pl.pallas_call(functools.partial(block_kernel, units, masked, whole_units...  40.5 us
    pallas_call x3, Pallas kernels, attention(): pl.pallas_call(functools.partial(attention_kernel, place, masked, arrivin...  39.2 us
    all_to_all x4, waiting for transfers between devices, exchange(): lax.all_to_all(part, 'chain', split_axis=0, concat_axis=0, tiled=True)  31.1 us
    all_to_all x4, starting transfers between devices, exchange(): lax.all_to_all(part, 'chain', split_axis=0, concat_axis=0, tiled=True)  21.4 us
    pallas_call x1, Pallas kernels, forward_owner(): pl.pallas_call(forward_owner_kernel, grid_spec=pltpu.PrefetchScalarGridSp...  15.4 us
    pallas_call x1, Pallas kernels, forward_home(): pl.pallas_call(forward_home_kernel, grid_spec=pltpu.PrefetchScalarGridSpe...  8.41 us
    ppermute x1, starting transfers between devices, body(): lax.ppermute(points[:HALF], axes, [((i + 1) % ring, i) for i in range(rin...  8.31 us
    pallas_call x1, Pallas kernels, qkv_own(): pl.pallas_call(qkv_own_kernel, grid=(rows // PATCH,), in_specs=[block, wh...  5.96 us
  transfers between devices with their start and end apart: 6, of which 4 were waited for; matrix products, arithmetic and copies ran while one was open for 0% of the time, Pallas kernels for 44%

profile of v7, /device:TPU:0, one launch (start us, length us, event | category | flops | bytes accessed | tf_op | source)
XLA Modules:
  0.0 177.6 jit_solution(11973567897017343456)
XLA Ops:
  0.0 1.2 fusion
  1.2 8.3 %collective-permute-start.1 = (bf16[512,384]{1,0:T(8,128)(2,1)S(1)}, bf16[512,384]{1,0:T(8,128)(2,1)S(1)}, u32[]{:S(2)}, u32[]{:S(2)}) collective-permute-start(bf16[512,384]{1,0:T(8,128)(2,1)S(1)} %get-tuple-element.43), channel_id=1, source_target_pairs={{1,0},{2,1},{3,2},{4,3},{5,4},{6,5},{7,6},{8,7},{9,8},{10,9},{11,1... | collective-permute-start | bytes 1179656 | tf_op jit(solution)/shard_map/ppermute | solution.py:637
  9.5 0.0 collective-permute-start
  9.5 6.0 %qkv_own.1 = (bf16[2048,384]{1,0:T(8,128)(2,1)}, bf16[3072,384]{1,0:T(8,128)(2,1)}, bf16[3072,384]{1,0:T(8,128)(2,1)}) custom-call(bf16[2048,384]{1,0:T(8,128)(2,1)} %x_ref.1, f32[4,384]{1,0:T(4,128)} %refs_4_.7, bf16[2,384,1152]{2,1,0:T(8,128)(2,1)} %refs_10_.1), custom_call_target="tpu_custom_call" | custom-call | tf_op jit(solution)/shard_map/qkv_own/pallas_call | solution.py:94
  15.5 0.0 copy-start
  15.5 0.0 copy-start.1
  15.5 8.4 %attention_a_middle.1 = (bf16[32,64,384]{2,1,0:T(8,128)(2,1)}, f32[8,128]{1,0:T(8,128)}) custom-call(s32[16]{0:T(128)} %table_ref.13, bf16[16,128,384]{2,1,0:T(8,128)(2,1)} %bitcast.3, bf16[16,128,384]{2,1,0:T(8,128)(2,1)} %bitcast.6, bf16[3072,384]{1,0:T(8,128)(2,1)} %get-tuple-element.25.k_ref.refs_0_.k_in, ...), custom_call_target="tpu_custom_call" | custom-call | tf_op jit(solution)/shard_map/attention_a_middle/pallas_call | solution.py:449
  23.8 0.0 collective-permute-done.1.b_ref
  23.9 0.0 collective-permute-done.a_ref
  23.9 0.0 copy-done
  23.9 0.0 copy-done.1
  23.9 0.0 copy-start.2
  23.9 0.7 copy-done.2
  24.6 2.4 %qkv_halo.1 = (bf16[3072,384]{1,0:T(8,128)(2,1)}, bf16[3072,384]{1,0:T(8,128)(2,1)}) custom-call(bf16[512,384]{1,0:T(8,128)(2,1)S(1)} %collective-permute-done.a_ref, bf16[512,384]{1,0:T(8,128)(2,1)S(1)} %collective-permute-done.1.b_ref, f32[4,384]{1,0:T(4,128)S(1)} %copy-done.1, ...), custom_call_target="tpu_custom_call", output_to_operand_aliasing={{0}: (4, {}), {1}: (5, {})} | custom-call | tf_op jit(solution)/shard_map/qkv_halo/pallas_call | solution.py:120
  27.0 8.2 %attention_a_edges.1 = (bf16[32,64,384]{2,1,0:T(8,128)(2,1)}, f32[8,128]{1,0:T(8,128)}) custom-call(s32[16]{0:T(128)} %table_ref.13, bf16[16,128,384]{2,1,0:T(8,128)(2,1)} %bitcast.4, bf16[16,128,384]{2,1,0:T(8,128)(2,1)} %bitcast.7, bf16[3072,384]{1,0:T(8,128)(2,1)} %get-tuple-element.28.k_ref.refs_0_.refs_1_, ...), custom_call_target="tpu_custom_call", output_to_operand_aliasing={{0}: (8, {})} | custom-call | tf_op jit(solution)/shard_map/attention_a_edges/pallas_call | solution.py:449
  35.2 4.9 %all-to-all-start = ((bf16[32,64,384]{2,1,0:T(8,128)(2,1)}), bf16[32,64,384]{2,1,0:T(8,128)(2,1)}, u32[]{:S(2)}, u32[]{:S(2)}) async-start(bf16[32,64,384]{2,1,0:T(8,128)(2,1)} %get-tuple-element.31), calls=%async_computation | async-start | bytes 3145728 | tf_op jit(solution)/shard_map/all_to_all | solution.py:627
  40.1 17.1 %block_a.1 = bf16[32,64,384]{2,1,0:T(8,128)(2,1)} custom-call(s32[16]{0:T(128)} %table_ref.13, bf16[16,128,384]{2,1,0:T(8,128)(2,1)} %bitcast.5, bf16[16,128,384]{2,1,0:T(8,128)(2,1)} %bitcast.8, bf16[3072,384]{1,0:T(8,128)(2,1)} %get-tuple-element.28.k_ref.refs_0_.refs_1_, bf16[3072,384]{1,0:T(8,128)(2,1)} %get-tuple-element.28.k_ref.refs_0_.refs_1_, ...), custom_call_target="tpu_custom_call" | custom-call | tf_op jit(solution)/shard_map/block_a/pallas_call | solution.py:472
  57.2 6.6 %all-to-all-done.refs_0_.refs_1_.refs_2_.refs_3_ = bf16[32,64,384]{2,1,0:T(8,128)(2,1)} async-done(((bf16[32,64,384]{2,1,0:T(8,128)(2,1)}), bf16[32,64,384]{2,1,0:T(8,128)(2,1)}, u32[]{:S(2)}, u32[]{:S(2)}) %all-to-all-start) | async-done | bytes 1572896 | tf_op jit(solution)/shard_map/all_to_all | solution.py:627
  63.9 4.7 %all-to-all-start.1 = ((bf16[32,64,384]{2,1,0:T(8,128)(2,1)}), bf16[32,64,384]{2,1,0:T(8,128)(2,1)}, u32[]{:S(2)}, u32[]{:S(2)}) async-start(bf16[32,64,384]{2,1,0:T(8,128)(2,1)} %block_a.1), calls=%async_computation.1 | async-start | bytes 3145728 | tf_op jit(solution)/shard_map/all_to_all | solution.py:627
  68.6 15.4 %forward_owner.1 = (bf16[24,64,384]{2,1,0:T(8,128)(2,1)}, bf16[24,64,384]{2,1,0:T(8,128)(2,1)}, bf16[24,64,384]{2,1,0:T(8,128)(2,1)}, bf16[24,64,384]{2,1,0:T(8,128)(2,1)}) custom-call(s32[24]{0:T(128)} %table_ref.11, bf16[32,64,384]{2,1,0:T(8,128)(2,1)} %all-to-all-done.refs_0_.refs_1_.refs_2_.refs_3_, ...), custom_call_target="tpu_custom_call" | custom-call | tf_op jit(solution)/shard_map/forward_owner/pallas_call | solution.py:188
  83.9 8.5 %all-to-all-done.1.refs_1_.refs_2_.refs_3_.refs_4_.refs_5_.refs_6_.refs_7_.refs_8_ = bf16[32,64,384]{2,1,0:T(8,128)(2,1)} async-done(((bf16[32,64,384]{2,1,0:T(8,128)(2,1)}), bf16[32,64,384]{2,1,0:T(8,128)(2,1)}, u32[]{:S(2)}, u32[]{:S(2)}) %all-to-all-start.1) | async-done | bytes 1572896 | tf_op jit(solution)/shard_map/all_to_all | solution.py:627
  92.5 22.6 %attention_b.1 = (bf16[32,64,384]{2,1,0:T(8,128)(2,1)}, f32[8,128]{1,0:T(8,128)}, bf16[24,64,384]{2,1,0:T(8,128)(2,1)}, bf16[24,64,384]{2,1,0:T(8,128)(2,1)}, bf...) custom-call(s32[24]{0:T(128)} %table_ref.11, bf16[24,64,384]{2,1,0:T(8,128)(2,1)} %get-tuple-element.32.x_ref, ...), custom_call_target="tpu_custom_call" | custom-call | tf_op jit(solution)/shard_map/attention_b/pallas_call | solution.py:449
  115.1 4.9 %all-to-all-start.3 = ((bf16[32,64,384]{2,1,0:T(8,128)(2,1)}), bf16[32,64,384]{2,1,0:T(8,128)(2,1)}, u32[]{:S(2)}, u32[]{:S(2)}) async-start(bf16[32,64,384]{2,1,0:T(8,128)(2,1)} %get-tuple-element.42), calls=%async_computation.3 | async-start | bytes 3145728 | tf_op jit(solution)/shard_map/all_to_all | solution.py:627
  120.0 23.4 %block_b.1 = bf16[32,64,384]{2,1,0:T(8,128)(2,1)} custom-call(s32[24]{0:T(128)} %table_ref.11, bf16[24,64,384]{2,1,0:T(8,128)(2,1)} %get-tuple-element.37.x_ref, bf16[24,64,384]{2,1,0:T(8,128)(2,1)} %get-tuple-element.38.q_ref, bf16[24,64,384]{2,1,0:T(8,128)(2,1)} %get-tuple-element.34.k_ref.refs_0_, bf16[24,64,384]{2,1,0:T(8,128)(2,1)} %get-tuple-element.39.refs_1_, ...), custom_call_target="tpu_custom_call" | custom-call | tf_op jit(solution)/shard_map/block_b/pallas_call | solution.py:472
  143.4 0.5 all-to-all-done.3.refs_0_.refs_1_.refs_2_.refs_3_
  143.9 6.9 %all-to-all-start.2 = ((bf16[32,64,384]{2,1,0:T(8,128)(2,1)}), bf16[32,64,384]{2,1,0:T(8,128)(2,1)}, u32[]{:S(2)}, u32[]{:S(2)}) async-start(bf16[32,64,384]{2,1,0:T(8,128)(2,1)} %block_b.1), calls=%async_computation.2 | async-start | bytes 3145728 | tf_op jit(solution)/shard_map/all_to_all | solution.py:627
  150.9 8.4 %forward_home.1.done_in = bf16[16,128,384]{2,1,0:T(8,128)(2,1)} custom-call(s32[16]{0:T(128)} %table_ref.13, bf16[32,64,384]{2,1,0:T(8,128)(2,1)} %all-to-all-done.3.refs_0_.refs_1_.refs_2_.refs_3_, bf16[32,64,384]{2,1,0:T(8,128)(2,1)} %all-to-all-done.3.refs_0_.refs_1_.refs_2_.refs_3_, bf16[32,64,384]{2,1,0:T(8,128)(2,1)} %all-to-all-done.3.refs_0_.refs_1_.refs_2_.refs_3_, ...), custom_call_target="tpu_custom_call" | custom-call | tf_op jit(solution)/shard_map/forward_home/pallas_call | solution.py:570
  159.3 15.5 %all-to-all-done.2.part_ref = bf16[32,64,384]{2,1,0:T(8,128)(2,1)} async-done(((bf16[32,64,384]{2,1,0:T(8,128)(2,1)}), bf16[32,64,384]{2,1,0:T(8,128)(2,1)}, u32[]{:S(2)}, u32[]{:S(2)}) %all-to-all-start.2) | async-done | bytes 1572896 | tf_op jit(solution)/shard_map/all_to_all | solution.py:627
  174.8 2.7 %home.1 = bf16[16,128,384]{2,1,0:T(8,128)(2,1)} custom-call(s32[16]{0:T(128)} %table_ref.13, bf16[32,64,384]{2,1,0:T(8,128)(2,1)} %all-to-all-done.2.part_ref, bf16[16,128,384]{2,1,0:T(8,128)(2,1)} %forward_home.1.done_in), custom_call_target="tpu_custom_call", output_to_operand_aliasing={{}: (2, {})} | custom-call | tf_op jit(solution)/shard_map/home/pallas_call | solution.py:607
Async XLA Ops:
  1.2 22.7 %collective-permute-start.1 = (bf16[512,384]{1,0:T(8,128)(2,1)S(1)}, bf16[512,384]{1,0:T(8,128)(2,1)S(1)}, u32[]{:S(2)}, u32[]{:S(2)}) collective-permute-start(bf16[512,384]{1,0:T(8,128)(2,1)S(1)} %get-tuple-element.43), channel_id=1, source_target_pairs={{1,0},{2,1},{3,2},{4,3},{5,4},{6,5},{7,6},{8,7},{9,8},{10,9},{11,1... | collective-permute-start | bytes 1179656 | tf_op jit(solution)/shard_map/ppermute | solution.py:637
  9.5 14.4 %collective-permute-start = (bf16[512,384]{1,0:T(8,128)(2,1)S(1)}, bf16[512,384]{1,0:T(8,128)(2,1)S(1)}, u32[]{:S(2)}, u32[]{:S(2)}) collective-permute-start(bf16[512,384]{1,0:T(8,128)(2,1)S(1)} %get-tuple-element.44), channel_id=1, source_target_pairs={{0,1},{1,2},{2,3},{3,4},{4,5},{5,6},{6,7},{7,8},{8,9},{9,10},{10,1... | collective-permute-start | bytes 1179656 | tf_op jit(solution)/shard_map/ppermute | solution.py:636
  15.5 8.4 %copy-start = (bf16[2,384,1152]{2,1,0:T(8,128)(2,1)S(1)}, bf16[2,384,1152]{2,1,0:T(8,128)(2,1)}, u32[]{:S(2)}) copy-start(bf16[2,384,1152]{2,1,0:T(8,128)(2,1)} %refs_10_.1) | copy-start | bytes 5308420
  15.5 8.4 %copy-start.1 = (f32[4,384]{1,0:T(4,128)S(1)}, f32[4,384]{1,0:T(4,128)}, u32[]{:S(2)}) copy-start(f32[4,384]{1,0:T(4,128)} %refs_4_.7) | copy-start | bytes 18436
  23.9 0.7 copy-start.2
  35.2 28.6 %all-to-all-start = ((bf16[32,64,384]{2,1,0:T(8,128)(2,1)}), bf16[32,64,384]{2,1,0:T(8,128)(2,1)}, u32[]{:S(2)}, u32[]{:S(2)}) async-start(bf16[32,64,384]{2,1,0:T(8,128)(2,1)} %get-tuple-element.31), calls=%async_computation | async-start | bytes 3145728 | tf_op jit(solution)/shard_map/all_to_all | solution.py:627
  63.9 28.6 %all-to-all-start.1 = ((bf16[32,64,384]{2,1,0:T(8,128)(2,1)}), bf16[32,64,384]{2,1,0:T(8,128)(2,1)}, u32[]{:S(2)}, u32[]{:S(2)}) async-start(bf16[32,64,384]{2,1,0:T(8,128)(2,1)} %block_a.1), calls=%async_computation.1 | async-start | bytes 3145728 | tf_op jit(solution)/shard_map/all_to_all | solution.py:627
  115.1 28.8 %all-to-all-start.3 = ((bf16[32,64,384]{2,1,0:T(8,128)(2,1)}), bf16[32,64,384]{2,1,0:T(8,128)(2,1)}, u32[]{:S(2)}, u32[]{:S(2)}) async-start(bf16[32,64,384]{2,1,0:T(8,128)(2,1)} %get-tuple-element.42), calls=%async_computation.3 | async-start | bytes 3145728 | tf_op jit(solution)/shard_map/all_to_all | solution.py:627
  143.9 30.8 %all-to-all-start.2 = ((bf16[32,64,384]{2,1,0:T(8,128)(2,1)}), bf16[32,64,384]{2,1,0:T(8,128)(2,1)}, u32[]{:S(2)}, u32[]{:S(2)}) async-start(bf16[32,64,384]{2,1,0:T(8,128)(2,1)} %block_b.1), calls=%async_computation.2 | async-start | bytes 3145728 | tf_op jit(solution)/shard_map/all_to_all | solution.py:627

commit v8 on v7

--- a/solution.py
+++ b/solution.py
@@ -23,7 +23,7 @@
 UNIT_TILES = 4
 HALF = PATCH // 2
 HID = 256
-FULL_VMEM = 65000 << 10
+FULL_VMEM = 65300 << 10
 
 norm_epsilon = 1e-05
 masked_score = -1000000000.0
@@ -121,8 +121,8 @@
         qkv_halo_kernel,
         grid=(1,),
         in_specs=[
-            pl.BlockSpec(memory_space=pltpu.VMEM),
-            pl.BlockSpec(memory_space=pltpu.VMEM),
+            whole((HALF, D)),
+            whole((HALF, D)),
             whole((4, D)),
             layer_of((D, 3 * D), 0),
             pl.BlockSpec(memory_space=pltpu.HBM),
@@ -132,7 +132,7 @@
         out_specs=[pl.BlockSpec((PATCH, D), lambda i: (last, 0))] * 2,
         out_shape=[ext, ext],
         input_output_aliases={4: 0, 5: 1},
-        compiler_params=pltpu.CompilerParams(vmem_limit_bytes=24 << 20),
+        compiler_params=pltpu.CompilerParams(vmem_limit_bytes=FULL_VMEM),
         name="qkv_halo",
     )(before, after, gains, qkv_weight, keys, values, earlier)
 
@@ -376,13 +376,12 @@
         v_ref, *refs = refs
         part_refs, refs = refs[:PATCH_TILES], refs[PATCH_TILES:]
         gains_ref, w_ref, proj_ref, *refs = refs
-        out_ref, token_ref, x1_ref, q1_ref, k1_ref, v1_ref, mixed_ref, tiles_ref, sems = refs
+        out_ref, x1_ref, q1_ref, k1_ref, v1_ref, mixed_ref, tiles_ref, sems = refs
         k_refs, v_refs = [k_ref, k1_ref], [v_ref, v1_ref]
     else:
         k_refs, v_refs = [k_ref, refs[0]], refs[1:3]
         proj_ref = refs[3]
-        out_ref, token_ref, mixed_ref, tiles_ref, sems = refs[-5:]
-    token_ref[...] = jnp.zeros_like(token_ref)
+        out_ref, mixed_ref, tiles_ref, sems = refs[-4:]
     step = pl.program_id(0)
     units = pl.num_programs(0)
     count = UNIT_TILES * PART
@@ -441,8 +440,8 @@
         aliases = {len(args): 0}
         args = [*args, packed]
         specs = [*specs, hbm]
-    out_specs = [hbm, whole((8, 128))]
-    out_shape = [pltpu.HBM((PEERS, PART, D), bf16), jax.ShapeDtypeStruct((8, 128), f32)]
+    out_specs = [hbm]
+    out_shape = [pltpu.HBM((PEERS, PART, D), bf16)]
     if arriving:
         out_specs += [pl.BlockSpec((PATCH_TILES, PART, D), lambda i, *_: (i // 2, 0, 0))] * 4
         out_shape += [pltpu.HBM((SLOTS, PART, D), bf16)] * 4
@@ -461,11 +460,12 @@
         ),
         out_shape=out_shape,
         input_output_aliases=aliases,
+        compiler_params=pltpu.CompilerParams(vmem_limit_bytes=FULL_VMEM),
         name=name,
     )(*args)
 
 
-def block(name, table, x, q, keys, values, specs, units, masked, whole_units, layer, weights, token):
+def block(name, table, x, q, keys, values, specs, units, masked, whole_units, layer, weights, earlier):
     gains, *matrices = weights
     pieces = len(keys)
     count = UNIT_TILES * PART
@@ -475,7 +475,7 @@
             num_scalar_prefetch=1,
             grid=(units if whole_units else units + 1,),
             in_specs=specs
-            + [whole((4, D)), whole((8, 128))]
+            + [whole((4, D)), pl.BlockSpec(memory_space=pltpu.HBM)]
             + [pl.BlockSpec(memory_space=pl.ANY)] * len(matrices),
             out_specs=whole((PEERS, PART, D)),
             scratch_shapes=[
@@ -489,7 +489,7 @@
         out_shape=jax.ShapeDtypeStruct((PEERS, PART, D), bf16),
         compiler_params=pltpu.CompilerParams(vmem_limit_bytes=FULL_VMEM),
         name=name,
-    )(table, x, q, *keys, *values, gains, token, *matrices)
+    )(table, x, q, *keys, *values, gains, earlier, *matrices)
 
 
 def specs_a(chunk, x_place, place):
@@ -519,11 +519,11 @@
     return attention(name, args, specs, 2, place, False, False, packed)
 
 
-def block_a(chunk, table, x, q, keys, values, weights, token):
+def block_a(chunk, table, x, q, keys, values, weights, earlier):
     units = TILES_DEV // UNIT_TILES
     specs = specs_a(chunk, prior, lambda i: now(i, units))
     return block(
-        "block_a", table, x, q, [keys] * 2, [values] * 2, specs, units, False, False, 0, weights, token
+        "block_a", table, x, q, [keys] * 2, [values] * 2, specs, units, False, False, 0, weights, earlier
     )
 
 
@@ -549,11 +549,11 @@
     return attention("attention_b", args, specs, units, place, True, True, None)
 
 
-def block_b(table, x, q, keys, values, weights, token):
+def block_b(table, x, q, keys, values, weights, earlier):
     units = SLOTS // UNIT_TILES
     specs = specs_b(prior, lambda i: now(i, units))
     return block(
-        "block_b", table, x, q, keys, values, specs, units, True, False, 1, weights, token
+        "block_b", table, x, q, keys, values, specs, units, True, False, 1, weights, earlier
     )
 
 
@@ -640,21 +640,21 @@
     x = points.reshape(tiled)
     q, keys, values = qkv_own(points, norm_gains, qkv_weight)
     q = q.reshape(tiled)
-    packed, token = attention_a(
+    (packed,) = attention_a(
         "attention_a_middle", 0, lambda i: i + 1, dest_slot, x, q, keys, values, proj_weight, None
     )
-    keys, values = qkv_halo(before, after, norm_gains, qkv_weight, keys, values, token)
-    packed, token = attention_a(
+    keys, values = qkv_halo(before, after, norm_gains, qkv_weight, keys, values, packed)
+    (packed,) = attention_a(
         "attention_a_edges", 0, lambda i: 3 * i, dest_slot, x, q, keys, values, proj_weight, packed
     )
     early = exchange(packed)
-    late = exchange(block_a(1, dest_slot, x, q, keys, values, weights, token))
+    late = exchange(block_a(1, dest_slot, x, q, keys, values, weights, packed))
     x0, q0, k0, v0 = forward_owner(owner_from, early, weights, qkv_weight)
-    packed, token, x1, q1, k1, v1 = attention_b(
+    packed, x1, q1, k1, v1 = attention_b(
         owner_from, x0, q0, k0, v0, late, norm_gains, qkv_weight, proj_weight
     )
     early = exchange(packed)
-    late = exchange(block_b(owner_from, x1, q1, [k0, k1], [v0, v1], weights, token))
+    late = exchange(block_b(owner_from, x1, q1, [k0, k1], [v0, v1], weights, packed))
     done = forward_home(dest_slot, early, weights)
     return home(dest_slot, late, done).reshape(rows, D)
 

time: 180 us -> 180 us (level)
    pallas_call x3, Pallas kernels: 39.2 us -> 37.2 us  [attention(): pl.pallas_call(functools.partial(attention_kernel, place, masked, arrivin...]
where the time goes in v8:
time: 180 us; the launch traced here: 177 us
  Pallas kernels  114 us (63%)
  waiting for transfers between devices  31.3 us (17%)
  starting transfers between devices  29.6 us (16%)
  local copies, waits for them, and re-layouts  2.07 us (1%)
    pallas_call x2, Pallas kernels, block(): pl.pallas_call(functools.partial(block_kernel, units, masked, whole_units...  40.4 us
    pallas_call x3, Pallas kernels, attention(): pl.pallas_call(functools.partial(attention_kernel, place, masked, arrivin...  37.2 us
    all_to_all x4, waiting for transfers between devices, exchange(): lax.all_to_all(part, 'chain', split_axis=0, concat_axis=0, tiled=True)  31.2 us
    all_to_all x4, starting transfers between devices, exchange(): lax.all_to_all(part, 'chain', split_axis=0, concat_axis=0, tiled=True)  21.4 us
    pallas_call x1, Pallas kernels, forward_owner(): pl.pallas_call(forward_owner_kernel, grid_spec=pltpu.PrefetchScalarGridSp...  15.4 us
    pallas_call x1, Pallas kernels, forward_home(): pl.pallas_call(forward_home_kernel, grid_spec=pltpu.PrefetchScalarGridSpe...  8.41 us
    ppermute x1, starting transfers between devices, body(): lax.ppermute(points[:HALF], axes, [((i + 1) % ring, i) for i in range(rin...  8.23 us
    pallas_call x1, Pallas kernels, qkv_own(): pl.pallas_call(qkv_own_kernel, grid=(rows // PATCH,), in_specs=[block, wh...  5.96 us
  transfers between devices with their start and end apart: 6, of which 4 were waited for; matrix products, arithmetic and copies ran while one was open for 0% of the time, Pallas kernels for 44%

profile of v8, /device:TPU:0, one launch (start us, length us, event | category | flops | bytes accessed | tf_op | source)
XLA Modules:
  0.0 177.2 jit_solution(18095981152950531880)
XLA Ops:
  0.0 2.1 %fusion = (bf16[512,384]{1,0:T(8,128)(2,1)}, bf16[512,384]{1,0:T(8,128)(2,1)}) fusion(bf16[2048,384]{1,0:T(8,128)(2,1)} %x_ref.1), kind=kLoop, calls=%fused_computation | loop fusion | bytes 1572864 | tf_op jit(solution)/shard_map/slice | solution.py:637
  2.1 8.2 %collective-permute-start.1 = (bf16[512,384]{1,0:T(8,128)(2,1)}, bf16[512,384]{1,0:T(8,128)(2,1)}, u32[]{:S(2)}, u32[]{:S(2)}) collective-permute-start(bf16[512,384]{1,0:T(8,128)(2,1)} %get-tuple-element.33), channel_id=1, source_target_pairs={{1,0},{2,1},{3,2},{4,3},{5,4},{6,5},{7,6},{8,7},{9,8},{10,9},{11,1... | collective-permute-start | bytes 1179656 | tf_op jit(solution)/shard_map/ppermute | solution.py:637
  10.3 0.0 collective-permute-start
  10.3 6.0 %qkv_own.1 = (bf16[2048,384]{1,0:T(8,128)(2,1)}, bf16[3072,384]{1,0:T(8,128)(2,1)}, bf16[3072,384]{1,0:T(8,128)(2,1)}) custom-call(bf16[2048,384]{1,0:T(8,128)(2,1)} %x_ref.1, f32[4,384]{1,0:T(4,128)} %refs_4_.7, bf16[2,384,1152]{2,1,0:T(8,128)(2,1)} %refs_10_.1), custom_call_target="tpu_custom_call" | custom-call | tf_op jit(solution)/shard_map/qkv_own/pallas_call | solution.py:94
  16.3 7.6 %attention_a_middle.1.after_in.refs_4_ = bf16[32,64,384]{2,1,0:T(8,128)(2,1)} custom-call(s32[16]{0:T(128)} %table_ref.13, bf16[16,128,384]{2,1,0:T(8,128)(2,1)} %bitcast.3, bf16[16,128,384]{2,1,0:T(8,128)(2,1)} %bitcast.6, bf16[3072,384]{1,0:T(8,128)(2,1)} %get-tuple-element.20.k_ref.refs_0_.k_in, bf16[3072,384]{1,0:T(8,128)(2,1)} %get-tuple-element.20.k_ref.refs_0_.k_in, ...), custom_call_target="tpu_custom_call" | custom-call | tf_op jit(solution)/shard_map/attention_a_middle/pallas_call | solution.py:448
  23.9 0.0 collective-permute-done.1.b_ref
  23.9 0.0 collective-permute-done.a_ref
  23.9 3.9 %qkv_halo.1 = (bf16[3072,384]{1,0:T(8,128)(2,1)}, bf16[3072,384]{1,0:T(8,128)(2,1)}) custom-call(bf16[512,384]{1,0:T(8,128)(2,1)} %collective-permute-done.a_ref, bf16[512,384]{1,0:T(8,128)(2,1)} %collective-permute-done.1.b_ref, f32[4,384]{1,0:T(4,128)} %refs_4_.7, bf16[2,384,1152]{2,1,0:T(8,128)(2,1)} %refs_10_.1, ...), custom_call_target="tpu_custom_call", output_to_operand_aliasing={{0}: (4, {}), {1}: (5, {})} | custom-call | tf_op jit(solution)/shard_map/qkv_halo/pallas_call | solution.py:120
  27.8 7.6 %attention_a_edges.1.refs_5_ = bf16[32,64,384]{2,1,0:T(8,128)(2,1)} custom-call(s32[16]{0:T(128)} %table_ref.13, bf16[16,128,384]{2,1,0:T(8,128)(2,1)} %bitcast.4, bf16[16,128,384]{2,1,0:T(8,128)(2,1)} %bitcast.7, bf16[3072,384]{1,0:T(8,128)(2,1)} %get-tuple-element.22.k_ref.refs_0_.refs_1_, ...), custom_call_target="tpu_custom_call", output_to_operand_aliasing={{}: (8, {})} | custom-call | tf_op jit(solution)/shard_map/attention_a_edges/pallas_call | solution.py:448
  35.4 4.9 %all-to-all-start = ((bf16[32,64,384]{2,1,0:T(8,128)(2,1)}), bf16[32,64,384]{2,1,0:T(8,128)(2,1)}, u32[]{:S(2)}, u32[]{:S(2)}) async-start(bf16[32,64,384]{2,1,0:T(8,128)(2,1)} %attention_a_edges.1.refs_5_), calls=%async_computation | async-start | bytes 3145728 | tf_op jit(solution)/shard_map/all_to_all | solution.py:627
  40.3 17.1 %block_a.1 = bf16[32,64,384]{2,1,0:T(8,128)(2,1)} custom-call(s32[16]{0:T(128)} %table_ref.13, bf16[16,128,384]{2,1,0:T(8,128)(2,1)} %bitcast.5, bf16[16,128,384]{2,1,0:T(8,128)(2,1)} %bitcast.8, bf16[3072,384]{1,0:T(8,128)(2,1)} %get-tuple-element.22.k_ref.refs_0_.refs_1_, bf16[3072,384]{1,0:T(8,128)(2,1)} %get-tuple-element.22.k_ref.refs_0_.refs_1_, ...), custom_call_target="tpu_custom_call" | custom-call | tf_op jit(solution)/shard_map/block_a/pallas_call | solution.py:472
  57.4 6.6 %all-to-all-done.refs_0_.refs_1_.refs_2_.refs_3_ = bf16[32,64,384]{2,1,0:T(8,128)(2,1)} async-done(((bf16[32,64,384]{2,1,0:T(8,128)(2,1)}), bf16[32,64,384]{2,1,0:T(8,128)(2,1)}, u32[]{:S(2)}, u32[]{:S(2)}) %all-to-all-start) | async-done | bytes 1572896 | tf_op jit(solution)/shard_map/all_to_all | solution.py:627
  64.0 4.7 %all-to-all-start.1 = ((bf16[32,64,384]{2,1,0:T(8,128)(2,1)}), bf16[32,64,384]{2,1,0:T(8,128)(2,1)}, u32[]{:S(2)}, u32[]{:S(2)}) async-start(bf16[32,64,384]{2,1,0:T(8,128)(2,1)} %block_a.1), calls=%async_computation.1 | async-start | bytes 3145728 | tf_op jit(solution)/shard_map/all_to_all | solution.py:627
  68.7 15.4 %forward_owner.1 = (bf16[24,64,384]{2,1,0:T(8,128)(2,1)}, bf16[24,64,384]{2,1,0:T(8,128)(2,1)}, bf16[24,64,384]{2,1,0:T(8,128)(2,1)}, bf16[24,64,384]{2,1,0:T(8,128)(2,1)}) custom-call(s32[24]{0:T(128)} %table_ref.11, bf16[32,64,384]{2,1,0:T(8,128)(2,1)} %all-to-all-done.refs_0_.refs_1_.refs_2_.refs_3_, ...), custom_call_target="tpu_custom_call" | custom-call | tf_op jit(solution)/shard_map/forward_owner/pallas_call | solution.py:188
  84.1 8.5 %all-to-all-done.1.refs_1_.refs_2_.refs_3_.refs_4_.refs_5_.refs_6_.refs_7_.refs_8_ = bf16[32,64,384]{2,1,0:T(8,128)(2,1)} async-done(((bf16[32,64,384]{2,1,0:T(8,128)(2,1)}), bf16[32,64,384]{2,1,0:T(8,128)(2,1)}, u32[]{:S(2)}, u32[]{:S(2)}) %all-to-all-start.1) | async-done | bytes 1572896 | tf_op jit(solution)/shard_map/all_to_all | solution.py:627
  92.6 22.0 %attention_b.1 = (bf16[32,64,384]{2,1,0:T(8,128)(2,1)}, bf16[24,64,384]{2,1,0:T(8,128)(2,1)}, bf16[24,64,384]{2,1,0:T(8,128)(2,1)}, bf16[24,64,384]{2,1,0:T(8,128)(2,1)}, bf16[24,64,384]{2,1,0:T(8,128)(2,1)}) custom-call(s32[24]{0:T(128)} %table_ref.11, bf16[24,64,384]{2,1,0:T(8,128)(2,1)} %get-tuple-element.24.x_ref, ...), custom_call_target="tpu_custom_call" | custom-call | tf_op jit(solution)/shard_map/attention_b/pallas_call | solution.py:448
  114.7 4.9 %all-to-all-start.3 = ((bf16[32,64,384]{2,1,0:T(8,128)(2,1)}), bf16[32,64,384]{2,1,0:T(8,128)(2,1)}, u32[]{:S(2)}, u32[]{:S(2)}) async-start(bf16[32,64,384]{2,1,0:T(8,128)(2,1)} %get-tuple-element.32.refs_5_), calls=%async_computation.3 | async-start | bytes 3145728 | tf_op jit(solution)/shard_map/all_to_all | solution.py:627
  119.6 23.3 %block_b.1 = bf16[32,64,384]{2,1,0:T(8,128)(2,1)} custom-call(s32[24]{0:T(128)} %table_ref.11, bf16[24,64,384]{2,1,0:T(8,128)(2,1)} %get-tuple-element.28.x_ref, bf16[24,64,384]{2,1,0:T(8,128)(2,1)} %get-tuple-element.29.q_ref, bf16[24,64,384]{2,1,0:T(8,128)(2,1)} %get-tuple-element.26.k_ref.refs_0_, bf16[24,64,384]{2,1,0:T(8,128)(2,1)} %get-tuple-element.30.refs_1_, ...), custom_call_target="tpu_custom_call" | custom-call | tf_op jit(solution)/shard_map/block_b/pallas_call | solution.py:472
  142.9 0.6 all-to-all-done.3.refs_0_.refs_1_.refs_2_.refs_3_
  143.5 6.9 %all-to-all-start.2 = ((bf16[32,64,384]{2,1,0:T(8,128)(2,1)}), bf16[32,64,384]{2,1,0:T(8,128)(2,1)}, u32[]{:S(2)}, u32[]{:S(2)}) async-start(bf16[32,64,384]{2,1,0:T(8,128)(2,1)} %block_b.1), calls=%async_computation.2 | async-start | bytes 3145728 | tf_op jit(solution)/shard_map/all_to_all | solution.py:627
  150.4 8.4 %forward_home.1.done_in = bf16[16,128,384]{2,1,0:T(8,128)(2,1)} custom-call(s32[16]{0:T(128)} %table_ref.13, bf16[32,64,384]{2,1,0:T(8,128)(2,1)} %all-to-all-done.3.refs_0_.refs_1_.refs_2_.refs_3_, bf16[32,64,384]{2,1,0:T(8,128)(2,1)} %all-to-all-done.3.refs_0_.refs_1_.refs_2_.refs_3_, bf16[32,64,384]{2,1,0:T(8,128)(2,1)} %all-to-all-done.3.refs_0_.refs_1_.refs_2_.refs_3_, ...), custom_call_target="tpu_custom_call" | custom-call | tf_op jit(solution)/shard_map/forward_home/pallas_call | solution.py:570
  158.8 15.5 %all-to-all-done.2.part_ref = bf16[32,64,384]{2,1,0:T(8,128)(2,1)} async-done(((bf16[32,64,384]{2,1,0:T(8,128)(2,1)}), bf16[32,64,384]{2,1,0:T(8,128)(2,1)}, u32[]{:S(2)}, u32[]{:S(2)}) %all-to-all-start.2) | async-done | bytes 1572896 | tf_op jit(solution)/shard_map/all_to_all | solution.py:627
  174.3 2.7 %home.1 = bf16[16,128,384]{2,1,0:T(8,128)(2,1)} custom-call(s32[16]{0:T(128)} %table_ref.13, bf16[32,64,384]{2,1,0:T(8,128)(2,1)} %all-to-all-done.2.part_ref, bf16[16,128,384]{2,1,0:T(8,128)(2,1)} %forward_home.1.done_in), custom_call_target="tpu_custom_call", output_to_operand_aliasing={{}: (2, {})} | custom-call | tf_op jit(solution)/shard_map/home/pallas_call | solution.py:607
Async XLA Ops:
  2.1 21.8 %collective-permute-start.1 = (bf16[512,384]{1,0:T(8,128)(2,1)}, bf16[512,384]{1,0:T(8,128)(2,1)}, u32[]{:S(2)}, u32[]{:S(2)}) collective-permute-start(bf16[512,384]{1,0:T(8,128)(2,1)} %get-tuple-element.33), channel_id=1, source_target_pairs={{1,0},{2,1},{3,2},{4,3},{5,4},{6,5},{7,6},{8,7},{9,8},{10,9},{11,1... | collective-permute-start | bytes 1179656 | tf_op jit(solution)/shard_map/ppermute | solution.py:637
  10.3 13.6 %collective-permute-start = (bf16[512,384]{1,0:T(8,128)(2,1)}, bf16[512,384]{1,0:T(8,128)(2,1)}, u32[]{:S(2)}, u32[]{:S(2)}) collective-permute-start(bf16[512,384]{1,0:T(8,128)(2,1)} %get-tuple-element.34), channel_id=1, source_target_pairs={{0,1},{1,2},{2,3},{3,4},{4,5},{5,6},{6,7},{7,8},{8,9},{9,10},{10,1... | collective-permute-start | bytes 1179656 | tf_op jit(solution)/shard_map/ppermute | solution.py:636
  35.4 28.6 %all-to-all-start = ((bf16[32,64,384]{2,1,0:T(8,128)(2,1)}), bf16[32,64,384]{2,1,0:T(8,128)(2,1)}, u32[]{:S(2)}, u32[]{:S(2)}) async-start(bf16[32,64,384]{2,1,0:T(8,128)(2,1)} %attention_a_edges.1.refs_5_), calls=%async_computation | async-start | bytes 3145728 | tf_op jit(solution)/shard_map/all_to_all | solution.py:627
  64.0 28.6 %all-to-all-start.1 = ((bf16[32,64,384]{2,1,0:T(8,128)(2,1)}), bf16[32,64,384]{2,1,0:T(8,128)(2,1)}, u32[]{:S(2)}, u32[]{:S(2)}) async-start(bf16[32,64,384]{2,1,0:T(8,128)(2,1)} %block_a.1), calls=%async_computation.1 | async-start | bytes 3145728 | tf_op jit(solution)/shard_map/all_to_all | solution.py:627
  114.7 28.8 %all-to-all-start.3 = ((bf16[32,64,384]{2,1,0:T(8,128)(2,1)}), bf16[32,64,384]{2,1,0:T(8,128)(2,1)}, u32[]{:S(2)}, u32[]{:S(2)}) async-start(bf16[32,64,384]{2,1,0:T(8,128)(2,1)} %get-tuple-element.32.refs_5_), calls=%async_computation.3 | async-start | bytes 3145728 | tf_op jit(solution)/shard_map/all_to_all | solution.py:627
  143.5 30.8 %all-to-all-start.2 = ((bf16[32,64,384]{2,1,0:T(8,128)(2,1)}), bf16[32,64,384]{2,1,0:T(8,128)(2,1)}, u32[]{:S(2)}, u32[]{:S(2)}) async-start(bf16[32,64,384]{2,1,0:T(8,128)(2,1)} %block_b.1), calls=%async_computation.2 | async-start | bytes 3145728 | tf_op jit(solution)/shard_map/all_to_all | solution.py:627

commit v9 on v8

--- a/solution.py
+++ b/solution.py
@@ -23,7 +23,7 @@
 UNIT_TILES = 4
 HALF = PATCH // 2
 HID = 256
-FULL_VMEM = 65300 << 10
+FULL_VMEM = 65000 << 10
 
 norm_epsilon = 1e-05
 masked_score = -1000000000.0
@@ -121,8 +121,8 @@
         qkv_halo_kernel,
         grid=(1,),
         in_specs=[
-            whole((HALF, D)),
-            whole((HALF, D)),
+            pl.BlockSpec(memory_space=pltpu.VMEM),
+            pl.BlockSpec(memory_space=pltpu.VMEM),
             whole((4, D)),
             layer_of((D, 3 * D), 0),
             pl.BlockSpec(memory_space=pltpu.HBM),
@@ -132,7 +132,7 @@
         out_specs=[pl.BlockSpec((PATCH, D), lambda i: (last, 0))] * 2,
         out_shape=[ext, ext],
         input_output_aliases={4: 0, 5: 1},
-        compiler_params=pltpu.CompilerParams(vmem_limit_bytes=FULL_VMEM),
+        compiler_params=pltpu.CompilerParams(vmem_limit_bytes=24 << 20),
         name="qkv_halo",
     )(before, after, gains, qkv_weight, keys, values, earlier)
 
@@ -371,7 +371,7 @@
         emit(*result, step - 1)
 
 
-def attention_kernel(place, masked, arriving, table_ref, x_ref, q_ref, k_ref, *refs):
+def attention_kernel(place, masked, arriving, token, table_ref, before_ref, x_ref, q_ref, k_ref, *refs):
     if arriving:
         v_ref, *refs = refs
         part_refs, refs = refs[:PATCH_TILES], refs[PATCH_TILES:]
@@ -381,7 +381,11 @@
     else:
         k_refs, v_refs = [k_ref, refs[0]], refs[1:3]
         proj_ref = refs[3]
-        out_ref, mixed_ref, tiles_ref, sems = refs[-4:]
+        *refs, mixed_ref, tiles_ref, sems = refs[4:]
+        out_ref = refs[-1]
+        if token:
+            out_ref, token_ref = refs[-2:]
+            token_ref[...] = jnp.zeros_like(token_ref)
     step = pl.program_id(0)
     units = pl.num_programs(0)
     count = UNIT_TILES * PART
@@ -399,16 +403,21 @@
             v1_ref[...] = out[:, 2 * D :].astype(bf16).reshape(shape)
 
     scores, soften, mix = attention_parts(
-        masked, place(step) * UNIT_TILES, table_ref, q_ref, k_refs, v_refs, mixed_ref
-    )
+        masked, place(step) * UNIT_TILES, table_ref, q_ref, k_refs, v_refs, mixed_ref.at[step % 2]
+    )
+
+    def join(unit, base_ref):
+        base = base_ref[...].reshape(count, D).astype(f32)
+        inner = (base + dot(mixed_ref[unit % 2], proj_ref[...])).astype(bf16)
+        tiles_ref[pl.ds(unit * UNIT_TILES, UNIT_TILES)] = inner.reshape(UNIT_TILES, PART, D)
+
     s = scores(0)
+    earlier = jnp.maximum(step - 1, 0)
+    join(earlier, before_ref)
     for h in range(HEADS):
         later = scores(h + 1) if h + 1 < HEADS else None
         mix(h, soften(s))
         s = later
-    base = x_ref[...].reshape(count, D).astype(f32)
-    inner = (base + dot(mixed_ref[...], proj_ref[...])).astype(bf16)
-    tiles_ref[pl.ds(step * UNIT_TILES, UNIT_TILES)] = inner.reshape(UNIT_TILES, PART, D)
 
     def copy_of(unit, t, act):
         slot = table_ref[place(unit) * UNIT_TILES + t]
@@ -422,11 +431,17 @@
                 )
             )
 
-    for t in range(UNIT_TILES):
-        copy_of(step, t, lambda copy: copy.start())
+    @pl.when(step > 0)
+    def _():
+        for t in range(UNIT_TILES):
+            copy_of(earlier, t, lambda copy: copy.start())
 
     @pl.when(step == units - 1)
     def _():
+        join(step, x_ref)
+        for t in range(UNIT_TILES):
+            copy_of(step, t, lambda copy: copy.start())
+
         @pl.loop(0, units)
         def _(unit):
             for t in range(UNIT_TILES):
@@ -434,6 +449,7 @@
 
 
 def attention(name, args, specs, units, place, masked, arriving, packed):
+    token = packed is None and not arriving
     hbm = pl.BlockSpec(memory_space=pltpu.HBM)
     aliases = {}
     if packed is not None:
@@ -442,25 +458,27 @@
         specs = [*specs, hbm]
     out_specs = [hbm]
     out_shape = [pltpu.HBM((PEERS, PART, D), bf16)]
+    if token:
+        out_specs.append(whole((8, 128)))
+        out_shape.append(jax.ShapeDtypeStruct((8, 128), f32))
     if arriving:
         out_specs += [pl.BlockSpec((PATCH_TILES, PART, D), lambda i, *_: (i // 2, 0, 0))] * 4
         out_shape += [pltpu.HBM((SLOTS, PART, D), bf16)] * 4
     return pl.pallas_call(
-        functools.partial(attention_kernel, place, masked, arriving),
+        functools.partial(attention_kernel, place, masked, arriving, token),
         grid_spec=pltpu.PrefetchScalarGridSpec(
             num_scalar_prefetch=1,
             grid=(units,),
             in_specs=specs,
             out_specs=out_specs,
             scratch_shapes=[
-                pltpu.VMEM((UNIT_TILES * PART, D), bf16),
+                pltpu.VMEM((2, UNIT_TILES * PART, D), bf16),
                 pltpu.VMEM((units * UNIT_TILES, PART, D), bf16),
                 pltpu.SemaphoreType.DMA((units * UNIT_TILES,)),
             ],
         ),
         out_shape=out_shape,
         input_output_aliases=aliases,
-        compiler_params=pltpu.CompilerParams(vmem_limit_bytes=FULL_VMEM),
         name=name,
     )(*args)
 
@@ -514,8 +532,9 @@
 
 
 def attention_a(name, chunk, place, table, x, q, keys, values, proj, packed):
-    args = [table, x, q, keys, keys, values, values, proj]
-    specs = [*specs_a(chunk, place, place), layer_of((D, D), 0)]
+    args = [table, x, x, q, keys, keys, values, values, proj]
+    before = specs_a(chunk, lambda i: place(prior(i)), place)[0]
+    specs = [before, *specs_a(chunk, place, place), layer_of((D, D), 0)]
     return attention(name, args, specs, 2, place, False, False, packed)
 
 
@@ -542,9 +561,10 @@
         return i
 
     x_spec, q_spec, key_spec = specs_b(place, place)[:3]
-    specs = [x_spec, q_spec, key_spec, key_spec, *gather_specs(PATCH_TILES, 2)]
+    before = specs_b(prior, place)[0]
+    specs = [before, x_spec, q_spec, key_spec, key_spec, *gather_specs(PATCH_TILES, 2)]
     specs += [whole((4, D)), layer_of((D, 3 * D), 1), layer_of((D, D), 1)]
-    args = [table, x, q, keys, values, *[part] * PATCH_TILES, gains, qkv_weight, proj]
+    args = [table, x, x, q, keys, values, *[part] * PATCH_TILES, gains, qkv_weight, proj]
     units = SLOTS // UNIT_TILES
     return attention("attention_b", args, specs, units, place, True, True, None)
 
@@ -640,10 +660,10 @@
     x = points.reshape(tiled)
     q, keys, values = qkv_own(points, norm_gains, qkv_weight)
     q = q.reshape(tiled)
-    (packed,) = attention_a(
+    packed, token = attention_a(
         "attention_a_middle", 0, lambda i: i + 1, dest_slot, x, q, keys, values, proj_weight, None
     )
-    keys, values = qkv_halo(before, after, norm_gains, qkv_weight, keys, values, packed)
+    keys, values = qkv_halo(before, after, norm_gains, qkv_weight, keys, values, token)
     (packed,) = attention_a(
         "attention_a_edges", 0, lambda i: 3 * i, dest_slot, x, q, keys, values, proj_weight, packed
     )

time: 180 us -> 180 us (level)
    pallas_call x3, Pallas kernels: 37.2 us -> 39.8 us  [attention(): pl.pallas_call(functools.partial(attention_kernel, place, masked, arrivin...]
where the time goes in v9:
time: 180 us; the launch traced here: 178 us
  Pallas kernels  115 us (64%)
  waiting for transfers between devices  30.7 us (17%)
  starting transfers between devices  30.1 us (17%)
  local copies, waits for them, and re-layouts  1.86 us (1%)
    pallas_call x2, Pallas kernels, block(): pl.pallas_call(functools.partial(block_kernel, units, masked, whole_units...  40.5 us
    pallas_call x3, Pallas kernels, attention(): pl.pallas_call(functools.partial(attention_kernel, place, masked, arrivin...  39.8 us
    all_to_all x4, waiting for transfers between devices, exchange(): lax.all_to_all(part, 'chain', split_axis=0, concat_axis=0, tiled=True)  30.7 us
    all_to_all x4, starting transfers between devices, exchange(): lax.all_to_all(part, 'chain', split_axis=0, concat_axis=0, tiled=True)  21.8 us
    pallas_call x1, Pallas kernels, forward_owner(): pl.pallas_call(forward_owner_kernel, grid_spec=pltpu.PrefetchScalarGridSp...  15.4 us
    pallas_call x1, Pallas kernels, forward_home(): pl.pallas_call(forward_home_kernel, grid_spec=pltpu.PrefetchScalarGridSpe...  8.41 us
    ppermute x1, starting transfers between devices, body(): lax.ppermute(points[:HALF], axes, [((i + 1) % ring, i) for i in range(rin...  8.31 us
    pallas_call x1, Pallas kernels, qkv_own(): pl.pallas_call(qkv_own_kernel, grid=(rows // PATCH,), in_specs=[block, wh...  5.95 us
  transfers between devices with their start and end apart: 6, of which 4 were waited for; matrix products, arithmetic and copies ran while one was open for 0% of the time, Pallas kernels for 44%

profile of v9, /device:TPU:0, one launch (start us, length us, event | category | flops | bytes accessed | tf_op | source)
XLA Modules:
  0.0 178.1 jit_solution(687222368160892134)
XLA Ops:
  0.0 1.2 fusion
  1.2 8.3 %collective-permute-start.1 = (bf16[512,384]{1,0:T(8,128)(2,1)S(1)}, bf16[512,384]{1,0:T(8,128)(2,1)S(1)}, u32[]{:S(2)}, u32[]{:S(2)}) collective-permute-start(bf16[512,384]{1,0:T(8,128)(2,1)S(1)} %get-tuple-element.37), channel_id=1, source_target_pairs={{1,0},{2,1},{3,2},{4,3},{5,4},{6,5},{7,6},{8,7},{9,8},{10,9},{11,1... | collective-permute-start | bytes 1179656 | tf_op jit(solution)/shard_map/ppermute | solution.py:657
  9.5 0.0 collective-permute-start
  9.5 5.9 %qkv_own.1 = (bf16[2048,384]{1,0:T(8,128)(2,1)}, bf16[3072,384]{1,0:T(8,128)(2,1)}, bf16[3072,384]{1,0:T(8,128)(2,1)}) custom-call(bf16[2048,384]{1,0:T(8,128)(2,1)} %x_ref.1, f32[4,384]{1,0:T(4,128)} %refs_4_.7, bf16[2,384,1152]{2,1,0:T(8,128)(2,1)} %refs_10_.1), custom_call_target="tpu_custom_call" | custom-call | tf_op jit(solution)/shard_map/qkv_own/pallas_call | solution.py:94
  15.5 0.0 copy-start
  15.5 0.0 copy-start.1
  15.5 8.7 %attention_a_middle.1 = (bf16[32,64,384]{2,1,0:T(8,128)(2,1)}, f32[8,128]{1,0:T(8,128)}) custom-call(s32[16]{0:T(128)} %table_ref.13, bf16[16,128,384]{2,1,0:T(8,128)(2,1)} %bitcast.3, bf16[16,128,384]{2,1,0:T(8,128)(2,1)} %bitcast.4, bf16[16,128,384]{2,1,0:T(8,128)(2,1)} %bitcast.8, bf16[3072,384]{1,0:T(8,128)(2,1)} %get-tuple-element.22.k_ref.refs_0_.k_in, ...), custom_call_target="tpu_custom_call" | custom-call | tf_op jit(solution)/shard_map/attention_a_middle/pallas_call | solution.py:467
  24.2 0.0 collective-permute-done.1.b_ref
  24.2 0.0 collective-permute-done.a_ref
  24.2 0.0 copy-done
  24.2 0.0 copy-done.1
  24.2 0.0 copy-start.2
  24.3 0.7 copy-done.2
  24.9 2.4 %qkv_halo.1 = (bf16[3072,384]{1,0:T(8,128)(2,1)}, bf16[3072,384]{1,0:T(8,128)(2,1)}) custom-call(bf16[512,384]{1,0:T(8,128)(2,1)S(1)} %collective-permute-done.a_ref, bf16[512,384]{1,0:T(8,128)(2,1)S(1)} %collective-permute-done.1.b_ref, f32[4,384]{1,0:T(4,128)S(1)} %copy-done.1, ...), custom_call_target="tpu_custom_call", output_to_operand_aliasing={{0}: (4, {}), {1}: (5, {})} | custom-call | tf_op jit(solution)/shard_map/qkv_halo/pallas_call | solution.py:120
  27.4 8.0 %attention_a_edges.1.refs_5_ = bf16[32,64,384]{2,1,0:T(8,128)(2,1)} custom-call(s32[16]{0:T(128)} %table_ref.13, bf16[16,128,384]{2,1,0:T(8,128)(2,1)} %bitcast.5, bf16[16,128,384]{2,1,0:T(8,128)(2,1)} %bitcast.6, bf16[16,128,384]{2,1,0:T(8,128)(2,1)} %bitcast.9, ...), custom_call_target="tpu_custom_call", output_to_operand_aliasing={{}: (9, {})} | custom-call | tf_op jit(solution)/shard_map/attention_a_edges/pallas_call | solution.py:467
  35.4 4.9 %all-to-all-start = ((bf16[32,64,384]{2,1,0:T(8,128)(2,1)}), bf16[32,64,384]{2,1,0:T(8,128)(2,1)}, u32[]{:S(2)}, u32[]{:S(2)}) async-start(bf16[32,64,384]{2,1,0:T(8,128)(2,1)} %attention_a_edges.1.refs_5_), calls=%async_computation | async-start | bytes 3145728 | tf_op jit(solution)/shard_map/all_to_all | solution.py:647
  40.3 17.1 %block_a.1 = bf16[32,64,384]{2,1,0:T(8,128)(2,1)} custom-call(s32[16]{0:T(128)} %table_ref.13, bf16[16,128,384]{2,1,0:T(8,128)(2,1)} %bitcast.7, bf16[16,128,384]{2,1,0:T(8,128)(2,1)} %bitcast.10, bf16[3072,384]{1,0:T(8,128)(2,1)} %get-tuple-element.25.k_ref.refs_0_.refs_1_, bf16[3072,384]{1,0:T(8,128)(2,1)} %get-tuple-element.25.k_ref.refs_0_.refs_1_, ...), custom_call_target="tpu_custom_call" | custom-call | tf_op jit(solution)/shard_map/block_a/pallas_call | solution.py:490
  57.4 6.6 %all-to-all-done.refs_0_.refs_1_.refs_2_.refs_3_ = bf16[32,64,384]{2,1,0:T(8,128)(2,1)} async-done(((bf16[32,64,384]{2,1,0:T(8,128)(2,1)}), bf16[32,64,384]{2,1,0:T(8,128)(2,1)}, u32[]{:S(2)}, u32[]{:S(2)}) %all-to-all-start) | async-done | bytes 1572896 | tf_op jit(solution)/shard_map/all_to_all | solution.py:647
  64.0 4.9 %all-to-all-start.1 = ((bf16[32,64,384]{2,1,0:T(8,128)(2,1)}), bf16[32,64,384]{2,1,0:T(8,128)(2,1)}, u32[]{:S(2)}, u32[]{:S(2)}) async-start(bf16[32,64,384]{2,1,0:T(8,128)(2,1)} %block_a.1), calls=%async_computation.1 | async-start | bytes 3145728 | tf_op jit(solution)/shard_map/all_to_all | solution.py:647
  68.9 15.4 %forward_owner.1 = (bf16[24,64,384]{2,1,0:T(8,128)(2,1)}, bf16[24,64,384]{2,1,0:T(8,128)(2,1)}, bf16[24,64,384]{2,1,0:T(8,128)(2,1)}, bf16[24,64,384]{2,1,0:T(8,128)(2,1)}) custom-call(s32[24]{0:T(128)} %table_ref.11, bf16[32,64,384]{2,1,0:T(8,128)(2,1)} %all-to-all-done.refs_0_.refs_1_.refs_2_.refs_3_, ...), custom_call_target="tpu_custom_call" | custom-call | tf_op jit(solution)/shard_map/forward_owner/pallas_call | solution.py:188
  84.3 8.3 %all-to-all-done.1.refs_1_.refs_2_.refs_3_.refs_4_.refs_5_.refs_6_.refs_7_.refs_8_ = bf16[32,64,384]{2,1,0:T(8,128)(2,1)} async-done(((bf16[32,64,384]{2,1,0:T(8,128)(2,1)}), bf16[32,64,384]{2,1,0:T(8,128)(2,1)}, u32[]{:S(2)}, u32[]{:S(2)}) %all-to-all-start.1) | async-done | bytes 1572896 | tf_op jit(solution)/shard_map/all_to_all | solution.py:647
  92.6 23.1 %attention_b.1 = (bf16[32,64,384]{2,1,0:T(8,128)(2,1)}, bf16[24,64,384]{2,1,0:T(8,128)(2,1)}, bf16[24,64,384]{2,1,0:T(8,128)(2,1)}, bf16[24,64,384]{2,1,0:T(8,128)(2,1)}, bf16[24,64,384]{2,1,0:T(8,128)(2,1)}) custom-call(s32[24]{0:T(128)} %table_ref.11, bf16[24,64,384]{2,1,0:T(8,128)(2,1)} %get-tuple-element.28.before_ref.x_ref, ...), custom_call_target="tpu_custom_call" | custom-call | tf_op jit(solution)/shard_map/attention_b/pallas_call | solution.py:467
  115.7 5.0 %all-to-all-start.3 = ((bf16[32,64,384]{2,1,0:T(8,128)(2,1)}), bf16[32,64,384]{2,1,0:T(8,128)(2,1)}, u32[]{:S(2)}, u32[]{:S(2)}) async-start(bf16[32,64,384]{2,1,0:T(8,128)(2,1)} %get-tuple-element.36.refs_5_), calls=%async_computation.3 | async-start | bytes 3145728 | tf_op jit(solution)/shard_map/all_to_all | solution.py:647
  120.7 23.4 %block_b.1 = bf16[32,64,384]{2,1,0:T(8,128)(2,1)} custom-call(s32[24]{0:T(128)} %table_ref.11, bf16[24,64,384]{2,1,0:T(8,128)(2,1)} %get-tuple-element.32.x_ref, bf16[24,64,384]{2,1,0:T(8,128)(2,1)} %get-tuple-element.33.q_ref, bf16[24,64,384]{2,1,0:T(8,128)(2,1)} %get-tuple-element.30.k_ref.refs_0_, bf16[24,64,384]{2,1,0:T(8,128)(2,1)} %get-tuple-element.34.refs_1_, ...), custom_call_target="tpu_custom_call" | custom-call | tf_op jit(solution)/shard_map/block_b/pallas_call | solution.py:490
  144.1 0.2 all-to-all-done.3.refs_0_.refs_1_.refs_2_.refs_3_
  144.3 7.0 %all-to-all-start.2 = ((bf16[32,64,384]{2,1,0:T(8,128)(2,1)}), bf16[32,64,384]{2,1,0:T(8,128)(2,1)}, u32[]{:S(2)}, u32[]{:S(2)}) async-start(bf16[32,64,384]{2,1,0:T(8,128)(2,1)} %block_b.1), calls=%async_computation.2 | async-start | bytes 3145728 | tf_op jit(solution)/shard_map/all_to_all | solution.py:647
  151.3 8.4 %forward_home.1.done_in = bf16[16,128,384]{2,1,0:T(8,128)(2,1)} custom-call(s32[16]{0:T(128)} %table_ref.13, bf16[32,64,384]{2,1,0:T(8,128)(2,1)} %all-to-all-done.3.refs_0_.refs_1_.refs_2_.refs_3_, bf16[32,64,384]{2,1,0:T(8,128)(2,1)} %all-to-all-done.3.refs_0_.refs_1_.refs_2_.refs_3_, bf16[32,64,384]{2,1,0:T(8,128)(2,1)} %all-to-all-done.3.refs_0_.refs_1_.refs_2_.refs_3_, ...), custom_call_target="tpu_custom_call" | custom-call | tf_op jit(solution)/shard_map/forward_home/pallas_call | solution.py:590
  159.7 15.5 %all-to-all-done.2.part_ref = bf16[32,64,384]{2,1,0:T(8,128)(2,1)} async-done(((bf16[32,64,384]{2,1,0:T(8,128)(2,1)}), bf16[32,64,384]{2,1,0:T(8,128)(2,1)}, u32[]{:S(2)}, u32[]{:S(2)}) %all-to-all-start.2) | async-done | bytes 1572896 | tf_op jit(solution)/shard_map/all_to_all | solution.py:647
  175.2 2.7 %home.1 = bf16[16,128,384]{2,1,0:T(8,128)(2,1)} custom-call(s32[16]{0:T(128)} %table_ref.13, bf16[32,64,384]{2,1,0:T(8,128)(2,1)} %all-to-all-done.2.part_ref, bf16[16,128,384]{2,1,0:T(8,128)(2,1)} %forward_home.1.done_in), custom_call_target="tpu_custom_call", output_to_operand_aliasing={{}: (2, {})} | custom-call | tf_op jit(solution)/shard_map/home/pallas_call | solution.py:627
Async XLA Ops:
  1.2 23.0 %collective-permute-start.1 = (bf16[512,384]{1,0:T(8,128)(2,1)S(1)}, bf16[512,384]{1,0:T(8,128)(2,1)S(1)}, u32[]{:S(2)}, u32[]{:S(2)}) collective-permute-start(bf16[512,384]{1,0:T(8,128)(2,1)S(1)} %get-tuple-element.37), channel_id=1, source_target_pairs={{1,0},{2,1},{3,2},{4,3},{5,4},{6,5},{7,6},{8,7},{9,8},{10,9},{11,1... | collective-permute-start | bytes 1179656 | tf_op jit(solution)/shard_map/ppermute | solution.py:657
  9.5 14.7 %collective-permute-start = (bf16[512,384]{1,0:T(8,128)(2,1)S(1)}, bf16[512,384]{1,0:T(8,128)(2,1)S(1)}, u32[]{:S(2)}, u32[]{:S(2)}) collective-permute-start(bf16[512,384]{1,0:T(8,128)(2,1)S(1)} %get-tuple-element.38), channel_id=1, source_target_pairs={{0,1},{1,2},{2,3},{3,4},{4,5},{5,6},{6,7},{7,8},{8,9},{9,10},{10,1... | collective-permute-start | bytes 1179656 | tf_op jit(solution)/shard_map/ppermute | solution.py:656
  15.5 8.8 %copy-start = (bf16[2,384,1152]{2,1,0:T(8,128)(2,1)S(1)}, bf16[2,384,1152]{2,1,0:T(8,128)(2,1)}, u32[]{:S(2)}) copy-start(bf16[2,384,1152]{2,1,0:T(8,128)(2,1)} %refs_10_.1) | copy-start | bytes 5308420
  15.5 8.8 %copy-start.1 = (f32[4,384]{1,0:T(4,128)S(1)}, f32[4,384]{1,0:T(4,128)}, u32[]{:S(2)}) copy-start(f32[4,384]{1,0:T(4,128)} %refs_4_.7) | copy-start | bytes 18436
  24.2 0.7 copy-start.2
  35.4 28.6 %all-to-all-start = ((bf16[32,64,384]{2,1,0:T(8,128)(2,1)}), bf16[32,64,384]{2,1,0:T(8,128)(2,1)}, u32[]{:S(2)}, u32[]{:S(2)}) async-start(bf16[32,64,384]{2,1,0:T(8,128)(2,1)} %attention_a_edges.1.refs_5_), calls=%async_computation | async-start | bytes 3145728 | tf_op jit(solution)/shard_map/all_to_all | solution.py:647
  64.0 28.6 %all-to-all-start.1 = ((bf16[32,64,384]{2,1,0:T(8,128)(2,1)}), bf16[32,64,384]{2,1,0:T(8,128)(2,1)}, u32[]{:S(2)}, u32[]{:S(2)}) async-start(bf16[32,64,384]{2,1,0:T(8,128)(2,1)} %block_a.1), calls=%async_computation.1 | async-start | bytes 3145728 | tf_op jit(solution)/shard_map/all_to_all | solution.py:647
  115.7 28.6 %all-to-all-start.3 = ((bf16[32,64,384]{2,1,0:T(8,128)(2,1)}), bf16[32,64,384]{2,1,0:T(8,128)(2,1)}, u32[]{:S(2)}, u32[]{:S(2)}) async-start(bf16[32,64,384]{2,1,0:T(8,128)(2,1)} %get-tuple-element.36.refs_5_), calls=%async_computation.3 | async-start | bytes 3145728 | tf_op jit(solution)/shard_map/all_to_all | solution.py:647
  144.3 30.9 %all-to-all-start.2 = ((bf16[32,64,384]{2,1,0:T(8,128)(2,1)}), bf16[32,64,384]{2,1,0:T(8,128)(2,1)}, u32[]{:S(2)}, u32[]{:S(2)}) async-start(bf16[32,64,384]{2,1,0:T(8,128)(2,1)} %block_b.1), calls=%async_computation.2 | async-start | bytes 3145728 | tf_op jit(solution)/shard_map/all_to_all | solution.py:647

commit v10 on v8

--- a/solution.py
+++ b/solution.py
@@ -23,7 +23,7 @@
 UNIT_TILES = 4
 HALF = PATCH // 2
 HID = 256
-FULL_VMEM = 65300 << 10
+FULL_VMEM = 65000 << 10
 
 norm_epsilon = 1e-05
 masked_score = -1000000000.0
@@ -121,8 +121,8 @@
         qkv_halo_kernel,
         grid=(1,),
         in_specs=[
-            whole((HALF, D)),
-            whole((HALF, D)),
+            pl.BlockSpec(memory_space=pltpu.VMEM),
+            pl.BlockSpec(memory_space=pltpu.VMEM),
             whole((4, D)),
             layer_of((D, 3 * D), 0),
             pl.BlockSpec(memory_space=pltpu.HBM),
@@ -132,7 +132,7 @@
         out_specs=[pl.BlockSpec((PATCH, D), lambda i: (last, 0))] * 2,
         out_shape=[ext, ext],
         input_output_aliases={4: 0, 5: 1},
-        compiler_params=pltpu.CompilerParams(vmem_limit_bytes=FULL_VMEM),
+        compiler_params=pltpu.CompilerParams(vmem_limit_bytes=24 << 20),
         name="qkv_halo",
     )(before, after, gains, qkv_weight, keys, values, earlier)
 
@@ -371,7 +371,7 @@
         emit(*result, step - 1)
 
 
-def attention_kernel(place, masked, arriving, table_ref, x_ref, q_ref, k_ref, *refs):
+def attention_kernel(place, masked, arriving, token, table_ref, x_ref, q_ref, k_ref, *refs):
     if arriving:
         v_ref, *refs = refs
         part_refs, refs = refs[:PATCH_TILES], refs[PATCH_TILES:]
@@ -381,7 +381,11 @@
     else:
         k_refs, v_refs = [k_ref, refs[0]], refs[1:3]
         proj_ref = refs[3]
-        out_ref, mixed_ref, tiles_ref, sems = refs[-4:]
+        *refs, mixed_ref, tiles_ref, sems = refs[4:]
+        out_ref = refs[-1]
+        if token:
+            out_ref, token_ref = refs[-2:]
+            token_ref[...] = jnp.zeros_like(token_ref)
     step = pl.program_id(0)
     units = pl.num_programs(0)
     count = UNIT_TILES * PART
@@ -434,6 +438,7 @@
 
 
 def attention(name, args, specs, units, place, masked, arriving, packed):
+    token = packed is None and not arriving
     hbm = pl.BlockSpec(memory_space=pltpu.HBM)
     aliases = {}
     if packed is not None:
@@ -442,11 +447,14 @@
         specs = [*specs, hbm]
     out_specs = [hbm]
     out_shape = [pltpu.HBM((PEERS, PART, D), bf16)]
+    if token:
+        out_specs.append(whole((8, 128)))
+        out_shape.append(jax.ShapeDtypeStruct((8, 128), f32))
     if arriving:
         out_specs += [pl.BlockSpec((PATCH_TILES, PART, D), lambda i, *_: (i // 2, 0, 0))] * 4
         out_shape += [pltpu.HBM((SLOTS, PART, D), bf16)] * 4
     return pl.pallas_call(
-        functools.partial(attention_kernel, place, masked, arriving),
+        functools.partial(attention_kernel, place, masked, arriving, token),
         grid_spec=pltpu.PrefetchScalarGridSpec(
             num_scalar_prefetch=1,
             grid=(units,),
@@ -460,7 +468,6 @@
         ),
         out_shape=out_shape,
         input_output_aliases=aliases,
-        compiler_params=pltpu.CompilerParams(vmem_limit_bytes=FULL_VMEM),
         name=name,
     )(*args)
 
@@ -640,10 +647,10 @@
     x = points.reshape(tiled)
     q, keys, values = qkv_own(points, norm_gains, qkv_weight)
     q = q.reshape(tiled)
-    (packed,) = attention_a(
+    packed, token = attention_a(
         "attention_a_middle", 0, lambda i: i + 1, dest_slot, x, q, keys, values, proj_weight, None
     )
-    keys, values = qkv_halo(before, after, norm_gains, qkv_weight, keys, values, packed)
+    keys, values = qkv_halo(before, after, norm_gains, qkv_weight, keys, values, token)
     (packed,) = attention_a(
         "attention_a_edges", 0, lambda i: 3 * i, dest_slot, x, q, keys, values, proj_weight, packed
     )

time: 180 us -> 179 us (level)
  transfers between devices with their start and end apart: 6 -> 6, of which waited for: 4 -> 4; matrix products, arithmetic and copies ran while one was open for 0% -> 0% of each run, Pallas kernels for 44% -> 45%
where the time goes in v10:
time: 179 us; the launch traced here: 176 us
  Pallas kernels  113 us (63%)
  waiting for transfers between devices  31.2 us (17%)
  starting transfers between devices  29.7 us (17%)
  local copies, waits for them, and re-layouts  1.86 us (1%)
    pallas_call x2, Pallas kernels, block(): pl.pallas_call(functools.partial(block_kernel, units, masked, whole_units...  40.4 us
    pallas_call x3, Pallas kernels, attention(): pl.pallas_call(functools.partial(attention_kernel, place, masked, arrivin...  38 us
    all_to_all x4, waiting for transfers between devices, exchange(): lax.all_to_all(part, 'chain', split_axis=0, concat_axis=0, tiled=True)  31.2 us
    all_to_all x4, starting transfers between devices, exchange(): lax.all_to_all(part, 'chain', split_axis=0, concat_axis=0, tiled=True)  21.4 us
    pallas_call x1, Pallas kernels, forward_owner(): pl.pallas_call(forward_owner_kernel, grid_spec=pltpu.PrefetchScalarGridSp...  15.4 us
    pallas_call x1, Pallas kernels, forward_home(): pl.pallas_call(forward_home_kernel, grid_spec=pltpu.PrefetchScalarGridSpe...  8.41 us
    ppermute x1, starting transfers between devices, body(): lax.ppermute(points[:HALF], axes, [((i + 1) % ring, i) for i in range(rin...  8.31 us
    pallas_call x1, Pallas kernels, qkv_own(): pl.pallas_call(qkv_own_kernel, grid=(rows // PATCH,), in_specs=[block, wh...  5.95 us
  transfers between devices with their start and end apart: 6, of which 4 were waited for; matrix products, arithmetic and copies ran while one was open for 0% of the time, Pallas kernels for 45%

profile of v10, /device:TPU:0, one launch (start us, length us, event | category | flops | bytes accessed | tf_op | source)
XLA Modules:
  0.0 176.3 jit_solution(3583718105046925752)
XLA Ops:
  0.0 1.2 fusion
  1.2 8.3 %collective-permute-start.1 = (bf16[512,384]{1,0:T(8,128)(2,1)S(1)}, bf16[512,384]{1,0:T(8,128)(2,1)S(1)}, u32[]{:S(2)}, u32[]{:S(2)}) collective-permute-start(bf16[512,384]{1,0:T(8,128)(2,1)S(1)} %get-tuple-element.37), channel_id=1, source_target_pairs={{1,0},{2,1},{3,2},{4,3},{5,4},{6,5},{7,6},{8,7},{9,8},{10,9},{11,1... | collective-permute-start | bytes 1179656 | tf_op jit(solution)/shard_map/ppermute | solution.py:644
  9.5 0.0 collective-permute-start
  9.5 5.9 %qkv_own.1 = (bf16[2048,384]{1,0:T(8,128)(2,1)}, bf16[3072,384]{1,0:T(8,128)(2,1)}, bf16[3072,384]{1,0:T(8,128)(2,1)}) custom-call(bf16[2048,384]{1,0:T(8,128)(2,1)} %x_ref.1, f32[4,384]{1,0:T(4,128)} %refs_4_.7, bf16[2,384,1152]{2,1,0:T(8,128)(2,1)} %refs_10_.1), custom_call_target="tpu_custom_call" | custom-call | tf_op jit(solution)/shard_map/qkv_own/pallas_call | solution.py:94
  15.5 0.0 copy-start
  15.5 0.0 copy-start.1
  15.5 8.3 %attention_a_middle.1 = (bf16[32,64,384]{2,1,0:T(8,128)(2,1)}, f32[8,128]{1,0:T(8,128)}) custom-call(s32[16]{0:T(128)} %table_ref.13, bf16[16,128,384]{2,1,0:T(8,128)(2,1)} %bitcast.3, bf16[16,128,384]{2,1,0:T(8,128)(2,1)} %bitcast.6, bf16[3072,384]{1,0:T(8,128)(2,1)} %get-tuple-element.22.k_ref.refs_0_.k_in, ...), custom_call_target="tpu_custom_call" | custom-call | tf_op jit(solution)/shard_map/attention_a_middle/pallas_call | solution.py:456
  23.8 0.0 collective-permute-done.1.b_ref
  23.8 0.0 collective-permute-done.a_ref
  23.8 0.0 copy-done
  23.8 0.0 copy-done.1
  23.9 0.0 copy-start.2
  23.9 0.7 copy-done.2
  24.5 2.4 %qkv_halo.1 = (bf16[3072,384]{1,0:T(8,128)(2,1)}, bf16[3072,384]{1,0:T(8,128)(2,1)}) custom-call(bf16[512,384]{1,0:T(8,128)(2,1)S(1)} %collective-permute-done.a_ref, bf16[512,384]{1,0:T(8,128)(2,1)S(1)} %collective-permute-done.1.b_ref, f32[4,384]{1,0:T(4,128)S(1)} %copy-done.1, ...), custom_call_target="tpu_custom_call", output_to_operand_aliasing={{0}: (4, {}), {1}: (5, {})} | custom-call | tf_op jit(solution)/shard_map/qkv_halo/pallas_call | solution.py:120
  27.0 7.6 %attention_a_edges.1.refs_5_ = bf16[32,64,384]{2,1,0:T(8,128)(2,1)} custom-call(s32[16]{0:T(128)} %table_ref.13, bf16[16,128,384]{2,1,0:T(8,128)(2,1)} %bitcast.4, bf16[16,128,384]{2,1,0:T(8,128)(2,1)} %bitcast.7, bf16[3072,384]{1,0:T(8,128)(2,1)} %get-tuple-element.25.k_ref.refs_0_.refs_1_, ...), custom_call_target="tpu_custom_call", output_to_operand_aliasing={{}: (8, {})} | custom-call | tf_op jit(solution)/shard_map/attention_a_edges/pallas_call | solution.py:456
  34.6 4.9 %all-to-all-start = ((bf16[32,64,384]{2,1,0:T(8,128)(2,1)}), bf16[32,64,384]{2,1,0:T(8,128)(2,1)}, u32[]{:S(2)}, u32[]{:S(2)}) async-start(bf16[32,64,384]{2,1,0:T(8,128)(2,1)} %attention_a_edges.1.refs_5_), calls=%async_computation | async-start | bytes 3145728 | tf_op jit(solution)/shard_map/all_to_all | solution.py:634
  39.5 17.1 %block_a.1 = bf16[32,64,384]{2,1,0:T(8,128)(2,1)} custom-call(s32[16]{0:T(128)} %table_ref.13, bf16[16,128,384]{2,1,0:T(8,128)(2,1)} %bitcast.5, bf16[16,128,384]{2,1,0:T(8,128)(2,1)} %bitcast.8, bf16[3072,384]{1,0:T(8,128)(2,1)} %get-tuple-element.25.k_ref.refs_0_.refs_1_, bf16[3072,384]{1,0:T(8,128)(2,1)} %get-tuple-element.25.k_ref.refs_0_.refs_1_, ...), custom_call_target="tpu_custom_call" | custom-call | tf_op jit(solution)/shard_map/block_a/pallas_call | solution.py:479
  56.6 6.6 %all-to-all-done.refs_0_.refs_1_.refs_2_.refs_3_ = bf16[32,64,384]{2,1,0:T(8,128)(2,1)} async-done(((bf16[32,64,384]{2,1,0:T(8,128)(2,1)}), bf16[32,64,384]{2,1,0:T(8,128)(2,1)}, u32[]{:S(2)}, u32[]{:S(2)}) %all-to-all-start) | async-done | bytes 1572896 | tf_op jit(solution)/shard_map/all_to_all | solution.py:634
  63.2 4.7 %all-to-all-start.1 = ((bf16[32,64,384]{2,1,0:T(8,128)(2,1)}), bf16[32,64,384]{2,1,0:T(8,128)(2,1)}, u32[]{:S(2)}, u32[]{:S(2)}) async-start(bf16[32,64,384]{2,1,0:T(8,128)(2,1)} %block_a.1), calls=%async_computation.1 | async-start | bytes 3145728 | tf_op jit(solution)/shard_map/all_to_all | solution.py:634
  67.9 15.4 %forward_owner.1 = (bf16[24,64,384]{2,1,0:T(8,128)(2,1)}, bf16[24,64,384]{2,1,0:T(8,128)(2,1)}, bf16[24,64,384]{2,1,0:T(8,128)(2,1)}, bf16[24,64,384]{2,1,0:T(8,128)(2,1)}) custom-call(s32[24]{0:T(128)} %table_ref.11, bf16[32,64,384]{2,1,0:T(8,128)(2,1)} %all-to-all-done.refs_0_.refs_1_.refs_2_.refs_3_, ...), custom_call_target="tpu_custom_call" | custom-call | tf_op jit(solution)/shard_map/forward_owner/pallas_call | solution.py:188
  83.3 8.5 %all-to-all-done.1.refs_1_.refs_2_.refs_3_.refs_4_.refs_5_.refs_6_.refs_7_.refs_8_ = bf16[32,64,384]{2,1,0:T(8,128)(2,1)} async-done(((bf16[32,64,384]{2,1,0:T(8,128)(2,1)}), bf16[32,64,384]{2,1,0:T(8,128)(2,1)}, u32[]{:S(2)}, u32[]{:S(2)}) %all-to-all-start.1) | async-done | bytes 1572896 | tf_op jit(solution)/shard_map/all_to_all | solution.py:634
  91.8 22.0 %attention_b.1 = (bf16[32,64,384]{2,1,0:T(8,128)(2,1)}, bf16[24,64,384]{2,1,0:T(8,128)(2,1)}, bf16[24,64,384]{2,1,0:T(8,128)(2,1)}, bf16[24,64,384]{2,1,0:T(8,128)(2,1)}, bf16[24,64,384]{2,1,0:T(8,128)(2,1)}) custom-call(s32[24]{0:T(128)} %table_ref.11, bf16[24,64,384]{2,1,0:T(8,128)(2,1)} %get-tuple-element.28.x_ref, ...), custom_call_target="tpu_custom_call" | custom-call | tf_op jit(solution)/shard_map/attention_b/pallas_call | solution.py:456
  113.9 4.9 %all-to-all-start.3 = ((bf16[32,64,384]{2,1,0:T(8,128)(2,1)}), bf16[32,64,384]{2,1,0:T(8,128)(2,1)}, u32[]{:S(2)}, u32[]{:S(2)}) async-start(bf16[32,64,384]{2,1,0:T(8,128)(2,1)} %get-tuple-element.36.refs_5_), calls=%async_computation.3 | async-start | bytes 3145728 | tf_op jit(solution)/shard_map/all_to_all | solution.py:634
  118.8 23.3 %block_b.1 = bf16[32,64,384]{2,1,0:T(8,128)(2,1)} custom-call(s32[24]{0:T(128)} %table_ref.11, bf16[24,64,384]{2,1,0:T(8,128)(2,1)} %get-tuple-element.32.x_ref, bf16[24,64,384]{2,1,0:T(8,128)(2,1)} %get-tuple-element.33.q_ref, bf16[24,64,384]{2,1,0:T(8,128)(2,1)} %get-tuple-element.30.k_ref.refs_0_, bf16[24,64,384]{2,1,0:T(8,128)(2,1)} %get-tuple-element.34.refs_1_, ...), custom_call_target="tpu_custom_call" | custom-call | tf_op jit(solution)/shard_map/block_b/pallas_call | solution.py:479
  142.1 0.6 all-to-all-done.3.refs_0_.refs_1_.refs_2_.refs_3_
  142.7 6.9 %all-to-all-start.2 = ((bf16[32,64,384]{2,1,0:T(8,128)(2,1)}), bf16[32,64,384]{2,1,0:T(8,128)(2,1)}, u32[]{:S(2)}, u32[]{:S(2)}) async-start(bf16[32,64,384]{2,1,0:T(8,128)(2,1)} %block_b.1), calls=%async_computation.2 | async-start | bytes 3145728 | tf_op jit(solution)/shard_map/all_to_all | solution.py:634
  149.6 8.4 %forward_home.1.done_in = bf16[16,128,384]{2,1,0:T(8,128)(2,1)} custom-call(s32[16]{0:T(128)} %table_ref.13, bf16[32,64,384]{2,1,0:T(8,128)(2,1)} %all-to-all-done.3.refs_0_.refs_1_.refs_2_.refs_3_, bf16[32,64,384]{2,1,0:T(8,128)(2,1)} %all-to-all-done.3.refs_0_.refs_1_.refs_2_.refs_3_, bf16[32,64,384]{2,1,0:T(8,128)(2,1)} %all-to-all-done.3.refs_0_.refs_1_.refs_2_.refs_3_, ...), custom_call_target="tpu_custom_call" | custom-call | tf_op jit(solution)/shard_map/forward_home/pallas_call | solution.py:577
  158.0 15.5 %all-to-all-done.2.part_ref = bf16[32,64,384]{2,1,0:T(8,128)(2,1)} async-done(((bf16[32,64,384]{2,1,0:T(8,128)(2,1)}), bf16[32,64,384]{2,1,0:T(8,128)(2,1)}, u32[]{:S(2)}, u32[]{:S(2)}) %all-to-all-start.2) | async-done | bytes 1572896 | tf_op jit(solution)/shard_map/all_to_all | solution.py:634
  173.5 2.7 %home.1 = bf16[16,128,384]{2,1,0:T(8,128)(2,1)} custom-call(s32[16]{0:T(128)} %table_ref.13, bf16[32,64,384]{2,1,0:T(8,128)(2,1)} %all-to-all-done.2.part_ref, bf16[16,128,384]{2,1,0:T(8,128)(2,1)} %forward_home.1.done_in), custom_call_target="tpu_custom_call", output_to_operand_aliasing={{}: (2, {})} | custom-call | tf_op jit(solution)/shard_map/home/pallas_call | solution.py:614
Async XLA Ops:
  1.2 22.6 %collective-permute-start.1 = (bf16[512,384]{1,0:T(8,128)(2,1)S(1)}, bf16[512,384]{1,0:T(8,128)(2,1)S(1)}, u32[]{:S(2)}, u32[]{:S(2)}) collective-permute-start(bf16[512,384]{1,0:T(8,128)(2,1)S(1)} %get-tuple-element.37), channel_id=1, source_target_pairs={{1,0},{2,1},{3,2},{4,3},{5,4},{6,5},{7,6},{8,7},{9,8},{10,9},{11,1... | collective-permute-start | bytes 1179656 | tf_op jit(solution)/shard_map/ppermute | solution.py:644
  9.5 14.3 %collective-permute-start = (bf16[512,384]{1,0:T(8,128)(2,1)S(1)}, bf16[512,384]{1,0:T(8,128)(2,1)S(1)}, u32[]{:S(2)}, u32[]{:S(2)}) collective-permute-start(bf16[512,384]{1,0:T(8,128)(2,1)S(1)} %get-tuple-element.38), channel_id=1, source_target_pairs={{0,1},{1,2},{2,3},{3,4},{4,5},{5,6},{6,7},{7,8},{8,9},{9,10},{10,1... | collective-permute-start | bytes 1179656 | tf_op jit(solution)/shard_map/ppermute | solution.py:643
  15.5 8.4 %copy-start = (bf16[2,384,1152]{2,1,0:T(8,128)(2,1)S(1)}, bf16[2,384,1152]{2,1,0:T(8,128)(2,1)}, u32[]{:S(2)}) copy-start(bf16[2,384,1152]{2,1,0:T(8,128)(2,1)} %refs_10_.1) | copy-start | bytes 5308420
  15.5 8.4 %copy-start.1 = (f32[4,384]{1,0:T(4,128)S(1)}, f32[4,384]{1,0:T(4,128)}, u32[]{:S(2)}) copy-start(f32[4,384]{1,0:T(4,128)} %refs_4_.7) | copy-start | bytes 18436
  23.9 0.7 copy-start.2
  34.6 28.6 %all-to-all-start = ((bf16[32,64,384]{2,1,0:T(8,128)(2,1)}), bf16[32,64,384]{2,1,0:T(8,128)(2,1)}, u32[]{:S(2)}, u32[]{:S(2)}) async-start(bf16[32,64,384]{2,1,0:T(8,128)(2,1)} %attention_a_edges.1.refs_5_), calls=%async_computation | async-start | bytes 3145728 | tf_op jit(solution)/shard_map/all_to_all | solution.py:634
  63.2 28.6 %all-to-all-start.1 = ((bf16[32,64,384]{2,1,0:T(8,128)(2,1)}), bf16[32,64,384]{2,1,0:T(8,128)(2,1)}, u32[]{:S(2)}, u32[]{:S(2)}) async-start(bf16[32,64,384]{2,1,0:T(8,128)(2,1)} %block_a.1), calls=%async_computation.1 | async-start | bytes 3145728 | tf_op jit(solution)/shard_map/all_to_all | solution.py:634
  113.9 28.8 %all-to-all-start.3 = ((bf16[32,64,384]{2,1,0:T(8,128)(2,1)}), bf16[32,64,384]{2,1,0:T(8,128)(2,1)}, u32[]{:S(2)}, u32[]{:S(2)}) async-start(bf16[32,64,384]{2,1,0:T(8,128)(2,1)} %get-tuple-element.36.refs_5_), calls=%async_computation.3 | async-start | bytes 3145728 | tf_op jit(solution)/shard_map/all_to_all | solution.py:634
  142.7 30.8 %all-to-all-start.2 = ((bf16[32,64,384]{2,1,0:T(8,128)(2,1)}), bf16[32,64,384]{2,1,0:T(8,128)(2,1)}, u32[]{:S(2)}, u32[]{:S(2)}) async-start(bf16[32,64,384]{2,1,0:T(8,128)(2,1)} %block_b.1), calls=%async_computation.2 | async-start | bytes 3145728 | tf_op jit(solution)/shard_map/all_to_all | solution.py:634
